TPU v7x, 128 devices: a whole 4x4x4 slice. The times are simulated.
128 devices in a mesh: row: 8 (over z, core), col: 16 (over y, x).
Axes of the slice: x: 4, y: 4, z: 4, core: 2. Of those that a mesh axis runs over, the one named last changes fastest.
Arguments:
- front_panel: float32 [12288, 1024], P('row', 'col')
- front_trail: float32 [12288, 8192], P('row', 'col'), may hold values from -6 to 6
- child_panel: float32 [2, 8192, 1024], P(None, 'row', 'col'), may hold values from -0.1875 to 0.1875
- child_trail: float32 [2, 8192, 8192], P(None, 'row', 'col'), may hold values from -4 to 4
- child_map: int32 [2, 8192], P(None, 'row'), may hold values from 0 to 1535, as said below
- child_count: int32 [2, 8], P(None, 'row'), may hold values from 256 to 1024, as said below
Outputs:
- factor: float32 [12288, 1024], P('row', 'col')
- schur_block: float32 [12288, 8192], P('row', 'col')
Inputs may be any that keep to these rules, and one draw needn't show every extreme that they name: `child_map`: within each slab and each aligned block of 1024 entries the values are distinct rows of one row block. `child_count`: some slab of some row block has all 1024 rows live in every draw.
All inputs are finite; a program needn't handle non-finite values.
Results may differ from a plain program's by a relative error of at most 0.00012.
Values sent between devices are 32-bit elements; how exact they have to be, the bound alone decides.
No kernel may reach another device: no remote copies, remote signals or barrier semaphores. Data moves between devices by JAX's collectives and lax.ppermute only.
A program may use at most 192 MiB of HBM per device.

v0:
```python
import jax
import jax.numpy as jnp
from jax import lax
from jax.sharding import PartitionSpec as P


def swapped(block, axis, distance):
    count = lax.axis_size(axis)
    route = []
    for low in range(count):
        high = low | 1 << distance
        if high != low and high < count:
            route += [(low, high), (high, low)]
    return lax.ppermute(block, axis, route)


def from_root(value, axis, root):
    mine = lax.axis_index(axis) == root
    return lax.psum(jnp.where(mine, value, jnp.zeros_like(value)), axis)


def on_device(front_panel, front_trail, child_panel, child_trail, child_map, child_count):
    block_rows, panel_cols = front_panel.shape
    trail_cols = front_trail.shape[1]
    slab_rows = child_map.shape[1]
    panel_width = panel_cols * lax.axis_size("col")
    top_bit = lax.axis_size("row").bit_length() - 2
    own_block = jnp.concatenate([front_panel, front_trail], axis=1)
    child_slabs = jnp.concatenate([child_panel, child_trail], axis=2)
    live_rows = jnp.arange(slab_rows, dtype=jnp.int32)[None, :] < child_count
    targets = jnp.where(live_rows, child_map, block_rows)
    assembled = own_block.at[targets[0]].add(child_slabs[0], mode="drop")
    partner = jnp.zeros_like(own_block).at[targets[1]].add(child_slabs[1], mode="drop")
    assembled = assembled + swapped(partner, "row", top_bit)
    assembled_panel = assembled[:, :panel_cols]
    assembled_trail = assembled[:, panel_cols:]
    row_id = lax.axis_index("row")
    col_id = lax.axis_index("col")
    first_row = row_id * block_rows
    window_start = panel_width + col_id * trail_cols
    window_root = window_start // block_rows
    window_offset = window_start - window_root * block_rows
    diag_piece = from_root(assembled_panel[:panel_width], "row", 0)
    panel_full, diag_full = (
        lax.all_gather(assembled_panel, "col", axis=1, tiled=True),
        lax.all_gather(diag_piece, "col", axis=1, tiled=True),
    )
    symmetric = 0.5 * (diag_full + diag_full.T)
    lower_factor = jnp.linalg.cholesky(symmetric)
    solved = jax.scipy.linalg.solve_triangular(lower_factor, panel_full.T, lower=True).T
    global_rows = first_row + jnp.arange(block_rows, dtype=jnp.int32)
    padded = jnp.concatenate(
        [lower_factor, jnp.zeros((block_rows - panel_width, panel_width), jnp.float32)], axis=0
    )
    factor_rows = jnp.where((global_rows < panel_width)[:, None], padded, solved)
    window_factor = from_root(
        lax.dynamic_slice_in_dim(factor_rows, window_offset, trail_cols, 0), "row", window_root
    )
    schur_block = assembled_trail - jnp.dot(
        factor_rows, window_factor.T, precision=lax.Precision.HIGHEST
    )
    factor_block = lax.dynamic_slice_in_dim(factor_rows, col_id * panel_cols, panel_cols, 1)
    return (factor_block, schur_block)


def solution(mesh):
    in_specs = (
        P("row", "col"),
        P("row", "col"),
        P(None, "row", "col"),
        P(None, "row", "col"),
        P(None, "row"),
        P(None, "row"),
    )
    out_specs = (P("row", "col"), P("row", "col"))
    return jax.shard_map(
        on_device, mesh=mesh, in_specs=in_specs, out_specs=out_specs, check_vma=False
    )
```

profile of v0, /device:TPU:21, one launch (start us, length us, event | category | flops | bytes accessed | tf_op | source)
XLA Modules:
  0.0 739.5 jit_solution(1922552528253355437)
XLA Ops:
  9.4 10.7 %scatter_custom_fusion = f32[1536,576]{1,0:T(8,128)} fusion(s32[1024]{0:T(1024)S(1)} %bitcast.134, f32[2,1024,64]{2,1,0:T(8,128)S(1)} %copy.52, f32[]{:T(128)} %constant.337, f32[2,1024,512]{2,1,0:T(8,128)} %param.9, f32[]{:T(128)} %constant.295.clone.1), kind=kCustom, calls=%fused_computation.26 | custom fusion | flops 1179648 | bytes 8781832 | tf_op jit(solution)/shard_map/scatter-add | solution.py:33
  29.3 76.3 %collective-permute-done = f32[1536,576]{0,1:T(8,128)} collective-permute-done((f32[1536,576]{0,1:T(8,128)}, f32[1536,576]{0,1:T(8,128)}, u32[]{:S(2)}, u32[]{:S(2)}) %collective-permute-start) | collective-permute-done | bytes 3538976 | tf_op jit(solution)/shard_map/ppermute | solution.py:14
  117.0 12.6 %scatter_custom_fusion.1 = f32[1536,576]{1,0:T(8,128)} fusion(f32[1536,576]{1,0:T(8,128)} %maximum_add_fusion, s32[1024]{0:T(1024)S(1)} %bitcast.133, f32[2,1024,512]{2,1,0:T(8,128)} %param.9, f32[]{:T(128)} %constant.337, f32[2,1024,64]{2,1,0:T(8,128)S(1)} %copy.52), kind=kCustom, calls=%fused_computation.29 | custom fusion | flops 1179648 | bytes 8782336 | tf_op jit(solution)/shard_map/scatter-add | solution.py:32
  131.6 60.2 %all-reduce.5.cloned.1.call-done = f32[1024,64]{0,1:T(8,128)} async-done(((f32[1024,64]{0,1:T(8,128)}), f32[1024,64]{0,1:T(8,128)}) %all-reduce.5.cloned.1.call-update) | async-done | bytes 262160 | tf_op jit(solution)/shard_map/psum | solution.py:19
  194.2 50.9 %all-gather.3.cloned.1.call-done = f32[1024,1024]{0,1:T(8,128)} async-done(((f32[1024,64]{0,1:T(8,128)}), f32[1024,1024]{0,1:T(8,128)}) %all-gather.3.cloned.1.call-update) | async-done | bytes 4194320 | tf_op jit(solution)/shard_map/all_gather | solution.py:46
  269.9 11.7 %cholesky.223 = f32[128,128]{1,0:T(8,128)S(1)} custom-call(f32[128,128]{1,0:T(8,128)S(1)} %cholesky.580), custom_call_target="Cholesky" | custom-call | tf_op jit(solution)/shard_map/jit(cholesky)/cholesky | solution.py:49
  284.2 9.8 %custom-call.63 = f32[1,128,128]{1,2,0:T(8,128)S(1)} custom-call(f32[1,128,128]{2,1,0:T(8,128)S(1)} %get-tuple-element.66), custom_call_target="InvertDiagBlocksLowerTriangular" | custom-call | tf_op jit(solution)/shard_map/jit(cholesky)/cholesky | solution.py:49
  297.8 11.9 %cholesky.244 = f32[128,128]{1,0:T(8,128)S(1)} custom-call(f32[128,128]{1,0:T(8,128)S(1)} %cholesky.584), custom_call_target="Cholesky" | custom-call | tf_op jit(solution)/shard_map/jit(cholesky)/cholesky | solution.py:49
  311.2 9.8 %custom-call.64 = f32[1,128,128]{1,2,0:T(8,128)S(1)} custom-call(f32[1,128,128]{2,1,0:T(8,128)S(1)} %get-tuple-element.63), custom_call_target="InvertDiagBlocksLowerTriangular" | custom-call | tf_op jit(solution)/shard_map/jit(cholesky)/cholesky | solution.py:49
  324.3 11.7 %cholesky.468 = f32[128,128]{1,0:T(8,128)S(1)} custom-call(f32[128,128]{1,0:T(8,128)S(1)} %cholesky.589), custom_call_target="Cholesky" | custom-call | tf_op jit(solution)/shard_map/jit(cholesky)/cholesky | solution.py:49
  336.7 9.8 %custom-call.65 = f32[1,128,128]{1,2,0:T(8,128)S(1)} custom-call(f32[1,128,128]{2,1,0:T(8,128)S(1)} %get-tuple-element.60), custom_call_target="InvertDiagBlocksLowerTriangular" | custom-call | tf_op jit(solution)/shard_map/jit(cholesky)/cholesky | solution.py:49
  350.0 11.9 %cholesky.487 = f32[128,128]{1,0:T(8,128)S(1)} custom-call(f32[128,128]{1,0:T(8,128)S(1)} %cholesky.594), custom_call_target="Cholesky" | custom-call | tf_op jit(solution)/shard_map/jit(cholesky)/cholesky | solution.py:49
  362.6 9.8 %custom-call.66 = f32[1,128,128]{1,2,0:T(8,128)S(1)} custom-call(f32[1,128,128]{2,1,0:T(8,128)S(1)} %get-tuple-element.57), custom_call_target="InvertDiagBlocksLowerTriangular" | custom-call | tf_op jit(solution)/shard_map/jit(cholesky)/cholesky | solution.py:49
  375.9 11.7 %cholesky.506 = f32[128,128]{1,0:T(8,128)S(1)} custom-call(f32[128,128]{1,0:T(8,128)S(1)} %cholesky.599), custom_call_target="Cholesky" | custom-call | tf_op jit(solution)/shard_map/jit(cholesky)/cholesky | solution.py:49
  388.3 10.2 %custom-call.67 = f32[1,128,128]{1,2,0:T(8,128)S(1)} custom-call(f32[1,128,128]{2,1,0:T(8,128)S(1)} %get-tuple-element.54), custom_call_target="InvertDiagBlocksLowerTriangular" | custom-call | tf_op jit(solution)/shard_map/jit(cholesky)/cholesky | solution.py:49
  401.8 11.7 %cholesky.526 = f32[128,128]{1,0:T(8,128)S(1)} custom-call(f32[128,128]{1,0:T(8,128)S(1)} %cholesky.604), custom_call_target="Cholesky" | custom-call | tf_op jit(solution)/shard_map/jit(cholesky)/cholesky | solution.py:49
  414.1 9.8 %custom-call.68 = f32[1,128,128]{1,2,0:T(8,128)S(1)} custom-call(f32[1,128,128]{2,1,0:T(8,128)S(1)} %get-tuple-element.51), custom_call_target="InvertDiagBlocksLowerTriangular" | custom-call | tf_op jit(solution)/shard_map/jit(cholesky)/cholesky | solution.py:49
  426.9 11.9 %cholesky.546 = f32[128,128]{1,0:T(8,128)S(1)} custom-call(f32[128,128]{1,0:T(8,128)S(1)} %cholesky.609), custom_call_target="Cholesky" | custom-call | tf_op jit(solution)/shard_map/jit(cholesky)/cholesky | solution.py:49
  439.4 9.8 %custom-call.69 = f32[1,128,128]{1,2,0:T(8,128)S(1)} custom-call(f32[1,128,128]{2,1,0:T(8,128)S(1)} %get-tuple-element.48), custom_call_target="InvertDiagBlocksLowerTriangular" | custom-call | tf_op jit(solution)/shard_map/jit(cholesky)/cholesky | solution.py:49
  451.9 11.7 %cholesky.564 = f32[128,128]{1,0:T(8,128)S(1)} custom-call(f32[128,128]{1,0:T(8,128)S(1)} %convolution_subtract_fusion.12), custom_call_target="Cholesky" | custom-call | tf_op jit(solution)/shard_map/jit(cholesky)/cholesky | solution.py:49
  480.0 23.2 %while.1 = (s32[]{:T(128)}, f32[1024,1024]{1,0:T(8,128)}, s32[8,2]{0,1:T(2,128)S(1)}, f32[8,128,128]{2,1,0:T(8,128)S(1)}, s32[]{:T(128)}) while((s32[]{:T(128)}, f32[1024,1024]{1,0:T(8,128)}, s32[8,2]{0,1:T(2,128)S(1)}, f32[8,128,128]{2,1,0:T(8,128)S(1)}, s32[]{:T(128)}) %tuple.61), condition=%wide.while_cond, body=%wide.while_body.sunk | while | flops 2 | bytes 131181 | solution.py:50
  503.2 78.8 %custom-call.70 = f32[8,128,128]{1,2,0:T(8,128)S(1)} custom-call(f32[8,128,128]{2,1,0:T(8,128)S(1)} %get-tuple-element.9), custom_call_target="InvertDiagBlocksLowerTriangular" | custom-call | tf_op jit(solution)/shard_map/jit(_solve_triangular)/triangular_solve | solution.py:50
  655.3 63.1 %all-reduce.7.cloned.1.call-done = f32[512,1024]{1,0:T(8,128)} async-done(((f32[512,1024]{1,0:T(8,128)}), f32[512,1024]{1,0:T(8,128)}) %all-reduce.7.cloned.1.call-update) | async-done | bytes 2097168 | tf_op jit(solution)/shard_map/psum | solution.py:19
  718.4 14.3 %slice_subtract_fusion = f32[1536,512]{1,0:T(8,128)} fusion(f32[1536,576]{1,0:T(8,128)} %scatter_custom_fusion.1, f32[1536,1024]{1,0:T(8,128)} %copy-done, f32[512,1024]{1,0:T(8,128)} %all-reduce.7.cloned.1.call-done), kind=kOutput, calls=%fused_computation.15 | convolution fusion | flops 9664462848 | bytes 14680064 | tf_op jit(solution)/shard_map/dot_general | solution.py:59
  (147 shorter events, 190.1 us)
Async XLA Ops:
  7.2 184.7 %all-reduce.5.cloned.1.call-start = ((), (), s32[]{:S(2)}) async-start(), calls=%async_computation | async-start | bytes 524288 | tf_op jit(solution)/shard_map/psum | solution.py:19
  20.1 9.0 %copy-start.9 = (f32[1536,64]{0,1:T(8,128)S(1)}, f32[1536,64]{0,1:T(8,128)}, u32[]{:S(2)}) copy-start(f32[1536,64]{0,1:T(8,128)} %param.6) | copy-start | bytes 1179652
  25.4 80.2 %collective-permute-start = (f32[1536,576]{0,1:T(8,128)}, f32[1536,576]{0,1:T(8,128)}, u32[]{:S(2)}, u32[]{:S(2)}) collective-permute-start(f32[1536,576]{0,1:T(8,128)} %copy.53), channel_id=1, source_target_pairs={{0,64},{64,0},{16,80},{80,16},{32,96},{96,32},{48,112},{112,48},{1... | collective-permute-start | bytes 10616840 | tf_op jit(solution)/shard_map/ppermute | solution.py:14
  131.6 113.5 %all-gather.3.cloned.1.call-start = ((), (), s32[]{:S(2)}) async-start(), calls=%async_computation.1 | async-start | bytes 4456448 | tf_op jit(solution)/shard_map/all_gather | solution.py:46
  191.8 390.2 %all-gather.5.cloned.1.call-start = ((), (), s32[]{:S(2)}) async-start(), calls=%async_computation.2 | async-start | bytes 6684672 | tf_op jit(solution)/shard_map/all_gather | solution.py:45
  194.1 524.3 %all-reduce.7.cloned.1.call-start = ((), (), s32[]{:S(2)}) async-start(), calls=%async_computation.3 | async-start | bytes 4194304 | tf_op jit(solution)/shard_map/psum | solution.py:19
  267.8 2.0 copy-start.2
  582.0 15.6 %copy-start.8 = (f32[8,128,128]{1,2,0:T(8,128)}, f32[8,128,128]{1,2,0:T(8,128)S(1)}, u32[]{:S(2)}) copy-start(f32[8,128,128]{1,2,0:T(8,128)S(1)} %custom-call.70) | copy-start | bytes 1572868
  599.9 0.9 copy-start.7
  635.2 8.5 %copy-start.3 = (f32[128,1536]{0,1:T(8,128)S(1)}, f32[128,1536]{0,1:T(8,128)}, u32[]{:S(2)}) copy-start(f32[128,1536]{0,1:T(8,128)} %copy.68) | copy-start | bytes 2359300
  642.3 1.7 copy-start.6
  642.3 1.8 copy-start.5
  643.6 1.2 copy-start.4
  643.9 3.5 copy-start.1
  648.7 2.7 copy-start
Sparse Core Ops, SparseCore 0:
  131.7 60.0 all-reduce.4
  194.2 50.8 all-gather.2
  248.0 60.9 all-gather.4
  653.0 65.3 all-reduce.6
where the time goes:
time: 752 us; the launch traced here: 739 us
  other arithmetic  303 us (40%)
  waiting for transfers between devices  251 us (33%)
  matrix products  87.8 us (12%)
  local copies, waits for them, and re-layouts  75.2 us (10%)
  between operations  19.2 us (3%)
    another operation x30, other arithmetic, on_device(): lower_factor = jnp.linalg.cholesky(symmetric)  172 us
    psum x2, waiting for transfers between devices, from_root(): return lax.psum(jnp.where(mine, value, jnp.zeros_like(value)), axis)  123 us
    another operation x3, other arithmetic, on_device(): jax.scipy.linalg.solve_triangular(lower_factor, panel_full.T, lower=True)  85.4 us
    ppermute x1, waiting for transfers between devices, swapped(): return lax.ppermute(block, axis, route)  76.3 us
    all_gather x1, waiting for transfers between devices, on_device(): lax.all_gather(diag_piece, 'col', axis=1, tiled=True)  50.9 us
    another operation x15, matrix products, on_device(): jax.scipy.linalg.solve_triangular(lower_factor, panel_full.T, lower=True)  50.7 us
    another operation x24, local copies, waits for them, and re-layouts  23 us
    another operation x14, matrix products, on_device(): lower_factor = jnp.linalg.cholesky(symmetric)  22.8 us
  transfers between devices with their start and end apart: 5, of which 4 were waited for; matrix products, arithmetic and copies ran while one was open for 45% of the time, Pallas kernels for 0%

commit v1 on v0

v1 whole, which is shorter than its diff:
```python
import jax
import jax.numpy as jnp
from jax import lax
from jax.experimental import pallas as pl
from jax.experimental.pallas import tpu as pltpu
from jax.sharding import PartitionSpec as P

f32 = jnp.float32
bf16 = jnp.bfloat16

F = 12288
PB = 1024
CR = 1024
FR = 1536
TC = 512
PC = 64
B = 128
NB = PB // B
Q = 256
MB = 1 << 20

NATURAL = (((1,), (0,)), ((), ()))
LHS_T = (((0,), (0,)), ((), ()))
RHS_T = (((1,), (1,)), ((), ()))


def split(x):
    hi = x.astype(bf16)
    return hi, (x - hi.astype(f32)).astype(bf16)


def dot1(a, b, dims=NATURAL):
    return lax.dot_general(a, b, dims, preferred_element_type=f32)


def dot3(a, b, dims=NATURAL):
    (ah, al), (bh, bl) = a, b
    return dot1(ah, bh, dims) + (dot1(ah, bl, dims) + dot1(al, bh, dims))


def one_hot(first, rows, target):
    at = first + lax.broadcasted_iota(jnp.int32, (rows, CR), 0)
    return (at == target).astype(f32).astype(bf16)


def live_target(count, map_row):
    k = lax.broadcasted_iota(jnp.int32, (1, CR), 1)
    return jnp.where(k < count, map_row, -1)


def panel_kernel(count_ref, map_ref, front_ref, child_ref, own_ref, send_ref):
    for slab in range(2):
        target = live_target(count_ref[slab, 0], map_ref[slab:slab + 1, :])
        c = child_ref[slab]
        hi = c.astype(bf16)
        rest = c - hi.astype(f32)
        mid = rest.astype(bf16)
        low = (rest - mid.astype(f32)).astype(bf16)
        parts = jnp.concatenate([hi, mid, low], axis=0)
        for at in range(0, FR, 512):
            moved = dot1(parts, one_hot(at, 512, target), RHS_T)
            moved = moved[:PC] + (moved[PC:2 * PC] + moved[2 * PC:])
            if slab == 0:
                own_ref[:, at:at + 512] = front_ref[:, at:at + 512] + moved
            else:
                send_ref[:PC, at:at + 512] = moved
        if slab == 1:
            send_ref[PC:, :CR] = jnp.broadcast_to(target.astype(f32), (8, CR))
            send_ref[PC:, CR:] = jnp.zeros((8, FR - CR), f32)


def panel_parts(count, child_map, front_t, child_t):
    return pl.pallas_call(
        panel_kernel,
        name="panel_parts",
        out_shape=(jax.ShapeDtypeStruct((PC, FR), f32), jax.ShapeDtypeStruct((PC + 8, FR), f32)),
        in_specs=[pl.BlockSpec(memory_space=pltpu.SMEM)] + [pl.BlockSpec(memory_space=pltpu.VMEM)] * 3,
        out_specs=(pl.BlockSpec(memory_space=pltpu.VMEM),) * 2,
        compiler_params=pltpu.CompilerParams(vmem_limit_bytes=24 * MB),
    )(count, child_map, front_t, child_t)


def trail_kernel(count_ref, map_ref, front_ref, child_ref, out_ref, ch, cl):
    @pl.when(pl.program_id(0) == 0)
    def _():
        ch[...], cl[...] = split(child_ref[...])

    target = live_target(count_ref[0, 0], map_ref[0:1, :])
    g = one_hot(pl.program_id(0) * 512, 512, target)
    out_ref[...] = front_ref[...] + (dot1(g, ch[...]) + dot1(g, cl[...]))


def trail_own(count, child_map, front, child):
    return pl.pallas_call(
        trail_kernel,
        name="trail_own",
        grid=(FR // 512,),
        out_shape=jax.ShapeDtypeStruct((FR, TC), f32),
        in_specs=[
            pl.BlockSpec(memory_space=pltpu.SMEM),
            pl.BlockSpec((2, CR), lambda s: (0, 0)),
            pl.BlockSpec((512, TC), lambda s: (s, 0)),
            pl.BlockSpec((None, CR, TC), lambda s: (0, 0, 0)),
        ],
        out_specs=pl.BlockSpec((512, TC), lambda s: (s, 0)),
        scratch_shapes=[pltpu.VMEM((CR, TC), bf16)] * 2,
        compiler_params=pltpu.CompilerParams(vmem_limit_bytes=24 * MB),
    )(count, child_map, front, child)


def lane(x, at):
    return jnp.broadcast_to(x[:, at:at + 1], (8, B))


def chain(w_ref):
    def rows(r):
        x = jnp.broadcast_to(w_ref[r:r + 1, :], (8, 2 * B))
        return x[:, :B], x[:, B:]

    for q in range(4):
        done = []
        for t in range(4):
            m = 4 * q + t
            p, a = [], []
            for i in range(8):
                x, y = rows(8 * m + i)
                p.append(x)
                a.append(y)

            def apply(u):
                b = [[lane(u[j][0], 8 * m + i) for j in range(8)] for i in range(8)]
                for i in range(8):
                    for j in range(8):
                        p[i] = p[i] - b[i][j] * u[j][0]
                        a[i] = a[i] - b[i][j] * u[j][1]
                return b

            for u in done[:-1]:
                apply(u)
            d = {(i, j): lane(p[i], 8 * m + j) for i in range(8) for j in range(i + 1)}
            if done:
                b = apply(done[-1])
                for i in range(8):
                    for j in range(i + 1):
                        for k in range(8):
                            d[i, j] = d[i, j] - b[i][k] * b[j][k]
            u = []
            for j in range(8):
                r = lax.rsqrt(d[j, j])
                low = {i: d[i, j] * r for i in range(j + 1, 8)}
                for i in range(j + 1, 8):
                    for k in range(j + 1, i + 1):
                        d[i, k] = d[i, k] - low[i] * low[k]
                uj, vj = p[j] * r, a[j] * r
                u.append((uj, vj))
                for i in range(j + 1, 8):
                    p[i] = p[i] - low[i] * uj
                    a[i] = a[i] - low[i] * vj
            sub = lax.broadcasted_iota(jnp.int32, (8, B), 0)
            cu, cv = u[0]
            for j in range(1, 8):
                cu = jnp.where(sub == j, u[j][0], cu)
                cv = jnp.where(sub == j, u[j][1], cv)
            w_ref[8 * m:8 * m + 8, :B] = cu
            w_ref[8 * m:8 * m + 8, B:] = cv
            done.append(u)
        if q < 3:
            um = w_ref[32 * q:32 * q + 32, :]
            ut = um[:, :B].T[32 * (q + 1):, :]
            w_ref[32 * (q + 1):, :] = w_ref[32 * (q + 1):, :] - dot3(split(ut), split(um))


def chol_kernel(at_ref, d_ref, uh, ul, lh, ll, ih, il, s_ref, w_ref, v_ref):
    col = at_ref[1]
    for j in range(PB // PC):
        s_ref[PC * j:PC * (j + 1), :] = d_ref[jnp.bitwise_xor(col, j)]
    for i in range(NB):
        for j in range(i, NB):
            up = s_ref[i * B:(i + 1) * B, j * B:(j + 1) * B]
            dn = s_ref[j * B:(j + 1) * B, i * B:(i + 1) * B]
            s_ref[i * B:(i + 1) * B, j * B:(j + 1) * B] = 0.5 * (up + dn.T)
    r = lax.broadcasted_iota(jnp.int32, (B, B), 0)
    c = lax.broadcasted_iota(jnp.int32, (B, B), 1)
    eye = (r == c).astype(f32)

    def step(k, _):
        for kk in range(NB):
            @pl.when(k == kk)
            def _():
                here = slice(kk * B, (kk + 1) * B)
                if kk:
                    left = (lh[here, :kk * B], ll[here, :kk * B])
                    right = (uh[:kk * B, kk * B:], ul[:kk * B, kk * B:])
                    s_ref[here, kk * B:] = s_ref[here, kk * B:] - dot3(left, right)
                w_ref[:, :B] = s_ref[here, here]

        w_ref[:, B:] = eye
        chain(w_ref)
        v = w_ref[:, B:]
        v_ref[k % 2] = v
        vs = split(v)
        for kk in range(NB):
            @pl.when(k == kk)
            def _():
                here = slice(kk * B, (kk + 1) * B)
                rest = slice((kk + 1) * B, PB)
                dh, dl = split(jnp.where(r <= c, w_ref[:, :B], 0.0))
                uh[here, here] = dh
                ul[here, here] = dl
                if kk:
                    uh[here, :kk * B] = jnp.zeros((B, kk * B), bf16)
                    ul[here, :kk * B] = jnp.zeros((B, kk * B), bf16)
                if kk < NB - 1:
                    rh, rl = split(dot3(vs, split(s_ref[here, rest])))
                    uh[here, rest] = rh
                    ul[here, rest] = rl
                    lh[rest, here] = rh.T
                    ll[rest, here] = rl.T
                half = kk % 2
                at = half * B
                ih[kk // 2, at:at + B, at:at + B] = vs[0]
                il[kk // 2, at:at + B, at:at + B] = vs[1]
                if half:
                    before = slice((kk - 1) * B, kk * B)
                    first = split(v_ref[0])
                    cross = split(dot3((lh[here, before], ll[here, before]), first))
                    th, tl = split(-dot3(vs, cross))
                    ih[kk // 2, B:, :B] = th
                    il[kk // 2, B:, :B] = tl
                    ih[kk // 2, :B, B:] = jnp.zeros((B, B), bf16)
                    il[kk // 2, :B, B:] = jnp.zeros((B, B), bf16)
        return 0

    lax.fori_loop(0, NB, step, 0)


def cholesky(at, pieces):
    full = jax.ShapeDtypeStruct((PB, PB), bf16)
    inv = jax.ShapeDtypeStruct((PB // Q, Q, Q), bf16)
    return pl.pallas_call(
        chol_kernel,
        name="chol",
        out_shape=(full,) * 4 + (inv,) * 2,
        in_specs=[pl.BlockSpec(memory_space=pltpu.SMEM), pl.BlockSpec(memory_space=pltpu.VMEM)],
        out_specs=(pl.BlockSpec(memory_space=pltpu.VMEM),) * 6,
        scratch_shapes=[
            pltpu.VMEM((PB, PB), f32),
            pltpu.VMEM((B, 2 * B), f32),
            pltpu.VMEM((2, B, B), f32),
        ],
        compiler_params=pltpu.CompilerParams(vmem_limit_bytes=40 * MB),
    )(at, pieces)


def finish_kernel(at_ref, win_ref, pan_ref, tgt_ref, trail_ref, child_ref, uh, ul, lh, ll, ih, il,
                  fac_ref, out_ref, a_ref, xh, xl, wh, wl, ch, cl):
    s = pl.program_id(0)
    row = at_ref[0]
    col = at_ref[1]

    def solve(yh, yl):
        for k in range(PB // Q):
            here = slice(k * Q, (k + 1) * Q)
            v = a_ref[here, :]
            if k:
                v = v - dot3((lh[here, :k * Q], ll[here, :k * Q]), (yh[:k * Q, :], yl[:k * Q, :]))
            yh[here, :], yl[here, :] = split(dot3((ih[k], il[k]), split(v)))

    @pl.when(s == 0)
    def _():
        for j in range(8):
            a_ref[B * j:B * (j + 1), :] = win_ref[jnp.bitwise_xor(row, j)]
        solve(wh, wl)
        ch[...], cl[...] = split(child_ref[...])

    @pl.when(s > 0)
    def _():
        own = jnp.logical_and(row == 0, s < 3)

        @pl.when(own)
        def _():
            here = pl.ds(pl.multiple_of((s - 1) * 512, 512), 512)
            xh[...] = uh[:, here]
            xl[...] = ul[:, here]

        @pl.when(jnp.logical_not(own))
        def _():
            a_ref[...] = pan_ref[...]
            solve(xh, xl)

        mine = pl.ds(pl.multiple_of(col * PC, PC), PC)
        fac_ref[...] = xh[mine, :].astype(f32) + xl[mine, :].astype(f32)
        target = tgt_ref[PC:PC + 1, :CR].astype(jnp.int32)
        g = one_hot((s - 1) * 512, 512, target)
        moved = dot1(g, ch[...]) + dot1(g, cl[...])
        prod = dot3((xh[...], xl[...]), (wh[...], wl[...]), LHS_T)
        out_ref[...] = trail_ref[...] + (moved - prod)


def finish(at, window, panel, got, trail, child, factors):
    def back(s):
        return jnp.maximum(s - 1, 0)

    whole = lambda shape: pl.BlockSpec(shape, lambda s: (0,) * len(shape), pipeline_mode=pl.Buffered(1))
    return pl.pallas_call(
        finish_kernel,
        name="finish",
        grid=(1 + FR // 512,),
        out_shape=(jax.ShapeDtypeStruct((PC, FR), f32), jax.ShapeDtypeStruct((FR, TC), f32)),
        in_specs=[
            pl.BlockSpec(memory_space=pltpu.SMEM),
            whole((8, B, TC)),
            pl.BlockSpec((PB, 512), lambda s: (0, back(s))),
            whole((PC + 8, FR)),
            pl.BlockSpec((512, TC), lambda s: (back(s), 0)),
            whole((CR, TC)),
            whole((PB, PB)), whole((PB, PB)), whole((PB, PB)), whole((PB, PB)),
            whole((PB // Q, Q, Q)), whole((PB // Q, Q, Q)),
        ],
        out_specs=(
            pl.BlockSpec((PC, 512), lambda s: (0, back(s))),
            pl.BlockSpec((512, TC), lambda s: (back(s), 0)),
        ),
        scratch_shapes=[pltpu.VMEM((PB, TC), f32)] + [pltpu.VMEM((PB, TC), bf16)] * 4
        + [pltpu.VMEM((CR, TC), bf16)] * 2,
        compiler_params=pltpu.CompilerParams(vmem_limit_bytes=48 * MB),
    )(at, window, panel, got, trail, child, *factors)


def flip(x, axis, bit, size):
    return lax.ppermute(x, axis, [(i, i ^ bit) for i in range(size)])


def window_pairs(w, parity):
    pairs = []
    for c in range(16):
        if (c + 2) % 3 == w:
            for r in range(8):
                pairs.append((((c + 2) // 3) * 16 + 2 * r + parity, r * 16 + c))
    return pairs


def on_device(front_panel, front_trail, child_panel, child_trail, child_map, child_count):
    row = lax.axis_index("row")
    col = lax.axis_index("col")
    at = jnp.stack([row, col]).astype(jnp.int32)

    own, send = panel_parts(child_count, child_map, front_panel.T, child_panel.transpose(0, 2, 1))
    got = flip(send, "row", 4, 8)
    own0 = lax.ppermute(own[:, :PB], "row", [(0, 4)])
    trail = trail_own(child_count, child_map, front_trail, child_trail)
    panel_t = own + got[:PC]

    diag = jnp.where(row == 4, own0 + send[:PC, :PB], panel_t[:, :PB])
    odd = jnp.bitwise_and(row, 1)
    lo, hi = diag[:, :512], diag[:, 512:]
    pieces = [
        lax.ppermute(hi, "row", [(0, 1), (4, 5)]),
        lax.ppermute(lo, "row", [(0, 2), (4, 6)]),
        lax.ppermute(hi, "row", [(0, 3), (4, 7)]),
    ]
    half = pieces[0] + pieces[1] + pieces[2] + jnp.where(row % 4 == 0, lo, 0.0)
    x4 = jnp.stack([half] + [flip(half, "col", b, 16) for b in (1, 2, 3)])
    y4 = jnp.stack([x4] + [flip(x4, "col", b, 16) for b in (4, 8, 12)]).reshape(16, PC, 512)
    other = flip(y4, "row", 1, 8)
    low = jnp.where(odd == 0, y4, other)
    high = jnp.where(odd == 0, other, y4)
    d_pieces = jnp.concatenate([low, high], axis=2)

    panel_full = lax.all_gather(panel_t, "col", axis=0, tiled=True)

    parts = []
    for parity in range(2):
        got_w = [
            lax.ppermute(panel_t[:, 512 * w:512 * (w + 1)], ("row", "col"), window_pairs(w, parity))
            for w in range(3)
        ]
        parts.append(got_w[0] + got_w[1] + got_w[2])
    win = jnp.concatenate(parts, axis=0)
    z4 = jnp.stack([win] + [flip(win, "row", b, 8) for b in (2, 4, 6)])
    zo = flip(z4, "row", 1, 8)
    window = jnp.stack([z4, zo], axis=1).reshape(8, B, TC)

    child1 = flip(child_trail[1], "row", 4, 8)
    factors = cholesky(at, d_pieces)
    factor_t, schur = finish(at, window, panel_full, got, trail, child1, factors)
    return factor_t.T, schur


def solution(mesh):
    in_specs = (
        P("row", "col"),
        P("row", "col"),
        P(None, "row", "col"),
        P(None, "row", "col"),
        P(None, "row"),
        P(None, "row"),
    )
    out_specs = (P("row", "col"), P("row", "col"))
    return jax.shard_map(
        on_device, mesh=mesh, in_specs=in_specs, out_specs=out_specs, check_vma=False
    )
```

time: 752 us -> 297 us (0.39)
  the two profiles are of different devices: /device:TPU:21 before, /device:TPU:11 now
where the time goes in v1:
time: 297 us
  waiting for transfers between devices  96.4 us (32%)
  Pallas kernels  84.1 us (28%)
  starting transfers between devices  76 us (26%)
  local copies, waits for them, and re-layouts  15.3 us (5%)
  between operations  14.4 us (5%)
  other arithmetic  10.7 us (4%)
    ppermute x13, waiting for transfers between devices, flip(): return lax.ppermute(x, axis, [(i, i ^ bit) for i in range(size)])  72.3 us
    pallas_call x1, Pallas kernels, cholesky(): pl.pallas_call(chol_kernel, name='chol', out_shape=(full,) * 4 + (inv,) *...  49.8 us
    ppermute x6, starting transfers between devices, on_device(): lax.ppermute(panel_t[:, 512 * w:512 * (w + 1)], ('row', 'col'), window_pa...  36.6 us
    ppermute x13, starting transfers between devices, flip(): return lax.ppermute(x, axis, [(i, i ^ bit) for i in range(size)])  35.9 us
    pallas_call x1, Pallas kernels, finish(): pl.pallas_call(finish_kernel, name='finish', grid=(1 + FR // 512,), out_s...  26.9 us
    ppermute x6, waiting for transfers between devices, on_device(): lax.ppermute(panel_t[:, 512 * w:512 * (w + 1)], ('row', 'col'), window_pa...  15.1 us
    unnamed x37, local copies, waits for them, and re-layouts  13.6 us
    ppermute x1, waiting for transfers between devices, on_device(): lax.ppermute(hi, 'row', [(0, 1), (4, 5)])  9 us
  transfers between devices with their start and end apart: 24, of which 8 were waited for; matrix products, arithmetic and copies ran while one was open for 4% of the time, Pallas kernels for 18%

profile of v1, /device:TPU:11, one launch (start us, length us, event | category | flops | bytes accessed | tf_op | source)
XLA Modules:
  0.0 296.9 jit_solution(10133582969093086949)
XLA Ops:
  10.7 2.8 panel_parts.1
  13.5 3.7 %collective-permute-start = (f32[72,1536]{1,0:T(8,128)S(1)}, f32[72,1536]{1,0:T(8,128)S(1)}, u32[]{:S(2)}, u32[]{:S(2)}) collective-permute-start(f32[72,1536]{1,0:T(8,128)S(1)} %get-tuple-element.13), channel_id=1, source_target_pairs={{0,64},{16,80},{32,96},{48,112},{64,0},{80,16},{96,32},{112,48},{1... | collective-permute-start | bytes 1327112 | tf_op jit(solution)/shard_map/ppermute | solution.py:331
  17.1 9.9 %collective-permute-done.tgt_ref = f32[72,1536]{1,0:T(8,128)S(1)} collective-permute-done((f32[72,1536]{1,0:T(8,128)S(1)}, f32[72,1536]{1,0:T(8,128)S(1)}, u32[]{:S(2)}, u32[]{:S(2)}) %collective-permute-start) | collective-permute-done | bytes 442400 | tf_op jit(solution)/shard_map/ppermute | solution.py:331
  33.2 9.0 %collective-permute-done.13 = f32[64,512]{1,0:T(8,128)S(1)} collective-permute-done((f32[64,512]{1,0:T(8,128)S(1)}, f32[64,512]{1,0:T(8,128)S(1)}, u32[]{:S(2)}, u32[]{:S(2)}) %collective-permute-start.13) | collective-permute-done | bytes 131104 | tf_op jit(solution)/shard_map/ppermute | solution.py:358
  42.6 2.1 collective-permute-start.17
  46.5 6.1 %collective-permute-done.17 = f32[64,512]{1,0:T(8,128)S(1)} collective-permute-done((f32[64,512]{1,0:T(8,128)S(1)}, f32[64,512]{1,0:T(8,128)S(1)}, u32[]{:S(2)}, u32[]{:S(2)}) %collective-permute-start.17) | collective-permute-done | bytes 131104 | tf_op jit(solution)/shard_map/ppermute | solution.py:331
  53.2 2.7 collective-permute-start.20
  58.5 15.0 %collective-permute-done.2 = f32[64,512]{1,0:T(8,128)S(1)} collective-permute-done((f32[64,512]{1,0:T(8,128)S(1)}, f32[64,512]{1,0:T(8,128)S(1)}, u32[]{:S(2)}, u32[]{:S(2)}) %collective-permute-start.2) | collective-permute-done | bytes 131104 | tf_op jit(solution)/shard_map/ppermute | solution.py:375
  73.6 4.8 %collective-permute-start.4 = (f32[64,512]{1,0:T(8,128)S(1)}, f32[64,512]{1,0:T(8,128)S(1)}, u32[]{:S(2)}, u32[]{:S(2)}) collective-permute-start(f32[64,512]{1,0:T(8,128)S(1)} %get-tuple-element.30), channel_id=1, source_target_pairs={{17,1},{19,17},{21,33},{23,49},{25,65},{27,81},{29,97},{31,113},{3... | collective-permute-start | bytes 393224 | tf_op jit(solution)/shard_map/ppermute | solution.py:375
  78.4 27.9 %collective-permute-start.5 = (f32[64,512]{1,0:T(8,128)S(1)}, f32[64,512]{1,0:T(8,128)S(1)}, u32[]{:S(2)}, u32[]{:S(2)}) collective-permute-start(f32[64,512]{1,0:T(8,128)S(1)} %get-tuple-element.28), channel_id=1, source_target_pairs={{17,2},{19,18},{21,34},{23,50},{25,66},{27,82},{29,98},{31,114},{3... | collective-permute-start | bytes 393224 | tf_op jit(solution)/shard_map/ppermute | solution.py:375
  107.7 1.6 pad_maximum_fusion.2
  109.3 18.6 %collective-permute-start.22 = (f32[16,64,512]{2,1,0:T(8,128)}, f32[16,64,512]{2,1,0:T(8,128)}, u32[]{:S(2)}, u32[]{:S(2)}) collective-permute-start(f32[16,64,512]{2,1,0:T(8,128)} %bitcast.20), channel_id=1, source_target_pairs={{0,16},{16,0},{32,48},{48,32},{64,80},{80,64},{96,112},{112,96},{1... | collective-permute-start | bytes 6291464 | tf_op jit(solution)/shard_map/ppermute | solution.py:331
  128.1 3.4 %collective-permute-start.8 = (f32[128,512]{1,0:T(8,128)S(1)}, f32[128,512]{1,0:T(8,128)S(1)}, u32[]{:S(2)}, u32[]{:S(2)}) collective-permute-start(f32[128,512]{1,0:T(8,128)S(1)} %get-tuple-element.34), channel_id=1, source_target_pairs={{0,64},{16,80},{32,96},{48,112},{64,0},{80,16},{96,32},{112,48},{1... | collective-permute-start | bytes 786440 | tf_op jit(solution)/shard_map/ppermute | solution.py:331
  133.4 2.2 collective-permute-start.11
  135.6 7.1 %collective-permute-done.8 = f32[128,512]{1,0:T(8,128)S(1)} collective-permute-done((f32[128,512]{1,0:T(8,128)S(1)}, f32[128,512]{1,0:T(8,128)S(1)}, u32[]{:S(2)}, u32[]{:S(2)}) %collective-permute-start.8) | collective-permute-done | bytes 262176 | tf_op jit(solution)/shard_map/ppermute | solution.py:331
  142.6 47.3 %collective-permute-done.9 = f32[128,512]{1,0:T(8,128)S(1)} collective-permute-done((f32[128,512]{1,0:T(8,128)S(1)}, f32[128,512]{1,0:T(8,128)S(1)}, u32[]{:S(2)}, u32[]{:S(2)}) %collective-permute-start.9) | collective-permute-done | bytes 262176 | tf_op jit(solution)/shard_map/ppermute | solution.py:331
  189.9 1.7 fusion.2
  191.6 2.1 collective-permute-start.10
  193.7 2.2 copy-done.2
  195.9 4.7 %trail_own.1.trail_ref = f32[1536,512]{1,0:T(8,128)S(1)} custom-call(s32[2,1]{1,0:T(2,128)S(1)} %copy.10.count_ref, s32[2,1024]{1,0:T(2,128)S(1)} %copy-done.15, f32[1536,512]{1,0:T(8,128)S(1)} %copy-done.3, f32[2,1024,512]{2,1,0:T(8,128)S(1)} %copy-done.2), custom_call_target="tpu_custom_call" | custom-call | tf_op jit(solution)/shard_map/trail_own/pallas_call | solution.py:94
  200.7 2.3 pad_maximum_fusion.1
  203.1 2.7 broadcast_select_fusion.1
  206.2 49.8 %chol.1 = (bf16[1024,1024]{1,0:T(8,128)(2,1)S(1)}, bf16[1024,1024]{1,0:T(8,128)(2,1)S(1)}, bf16[1024,1024]{1,0:T(8,128)(2,1)S(1)}, bf16[1024,1024]{1,0:T(8,128)(...) custom-call(s32[2]{0:T(128)S(1)} %pad_add_fusion.at_ref, ...), custom_call_target="tpu_custom_call" | custom-call | tf_op jit(solution)/shard_map/chol/pallas_call | solution.py:240
  263.2 26.9 %finish.1 = (f32[64,1536]{1,0:T(8,128)}, f32[1536,512]{1,0:T(8,128)}) custom-call(s32[2]{0:T(128)S(1)} %pad_add_fusion.at_ref, f32[8,128,512]{2,1,0:T(8,128)S(1)} %bitcast.28, f32[1024,1536]{1,0:T(8,128)} %all-gather.2.cloned.1.call-done.pan_ref, f32[72,1536]{1,0:T(8,128)S(1)} %copy-done.9, f32[1536,512]{1,0:T(8,128)} %copy-done, ...), custom_call_target="tpu_custom_call" | custom-call | tf_op jit(solution)/shard_map/finish/pallas_call | solution.py:305
  (84 shorter events, 26.1 us)
Async XLA Ops:
  7.2 255.0 %all-gather.2.cloned.1.call-start = ((), (), s32[]{:S(2)}) async-start(), calls=%async_computation | async-start | bytes 6684672 | tf_op jit(solution)/shard_map/all_gather | solution.py:370
  13.5 13.6 %collective-permute-start = (f32[72,1536]{1,0:T(8,128)S(1)}, f32[72,1536]{1,0:T(8,128)S(1)}, u32[]{:S(2)}, u32[]{:S(2)}) collective-permute-start(f32[72,1536]{1,0:T(8,128)S(1)} %get-tuple-element.13), channel_id=1, source_target_pairs={{0,64},{16,80},{32,96},{48,112},{64,0},{80,16},{96,32},{112,48},{1... | collective-permute-start | bytes 1327112 | tf_op jit(solution)/shard_map/ppermute | solution.py:331
  28.7 0.8 collective-permute-start.12
  30.5 11.7 %collective-permute-start.13 = (f32[64,512]{1,0:T(8,128)S(1)}, f32[64,512]{1,0:T(8,128)S(1)}, u32[]{:S(2)}, u32[]{:S(2)}) collective-permute-start(f32[64,512]{1,0:T(8,128)S(1)} %get-tuple-element.32), channel_id=1, source_target_pairs={{0,16},{64,80},{1,17},{65,81},{2,18},{66,82},{3,19},{67,83},{4,20}... | collective-permute-start | bytes 393224 | tf_op jit(solution)/shard_map/ppermute | solution.py:358
  31.8 10.4 %collective-permute-start.15 = (f32[64,512]{1,0:T(8,128)S(1)}, f32[64,512]{1,0:T(8,128)S(1)}, u32[]{:S(2)}, u32[]{:S(2)}) collective-permute-start(f32[64,512]{1,0:T(8,128)S(1)} %get-tuple-element.32), channel_id=1, source_target_pairs={{0,48},{64,112},{1,49},{65,113},{2,50},{66,114},{3,51},{67,115},{4... | collective-permute-start | bytes 393224 | tf_op jit(solution)/shard_map/ppermute | solution.py:360
  32.5 9.7 %collective-permute-start.14 = (f32[64,512]{1,0:T(8,128)S(1)}, f32[64,512]{1,0:T(8,128)S(1)}, u32[]{:S(2)}, u32[]{:S(2)}) collective-permute-start(f32[64,512]{1,0:T(8,128)S(1)} %get-tuple-element.31), channel_id=1, source_target_pairs={{0,32},{64,96},{1,33},{65,97},{2,34},{66,98},{3,35},{67,99},{4,36}... | collective-permute-start | bytes 393224 | tf_op jit(solution)/shard_map/ppermute | solution.py:359
  42.2 4.3 %collective-permute-start.16 = (f32[64,512]{1,0:T(8,128)S(1)}, f32[64,512]{1,0:T(8,128)S(1)}, u32[]{:S(2)}, u32[]{:S(2)}) collective-permute-start(f32[64,512]{1,0:T(8,128)S(1)} %select_add_fusion), channel_id=1, source_target_pairs={{0,1},{1,0},{2,3},{3,2},{4,5},{5,4},{6,7},{7,6},{8,9},{9,8},{10,11... | collective-permute-start | bytes 393224 | tf_op jit(solution)/shard_map/ppermute | solution.py:331
  42.6 10.1 %collective-permute-start.17 = (f32[64,512]{1,0:T(8,128)S(1)}, f32[64,512]{1,0:T(8,128)S(1)}, u32[]{:S(2)}, u32[]{:S(2)}) collective-permute-start(f32[64,512]{1,0:T(8,128)S(1)} %select_add_fusion), channel_id=1, source_target_pairs={{0,2},{1,3},{2,0},{3,1},{4,6},{5,7},{6,4},{7,5},{8,10},{9,11},{10,... | collective-permute-start | bytes 393224 | tf_op jit(solution)/shard_map/ppermute | solution.py:331
  44.7 8.3 %collective-permute-start.18 = (f32[64,512]{1,0:T(8,128)S(1)}, f32[64,512]{1,0:T(8,128)S(1)}, u32[]{:S(2)}, u32[]{:S(2)}) collective-permute-start(f32[64,512]{1,0:T(8,128)S(1)} %select_add_fusion), channel_id=1, source_target_pairs={{0,3},{1,2},{2,1},{3,0},{4,7},{5,6},{6,5},{7,4},{8,11},{9,10},{10,... | collective-permute-start | bytes 393224 | tf_op jit(solution)/shard_map/ppermute | solution.py:331
  53.1 53.3 %collective-permute-start.19 = (f32[4,64,512]{2,1,0:T(8,128)S(1)}, f32[4,64,512]{2,1,0:T(8,128)S(1)}, u32[]{:S(2)}, u32[]{:S(2)}) collective-permute-start(f32[4,64,512]{2,1,0:T(8,128)S(1)} %get-tuple-element.27), channel_id=1, source_target_pairs={{0,4},{1,5},{2,6},{3,7},{4,0},{5,1},{6,2},{7,3},{8,12},{9,13},{10,... | collective-permute-start | bytes 1572872 | tf_op jit(solution)/shard_map/ppermute | solution.py:331
  53.2 54.5 %collective-permute-start.20 = (f32[4,64,512]{2,1,0:T(8,128)S(1)}, f32[4,64,512]{2,1,0:T(8,128)S(1)}, u32[]{:S(2)}, u32[]{:S(2)}) collective-permute-start(f32[4,64,512]{2,1,0:T(8,128)S(1)} %get-tuple-element.27), channel_id=1, source_target_pairs={{0,8},{1,9},{2,10},{3,11},{4,12},{5,13},{6,14},{7,15},{8,0},{9,1},... | collective-permute-start | bytes 1572872 | tf_op jit(solution)/shard_map/ppermute | solution.py:331
  55.8 51.9 %collective-permute-start.21 = (f32[4,64,512]{2,1,0:T(8,128)S(1)}, f32[4,64,512]{2,1,0:T(8,128)S(1)}, u32[]{:S(2)}, u32[]{:S(2)}) collective-permute-start(f32[4,64,512]{2,1,0:T(8,128)S(1)} %get-tuple-element.27), channel_id=1, source_target_pairs={{0,12},{1,13},{2,14},{3,15},{4,8},{5,9},{6,10},{7,11},{8,4},{9,5},... | collective-permute-start | bytes 1572872 | tf_op jit(solution)/shard_map/ppermute | solution.py:331
  55.9 2.0 collective-permute-start.1
  56.5 17.0 %collective-permute-start.2 = (f32[64,512]{1,0:T(8,128)S(1)}, f32[64,512]{1,0:T(8,128)S(1)}, u32[]{:S(2)}, u32[]{:S(2)}) collective-permute-start(f32[64,512]{1,0:T(8,128)S(1)} %get-tuple-element.28), channel_id=1, source_target_pairs={{16,2},{18,18},{20,34},{22,50},{24,66},{26,82},{28,98},{30,114},{3... | collective-permute-start | bytes 393224 | tf_op jit(solution)/shard_map/ppermute | solution.py:375
  57.8 20.5 %collective-permute-start.3 = (f32[64,512]{1,0:T(8,128)S(1)}, f32[64,512]{1,0:T(8,128)S(1)}, u32[]{:S(2)}, u32[]{:S(2)}) collective-permute-start(f32[64,512]{1,0:T(8,128)S(1)} %get-tuple-element.29), channel_id=1, source_target_pairs={{0,0},{2,16},{4,32},{6,48},{8,64},{10,80},{12,96},{14,112},{16,3},... | collective-permute-start | bytes 393224 | tf_op jit(solution)/shard_map/ppermute | solution.py:375
  73.6 54.3 %collective-permute-start.4 = (f32[64,512]{1,0:T(8,128)S(1)}, f32[64,512]{1,0:T(8,128)S(1)}, u32[]{:S(2)}, u32[]{:S(2)}) collective-permute-start(f32[64,512]{1,0:T(8,128)S(1)} %get-tuple-element.30), channel_id=1, source_target_pairs={{17,1},{19,17},{21,33},{23,49},{25,65},{27,81},{29,97},{31,113},{3... | collective-permute-start | bytes 393224 | tf_op jit(solution)/shard_map/ppermute | solution.py:375
  78.4 49.5 %collective-permute-start.5 = (f32[64,512]{1,0:T(8,128)S(1)}, f32[64,512]{1,0:T(8,128)S(1)}, u32[]{:S(2)}, u32[]{:S(2)}) collective-permute-start(f32[64,512]{1,0:T(8,128)S(1)} %get-tuple-element.28), channel_id=1, source_target_pairs={{17,2},{19,18},{21,34},{23,50},{25,66},{27,82},{29,98},{31,114},{3... | collective-permute-start | bytes 393224 | tf_op jit(solution)/shard_map/ppermute | solution.py:375
  106.4 21.5 %collective-permute-start.6 = (f32[64,512]{1,0:T(8,128)S(1)}, f32[64,512]{1,0:T(8,128)S(1)}, u32[]{:S(2)}, u32[]{:S(2)}) collective-permute-start(f32[64,512]{1,0:T(8,128)S(1)} %get-tuple-element.29), channel_id=1, source_target_pairs={{1,0},{3,16},{5,32},{7,48},{9,64},{11,80},{13,96},{15,112},{17,3},... | collective-permute-start | bytes 393224 | tf_op jit(solution)/shard_map/ppermute | solution.py:375
  109.3 93.8 %collective-permute-start.22 = (f32[16,64,512]{2,1,0:T(8,128)}, f32[16,64,512]{2,1,0:T(8,128)}, u32[]{:S(2)}, u32[]{:S(2)}) collective-permute-start(f32[16,64,512]{2,1,0:T(8,128)} %bitcast.20), channel_id=1, source_target_pairs={{0,16},{16,0},{32,48},{48,32},{64,80},{80,64},{96,112},{112,96},{1... | collective-permute-start | bytes 6291464 | tf_op jit(solution)/shard_map/ppermute | solution.py:331
  128.0 7.6 %collective-permute-start.7 = (f32[128,512]{1,0:T(8,128)S(1)}, f32[128,512]{1,0:T(8,128)S(1)}, u32[]{:S(2)}, u32[]{:S(2)}) collective-permute-start(f32[128,512]{1,0:T(8,128)S(1)} %get-tuple-element.34), channel_id=1, source_target_pairs={{0,32},{16,48},{32,0},{48,16},{64,96},{80,112},{96,64},{112,80},{1... | collective-permute-start | bytes 786440 | tf_op jit(solution)/shard_map/ppermute | solution.py:331
  128.1 14.6 %collective-permute-start.8 = (f32[128,512]{1,0:T(8,128)S(1)}, f32[128,512]{1,0:T(8,128)S(1)}, u32[]{:S(2)}, u32[]{:S(2)}) collective-permute-start(f32[128,512]{1,0:T(8,128)S(1)} %get-tuple-element.34), channel_id=1, source_target_pairs={{0,64},{16,80},{32,96},{48,112},{64,0},{80,16},{96,32},{112,48},{1... | collective-permute-start | bytes 786440 | tf_op jit(solution)/shard_map/ppermute | solution.py:331
  131.5 58.4 %collective-permute-start.9 = (f32[128,512]{1,0:T(8,128)S(1)}, f32[128,512]{1,0:T(8,128)S(1)}, u32[]{:S(2)}, u32[]{:S(2)}) collective-permute-start(f32[128,512]{1,0:T(8,128)S(1)} %get-tuple-element.34), channel_id=1, source_target_pairs={{0,96},{16,112},{32,64},{48,80},{64,32},{80,48},{96,0},{112,16},{1... | collective-permute-start | bytes 786440 | tf_op jit(solution)/shard_map/ppermute | solution.py:331
  133.4 128.7 %collective-permute-start.11 = (f32[1024,512]{1,0:T(8,128)}, f32[1024,512]{1,0:T(8,128)}, u32[]{:S(2)}, u32[]{:S(2)}) collective-permute-start(f32[1024,512]{1,0:T(8,128)} %slice_bitcast_fusion), channel_id=1, source_target_pairs={{0,64},{16,80},{32,96},{48,112},{64,0},{80,16},{96,32},{112,48},{1... | collective-permute-start | bytes 6291464 | tf_op jit(solution)/shard_map/ppermute | solution.py:331
  191.6 9.1 %collective-permute-start.10 = (f32[4,128,512]{2,1,0:T(8,128)}, f32[4,128,512]{2,1,0:T(8,128)}, u32[]{:S(2)}, u32[]{:S(2)}) collective-permute-start(f32[4,128,512]{2,1,0:T(8,128)} %get-tuple-element.25), channel_id=1, source_target_pairs={{0,16},{16,0},{32,48},{48,32},{64,80},{80,64},{96,112},{112,96},{1... | collective-permute-start | bytes 3145736 | tf_op jit(solution)/shard_map/ppermute | solution.py:331
  (18 other events, 247.9 us)
Sparse Core Ops, SparseCore 0:
  28.7 86.9 all-gather.1

commit v2 on v1

v2 whole, which is shorter than its diff:
```python
import jax
import jax.numpy as jnp
from jax import lax
from jax.experimental import pallas as pl
from jax.experimental.pallas import tpu as pltpu
from jax.sharding import PartitionSpec as P

f32 = jnp.float32
bf16 = jnp.bfloat16

F = 12288
PB = 1024
CR = 1024
FR = 1536
TC = 512
PC = 64
B = 128
NB = PB // B
Q = 256
HF = 512
MB = 1 << 20

NATURAL = (((1,), (0,)), ((), ()))
LHS_T = (((0,), (0,)), ((), ()))
RHS_T = (((1,), (1,)), ((), ()))


def split(x):
    hi = x.astype(bf16)
    return hi, (x - hi.astype(f32)).astype(bf16)


def dot1(a, b, dims=NATURAL):
    return lax.dot_general(a, b, dims, preferred_element_type=f32)


def dot3(a, b, dims=NATURAL):
    (ah, al), (bh, bl) = a, b
    return dot1(ah, bh, dims) + (dot1(ah, bl, dims) + dot1(al, bh, dims))


def one_hot(first, rows, target):
    at = first + lax.broadcasted_iota(jnp.int32, (rows, CR), 0)
    return (at == target).astype(f32).astype(bf16)


def live_target(count, map_row):
    k = lax.broadcasted_iota(jnp.int32, (1, CR), 1)
    return jnp.where(k < count, map_row, -1)


def panel_kernel(at_ref, count_ref, map_ref, front_ref, child_ref, own_ref, send_ref, crit_ref):
    for slab in range(2):
        target = live_target(count_ref[0, slab], map_ref[slab:slab + 1, :])
        c = child_ref[slab]
        hi = c.astype(bf16)
        rest = c - hi.astype(f32)
        mid = rest.astype(bf16)
        low = (rest - mid.astype(f32)).astype(bf16)
        parts = jnp.concatenate([hi, mid, low], axis=0)
        for at in range(0, FR, 512):
            moved = dot1(parts, one_hot(at, 512, target), RHS_T)
            moved = moved[:PC] + (moved[PC:2 * PC] + moved[2 * PC:])
            if slab == 0:
                own_ref[:, at:at + 512] = front_ref[:, at:at + 512] + moved
            else:
                send_ref[:PC, at:at + 512] = moved
        if slab == 1:
            send_ref[PC:, :CR] = jnp.broadcast_to(target.astype(f32), (8, CR))
            send_ref[PC:, CR:] = jnp.zeros((8, FR - CR), f32)
    crit_ref[...] = send_ref[:PC, :PB]

    @pl.when(at_ref[0] == 0)
    def _():
        crit_ref[...] = own_ref[:, :PB]


def panel_parts(at, count, child_map, front_t, child_t):
    return pl.pallas_call(
        panel_kernel,
        name="panel_parts",
        out_shape=(
            jax.ShapeDtypeStruct((PC, FR), f32),
            jax.ShapeDtypeStruct((PC + 8, FR), f32),
            jax.ShapeDtypeStruct((PC, PB), f32),
        ),
        in_specs=[pl.BlockSpec(memory_space=pltpu.SMEM)] * 2 + [pl.BlockSpec(memory_space=pltpu.VMEM)] * 3,
        out_specs=(pl.BlockSpec(memory_space=pltpu.VMEM),) * 3,
        compiler_params=pltpu.CompilerParams(vmem_limit_bytes=58 * MB),
    )(at, count, child_map, front_t, child_t)


def trail_kernel(count_ref, map_ref, front_ref, child_ref, out_ref, ch, cl):
    @pl.when(pl.program_id(0) == 0)
    def _():
        ch[...], cl[...] = split(child_ref[...])

    target = live_target(count_ref[0, 0], map_ref[0:1, :])
    g = one_hot(pl.program_id(0) * 512, 512, target)
    out_ref[...] = front_ref[...] + (dot1(g, ch[...]) + dot1(g, cl[...]))


def trail_own(count, child_map, front, child):
    return pl.pallas_call(
        trail_kernel,
        name="trail_own",
        grid=(FR // 512,),
        out_shape=jax.ShapeDtypeStruct((FR, TC), f32),
        in_specs=[
            pl.BlockSpec(memory_space=pltpu.SMEM),
            pl.BlockSpec((2, CR), lambda s: (0, 0)),
            pl.BlockSpec((512, TC), lambda s: (s, 0)),
            pl.BlockSpec((None, CR, TC), lambda s: (0, 0, 0)),
        ],
        out_specs=pl.BlockSpec((512, TC), lambda s: (s, 0)),
        scratch_shapes=[pltpu.VMEM((CR, TC), bf16)] * 2,
        compiler_params=pltpu.CompilerParams(vmem_limit_bytes=58 * MB),
    )(count, child_map, front, child)


def lane(x, at):
    return jnp.broadcast_to(x[:, at:at + 1], (8, B))


def chain(w_ref):
    def rows(r):
        x = jnp.broadcast_to(w_ref[r:r + 1, :], (8, 2 * B))
        return x[:, :B], x[:, B:]

    for q in range(4):
        done = []
        for t in range(4):
            m = 4 * q + t
            p, a = [], []
            for i in range(8):
                x, y = rows(8 * m + i)
                p.append(x)
                a.append(y)

            def apply(u):
                b = [[lane(u[j][0], 8 * m + i) for j in range(8)] for i in range(8)]
                for i in range(8):
                    for j in range(8):
                        p[i] = p[i] - b[i][j] * u[j][0]
                        a[i] = a[i] - b[i][j] * u[j][1]
                return b

            for u in done[:-1]:
                apply(u)
            d = {(i, j): lane(p[i], 8 * m + j) for i in range(8) for j in range(i + 1)}
            if done:
                b = apply(done[-1])
                for i in range(8):
                    for j in range(i + 1):
                        for k in range(8):
                            d[i, j] = d[i, j] - b[i][k] * b[j][k]
            u = []
            for j in range(8):
                r = lax.rsqrt(d[j, j])
                low = {i: d[i, j] * r for i in range(j + 1, 8)}
                for i in range(j + 1, 8):
                    for k in range(j + 1, i + 1):
                        d[i, k] = d[i, k] - low[i] * low[k]
                uj, vj = p[j] * r, a[j] * r
                u.append((uj, vj))
                for i in range(j + 1, 8):
                    p[i] = p[i] - low[i] * uj
                    a[i] = a[i] - low[i] * vj
            sub = lax.broadcasted_iota(jnp.int32, (8, B), 0)
            cu, cv = u[0]
            for j in range(1, 8):
                cu = jnp.where(sub == j, u[j][0], cu)
                cv = jnp.where(sub == j, u[j][1], cv)
            w_ref[8 * m:8 * m + 8, :B] = cu
            w_ref[8 * m:8 * m + 8, B:] = cv
            done.append(u)
        if q < 3:
            um = w_ref[32 * q:32 * q + 32, :]
            ut = um[:, :B].T[32 * (q + 1):, :]
            w_ref[32 * (q + 1):, :] = w_ref[32 * (q + 1):, :] - dot3(split(ut), split(um))


def factor_blocks(rows, width, s_ref, w_ref, v_ref, uh, ul, lh, ll, ih, il):
    r = lax.broadcasted_iota(jnp.int32, (B, B), 0)
    c = lax.broadcasted_iota(jnp.int32, (B, B), 1)
    eye = (r == c).astype(f32)

    def step(k, _):
        for kk in range(rows // B):
            @pl.when(k == kk)
            def _():
                here = slice(kk * B, (kk + 1) * B)
                if kk:
                    left = (lh[here, :kk * B], ll[here, :kk * B])
                    right = (uh[:kk * B, kk * B:], ul[:kk * B, kk * B:])
                    s_ref[here, kk * B:] = s_ref[here, kk * B:] - dot3(left, right)
                w_ref[:, :B] = s_ref[here, here]

        w_ref[:, B:] = eye
        chain(w_ref)
        v = w_ref[:, B:]
        v_ref[k % 2] = v
        vs = split(v)
        for kk in range(rows // B):
            @pl.when(k == kk)
            def _():
                here = slice(kk * B, (kk + 1) * B)
                rest = slice((kk + 1) * B, width)
                dh, dl = split(jnp.where(r <= c, w_ref[:, :B], 0.0))
                lh[here, here] = dh.T
                ll[here, here] = dl.T
                if kk < width // B - 1:
                    rh, rl = split(dot3(vs, split(s_ref[here, rest])))
                    uh[here, rest] = rh
                    ul[here, rest] = rl
                    lh[rest, here] = rh.T
                    ll[rest, here] = rl.T
                if kk < rows // B - 1:
                    lh[here, (kk + 1) * B:rows] = jnp.zeros((B, rows - (kk + 1) * B), bf16)
                    ll[here, (kk + 1) * B:rows] = jnp.zeros((B, rows - (kk + 1) * B), bf16)
                half = kk % 2
                at = half * B
                ih[kk // 2, at:at + B, at:at + B] = vs[0]
                il[kk // 2, at:at + B, at:at + B] = vs[1]
                if half:
                    before = slice((kk - 1) * B, kk * B)
                    first = split(v_ref[0])
                    cross = split(dot3((lh[here, before], ll[here, before]), first))
                    th, tl = split(-dot3(vs, cross))
                    ih[kk // 2, B:, :B] = th
                    il[kk // 2, B:, :B] = tl
                    ih[kk // 2, :B, B:] = jnp.zeros((B, B), bf16)
                    il[kk // 2, :B, B:] = jnp.zeros((B, B), bf16)
        return 0

    lax.fori_loop(0, rows // B, step, 0)


def chol_head_kernel(at_ref, *refs):
    pieces = refs[:8]
    lh, ll, ih, il, next_ref, uh, ul, s_ref, w_ref, v_ref = refs[8:]
    row = at_ref[0]
    col = at_ref[1]
    for par in range(2):
        @pl.when(row % 2 == par)
        def _():
            for k in range(16):
                here = pl.ds(pl.multiple_of(jnp.bitwise_xor(col, k) * PC, PC), PC)
                s_ref[here, 512 * par:512 * (par + 1)] = pieces[k // 4][k % 4]
                s_ref[here, 512 * (1 - par):512 * (2 - par)] = pieces[4 + k // 4][k % 4]
    for i in range(NB):
        for j in range(i, NB):
            up = s_ref[i * B:(i + 1) * B, j * B:(j + 1) * B]
            dn = s_ref[j * B:(j + 1) * B, i * B:(i + 1) * B]
            s_ref[i * B:(i + 1) * B, j * B:(j + 1) * B] = 0.5 * (up + dn.T)
    factor_blocks(HF, PB, s_ref, w_ref, v_ref, uh, ul, lh, ll, ih, il)
    left = (lh[HF:, :], ll[HF:, :])
    next_ref[...] = s_ref[HF:, HF:] - dot3(left, (uh[:, HF:], ul[:, HF:]))


def chol_tail_kernel(s_in, lh, ll, ih, il, uh, ul, s_ref, w_ref, v_ref):
    s_ref[...] = s_in[...]
    factor_blocks(HF, HF, s_ref, w_ref, v_ref, uh, ul, lh, ll, ih, il)


def chol_call(kernel, name, width, extra_out, args):
    part = jax.ShapeDtypeStruct((width, HF), bf16)
    inv = jax.ShapeDtypeStruct((HF // Q, Q, Q), bf16)
    vmem = pl.BlockSpec(memory_space=pltpu.VMEM)
    return pl.pallas_call(
        kernel,
        name=name,
        out_shape=(part, part, inv, inv) + extra_out,
        in_specs=[pl.BlockSpec(memory_space=pltpu.SMEM) if a.dtype == jnp.int32 else vmem for a in args],
        out_specs=(vmem,) * (4 + len(extra_out)),
        scratch_shapes=[
            pltpu.VMEM((HF, width), bf16),
            pltpu.VMEM((HF, width), bf16),
            pltpu.VMEM((width, width), f32),
            pltpu.VMEM((B, 2 * B), f32),
            pltpu.VMEM((2, B, B), f32),
        ],
        compiler_params=pltpu.CompilerParams(vmem_limit_bytes=58 * MB),
        cost_estimate=pl.CostEstimate(flops=25_000_000_000, transcendentals=0, bytes_accessed=8 * MB),
    )(*args)


def chol_head(at, pieces):
    nxt = jax.ShapeDtypeStruct((HF, HF), f32)
    return chol_call(chol_head_kernel, "chol_head", PB, (nxt,), [at, *pieces])


def chol_tail(nxt):
    return chol_call(chol_tail_kernel, "chol_tail", HF, (), [nxt])


def finish_kernel(at_ref, w0, w1, w2, w3, pan, got, trail, child_a, child_b,
                  lh1, ll1, ih1, il1, lh2, ll2, ih2, il2,
                  fac_out, out_out,
                  a_ref, p_ref, t_ref, c_ref, g_ref, lh, ll, ih, il, xh, xl, wh, wl, ch, cl,
                  fac_ref, out_ref, sem, pan_sem, trail_sem, out_sem):
    row = at_ref[0]
    col = at_ref[1]
    copy = pltpu.make_async_copy
    lo, hi = pl.ds(0, HF), pl.ds(HF, HF)
    loads = [
        copy(ih1, ih.at[pl.ds(0, 2)], sem.at[0]), copy(il1, il.at[pl.ds(0, 2)], sem.at[1]),
        copy(lh1, lh.at[:, lo], sem.at[2]), copy(ll1, ll.at[:, lo], sem.at[3]),
        copy(ih2, ih.at[pl.ds(2, 2)], sem.at[4]), copy(il2, il.at[pl.ds(2, 2)], sem.at[5]),
        copy(lh2, lh.at[hi, hi], sem.at[6]), copy(ll2, ll.at[hi, hi], sem.at[7]),
    ]
    for k in range(8):
        here = pl.ds(pl.multiple_of(jnp.bitwise_xor(row, k) * B, B), B)
        loads.append(copy((w0, w1, w2, w3)[k // 2].at[k % 2], a_ref.at[here], sem.at[8 + k]))
    late = [
        copy(child_a, c_ref.at[pl.ds(0, CR // 2)], sem.at[16]),
        copy(child_b, c_ref.at[pl.ds(CR // 2, CR // 2)], sem.at[17]),
        copy(got.at[pl.ds(PC, 8)], g_ref, sem.at[18]),
    ]

    def panel_copy(n):
        return copy(pan.at[:, pl.ds(n * 512, 512)], p_ref.at[n], pan_sem.at[n])

    def trail_copy(n):
        return copy(trail.at[pl.ds(n * 512, 512)], t_ref.at[n], trail_sem.at[n])

    def fac_copy(n):
        return copy(fac_ref.at[n], fac_out.at[:, pl.ds(n * 512, 512)], out_sem.at[n])

    def out_copy(n):
        return copy(out_ref.at[n], out_out.at[pl.ds(n * 512, 512)], out_sem.at[3 + n])

    for d in loads:
        d.start()
    panel_copy(0).start()
    for d in late:
        d.start()
    for n in range(3):
        if n:
            panel_copy(n).start()
        trail_copy(n).start()
    for d in loads:
        d.wait()

    def solve(src, yh, yl):
        for k in range(PB // Q):
            here = slice(k * Q, (k + 1) * Q)
            v = src[here, :]
            if k:
                v = v - dot3((lh[here, :k * Q], ll[here, :k * Q]), (yh[:k * Q, :], yl[:k * Q, :]))
            yh[here, :], yl[here, :] = split(dot3((ih[k], il[k]), split(v)))

    solve(a_ref, wh, wl)
    for d in late:
        d.wait()
    ch[...], cl[...] = split(c_ref[...])
    target = g_ref[0:1, :CR].astype(jnp.int32)
    mine = pl.ds(pl.multiple_of(col * PC, PC), PC)

    def block(n, _):
        panel_copy(n).wait()
        own = jnp.logical_and(row == 0, n < 2)

        @pl.when(own)
        def _():
            here = pl.ds(pl.multiple_of(n * 512, 512), 512)
            xh[...] = lh[here, :].T
            xl[...] = ll[here, :].T

        @pl.when(jnp.logical_and(row == 0, n == 0))
        def _():
            xh[HF:, :] = jnp.zeros((HF, 512), bf16)
            xl[HF:, :] = jnp.zeros((HF, 512), bf16)

        @pl.when(jnp.logical_not(own))
        def _():
            solve(p_ref.at[n], xh, xl)

        fac_ref[n] = xh[mine, :].astype(f32) + xl[mine, :].astype(f32)
        fac_copy(n).start()
        g = one_hot(n * 512, 512, target)
        moved = dot1(g, ch[...]) + dot1(g, cl[...])
        prod = dot3((xh[...], xl[...]), (wh[...], wl[...]), LHS_T)
        trail_copy(n).wait()
        out_ref[n] = t_ref[n] + (moved - prod)
        out_copy(n).start()
        return 0

    lax.fori_loop(0, 3, block, 0)
    for n in range(3):
        fac_copy(n).wait()
        out_copy(n).wait()


def finish(at, window, panel, got, trail, child, head, tail):
    hbm = pl.BlockSpec(memory_space=pl.ANY)
    dma = pltpu.SemaphoreType.DMA
    vm = pltpu.VMEM
    return pl.pallas_call(
        finish_kernel,
        name="finish",
        out_shape=(jax.ShapeDtypeStruct((PC, FR), f32), jax.ShapeDtypeStruct((FR, TC), f32)),
        in_specs=[pl.BlockSpec(memory_space=pltpu.SMEM)] + [hbm] * 17,
        out_specs=(hbm, hbm),
        scratch_shapes=[
            vm((PB, TC), f32), vm((3, PB, 512), f32), vm((3, 512, TC), f32), vm((CR, TC), f32),
            vm((8, FR), f32),
            vm((PB, PB), bf16), vm((PB, PB), bf16),
            vm((PB // Q, Q, Q), bf16), vm((PB // Q, Q, Q), bf16),
            vm((PB, 512), bf16), vm((PB, 512), bf16), vm((PB, TC), bf16), vm((PB, TC), bf16),
            vm((CR, TC), bf16), vm((CR, TC), bf16),
            vm((3, PC, 512), f32), vm((3, 512, TC), f32),
            dma((19,)), dma((3,)), dma((3,)), dma((6,)),
        ],
        compiler_params=pltpu.CompilerParams(vmem_limit_bytes=58 * MB),
        cost_estimate=pl.CostEstimate(flops=15_000_000_000, transcendentals=0, bytes_accessed=25 * MB),
    )(at, *window, panel, got, trail, *child, *head, *tail)


def flip(x, axis, bit, size):
    return lax.ppermute(x, axis, [(i, i ^ bit) for i in range(size)])


def window_pairs(step):
    pairs = []
    for c in range(16):
        for parity in range(2):
            if ((c + 2) % 3 + parity) % 3 == step:
                for r in range(8):
                    pairs.append((((c + 2) // 3) * 16 + 2 * r + parity, r * 16 + c))
    return pairs


def on_device(front_panel, front_trail, child_panel, child_trail, child_map, child_count):
    row = lax.axis_index("row")
    col = lax.axis_index("col")
    at = jnp.stack([row, col]).astype(jnp.int32)

    count = child_count.T
    own, send, crit = panel_parts(
        at, count, child_map, front_panel.T, child_panel.transpose(0, 2, 1)
    )
    there = lax.ppermute(crit, "row", [(0, 4), (4, 0)])
    there, send = lax.optimization_barrier((there, send))
    got = flip(send, "row", 4, 8)
    diag = crit + there
    lo, hi = diag[:, :512], diag[:, 512:]
    half = jnp.where(row % 4 == 0, lo, 0.0)
    for k, part in ((1, hi), (2, lo), (3, hi)):
        half = half + lax.ppermute(part, "row", [(0, k), (4, 4 + k)])
    x4 = jnp.stack([half] + [flip(half, "col", b, 16) for b in (1, 2, 3)])
    x4, got, count, child_a = lax.optimization_barrier((x4, got, count, child_trail[1, :CR // 2]))
    child_a = flip(child_a, "row", 4, 8)
    mine = [x4] + [flip(x4, "col", b, 16) for b in (4, 8, 12)]
    other = [flip(x4, "row", 1, 8)]
    panel_t = own + got[:PC]
    trail = trail_own(count, child_map, front_trail, child_trail)
    *mine, panel_t, trail, child_a, child_b = lax.optimization_barrier(
        (*mine, panel_t, trail, child_a, child_trail[1, CR // 2:])
    )
    other += [flip(piece, "row", 1, 8) for piece in mine[1:]]
    panel_full = lax.all_gather(panel_t, "col", axis=0, tiled=True)
    child_b = flip(child_b, "row", 4, 8)

    odd = jnp.bitwise_and(col, 1)
    panes = [panel_t[:, 512 * w:512 * (w + 1)] for w in range(3)]
    steps = [
        lax.ppermute(jnp.where(odd == 0, panes[k], panes[(k + 2) % 3]), ("row", "col"), window_pairs(k))
        for k in range(3)
    ]
    *head, nxt = chol_head(at, mine + other)
    *steps, nxt, child_b = lax.optimization_barrier((*steps, nxt, child_b))
    at_w = (col + 2) % 3
    first = jnp.where(at_w == 0, steps[0], jnp.where(at_w == 1, steps[1], steps[2]))
    second = jnp.where(at_w == 0, steps[1], jnp.where(at_w == 1, steps[2], steps[0]))
    win = jnp.concatenate([first, second], axis=0)
    pair = jnp.stack([win, flip(win, "row", 1, 8)])
    window = [pair] + [flip(pair, "row", b, 8) for b in (2, 4, 6)]
    tail = chol_tail(nxt)

    factor_t, schur = finish(at, window, panel_full, got, trail, [child_a, child_b], head, tail)
    return factor_t.T, schur


def solution(mesh):
    in_specs = (
        P("row", "col"),
        P("row", "col"),
        P(None, "row", "col"),
        P(None, "row", "col"),
        P(None, "row"),
        P(None, "row"),
    )
    out_specs = (P("row", "col"), P("row", "col"))
    return jax.shard_map(
        on_device, mesh=mesh, in_specs=in_specs, out_specs=out_specs, check_vma=False
    )
```

time: 297 us -> 185 us (0.62)
  the two profiles are of different devices: /device:TPU:11 before, /device:TPU:9 now
where the time goes in v2:
time: 185 us; the launch traced here: 184 us
  Pallas kernels  92.1 us (50%)
  starting transfers between devices  44.5 us (24%)
  waiting for transfers between devices  26.7 us (14%)
  between operations  14.4 us (8%)
  other arithmetic  3.65 us (2%)
  local copies, waits for them, and re-layouts  2.84 us (2%)
    pallas_call x2, Pallas kernels, chol_call(): pl.pallas_call(kernel, name=name, out_shape=(part, part, inv, inv) + extr...  55.1 us
    ppermute x17, starting transfers between devices, flip(): return lax.ppermute(x, axis, [(i, i ^ bit) for i in range(size)])  28.8 us
    pallas_call x1, Pallas kernels, finish(): pl.pallas_call(finish_kernel, name='finish', out_shape=(jax.ShapeDtypeStr...  25.3 us
    ppermute x17, waiting for transfers between devices, flip(): return lax.ppermute(x, axis, [(i, i ^ bit) for i in range(size)])  16.9 us
    ppermute x3, starting transfers between devices, on_device(): lax.ppermute(jnp.where(odd == 0, panes[k], panes[(k + 2) % 3]), ('row', '...  12.3 us
    ppermute x3, waiting for transfers between devices, on_device(): half = half + lax.ppermute(part, 'row', [(0, k), (4, 4 + k)])  9.73 us
    pallas_call x1, Pallas kernels, trail_own(): pl.pallas_call(trail_kernel, name='trail_own', grid=(FR // 512,), out_sha...  7.35 us
    pallas_call x1, Pallas kernels, panel_parts(): pl.pallas_call(panel_kernel, name='panel_parts', out_shape=(jax.ShapeDtyp...  4.36 us
  transfers between devices with their start and end apart: 25, of which 6 were waited for; matrix products, arithmetic and copies ran while one was open for 2% of the time, Pallas kernels for 34%

profile of v2, /device:TPU:9, one launch (start us, length us, event | category | flops | bytes accessed | tf_op | source)
XLA Modules:
  0.0 184.1 jit_solution(3895311629523280125)
XLA Ops:
  7.8 4.4 %panel_parts.1 = (f32[64,1536]{1,0:T(8,128)}, f32[72,1536]{1,0:T(8,128)}, f32[64,1024]{1,0:T(8,128)}) custom-call(s32[2]{0:T(128)} %pad_add_fusion.at_ref, s32[1,2]{1,0:T(1,128)} %bitcast.24, s32[2,1024]{1,0:T(2,128)} %map_ref.3, f32[64,1536]{1,0:T(8,128)} %bitcast.19, f32[2,64,1024]{2,1,0:T(8,128)} %bitcast.17), custom_call_target="tpu_custom_call" | custom-call | tf_op jit(solution)/shard_map/panel_parts/pallas_call | solution.py:79
  15.2 1.3 collective-permute-start.1
  16.6 3.7 %collective-permute-start.7 = (f32[72,1536]{1,0:T(8,128)}, f32[72,1536]{1,0:T(8,128)S(1)}, u32[]{:S(2)}, u32[]{:S(2)}) collective-permute-start(f32[72,1536]{1,0:T(8,128)} %get-tuple-element.38), channel_id=1, source_target_pairs={{0,64},{16,80},{32,96},{48,112},{64,0},{80,16},{96,32},{112,48},{1... | collective-permute-start | bytes 1327112 | tf_op jit(solution)/shard_map/ppermute | solution.py:421
  20.2 9.7 %collective-permute-done.1 = f32[64,512]{1,0:T(8,128)S(1)} collective-permute-done((f32[64,512]{1,0:T(8,128)S(1)}, f32[64,512]{1,0:T(8,128)S(1)}, u32[]{:S(2)}, u32[]{:S(2)}) %collective-permute-start.1) | collective-permute-done | bytes 131104 | tf_op jit(solution)/shard_map/ppermute | solution.py:450
  30.0 2.6 %collective-permute-start.6 = (f32[64,512]{1,0:T(8,128)S(1)}, f32[64,512]{1,0:T(8,128)S(1)}, u32[]{:S(2)}, u32[]{:S(2)}) collective-permute-start(f32[64,512]{1,0:T(8,128)S(1)} %add_add_fusion), channel_id=1, source_target_pairs={{0,3},{1,2},{2,1},{3,0},{4,7},{5,6},{6,5},{7,4},{8,11},{9,10},{10,... | collective-permute-start | bytes 393224 | tf_op jit(solution)/shard_map/ppermute | solution.py:421
  33.3 1.7 slice_bitcast_fusion
  35.9 2.3 %collective-permute-done.5 = f32[64,512]{1,0:T(8,128)S(1)} collective-permute-done((f32[64,512]{1,0:T(8,128)S(1)}, f32[64,512]{1,0:T(8,128)S(1)}, u32[]{:S(2)}, u32[]{:S(2)}) %collective-permute-start.5) | collective-permute-done | bytes 131104 | tf_op jit(solution)/shard_map/ppermute | solution.py:421
  38.3 4.5 %collective-permute-start.11 = (f32[512,512]{1,0:T(8,128)S(1)}, f32[512,512]{1,0:T(8,128)}, u32[]{:S(2)}, u32[]{:S(2)}) collective-permute-start(f32[512,512]{1,0:T(8,128)S(1)} %get-tuple-element.43), channel_id=1, source_target_pairs={{0,64},{16,80},{32,96},{48,112},{64,0},{80,16},{96,32},{112,48},{1... | collective-permute-start | bytes 3145736 | tf_op jit(solution)/shard_map/ppermute | solution.py:421
  42.8 1.3 collective-permute-start.10
  44.8 1.2 collective-permute-start.8
  46.0 7.3 %trail_own.1.trail = f32[1536,512]{1,0:T(8,128)} custom-call(s32[1,2]{1,0:T(1,128)} %bitcast.25, s32[2,1024]{1,0:T(2,128)} %map_ref.3, f32[1536,512]{1,0:T(8,128)} %front_ref.1, f32[2,1024,512]{2,1,0:T(8,128)} %child_ref.1), custom_call_target="tpu_custom_call" | custom-call | tf_op jit(solution)/shard_map/trail_own/pallas_call | solution.py:104
  54.2 11.0 %collective-permute-done.10.refs_3_ = f32[4,64,512]{2,1,0:T(8,128)} collective-permute-done((f32[4,64,512]{2,1,0:T(8,128)S(1)}, f32[4,64,512]{2,1,0:T(8,128)}, u32[]{:S(2)}, u32[]{:S(2)}) %collective-permute-start.10) | collective-permute-done | bytes 524320 | tf_op jit(solution)/shard_map/ppermute | solution.py:421
  65.2 1.5 collective-permute-done.8.refs_1_
  66.8 3.6 %collective-permute-start.15 = (f32[4,64,512]{2,1,0:T(8,128)S(1)}, f32[4,64,512]{2,1,0:T(8,128)S(1)}, u32[]{:S(2)}, u32[]{:S(2)}) collective-permute-start(f32[4,64,512]{2,1,0:T(8,128)S(1)} %pad_maximum_fusion.refs_0_), channel_id=1, source_target_pairs={{0,16},{16,0},{32,48},{48,32},{64,80},{80,64},{96,112},{112,96},{1... | collective-permute-start | bytes 1572872 | tf_op jit(solution)/shard_map/ppermute | solution.py:421
  72.1 6.9 %collective-permute-start.14 = (f32[64,512]{1,0:T(8,128)S(1)}, f32[64,512]{1,0:T(8,128)S(1)}, u32[]{:S(2)}, u32[]{:S(2)}) collective-permute-start(f32[64,512]{1,0:T(8,128)S(1)} %get-tuple-element.72), channel_id=1, source_target_pairs={{0,0},{2,16},{4,32},{6,48},{8,64},{10,80},{12,96},{14,112},{17,2},... | collective-permute-start | bytes 393224 | tf_op jit(solution)/shard_map/ppermute | solution.py:468
  78.9 2.2 %collective-permute-start.13 = (f32[64,512]{1,0:T(8,128)S(1)}, f32[64,512]{1,0:T(8,128)S(1)}, u32[]{:S(2)}, u32[]{:S(2)}) collective-permute-start(f32[64,512]{1,0:T(8,128)S(1)} %get-tuple-element.73), channel_id=1, source_target_pairs={{17,1},{19,17},{21,33},{23,49},{25,65},{27,81},{29,97},{31,113},{1... | collective-permute-start | bytes 393224 | tf_op jit(solution)/shard_map/ppermute | solution.py:468
  81.2 3.3 %collective-permute-start.12 = (f32[64,512]{1,0:T(8,128)S(1)}, f32[64,512]{1,0:T(8,128)S(1)}, u32[]{:S(2)}, u32[]{:S(2)}) collective-permute-start(f32[64,512]{1,0:T(8,128)S(1)} %get-tuple-element.74), channel_id=1, source_target_pairs={{1,0},{3,16},{5,32},{7,48},{9,64},{11,80},{13,96},{15,112},{16,1},... | collective-permute-start | bytes 393224 | tf_op jit(solution)/shard_map/ppermute | solution.py:468
  84.5 3.0 %collective-permute-start.19 = (f32[512,512]{1,0:T(8,128)S(1)}, f32[512,512]{1,0:T(8,128)S(1)}, u32[]{:S(2)}, u32[]{:S(2)}) collective-permute-start(f32[512,512]{1,0:T(8,128)S(1)} %get-tuple-element.50), channel_id=1, source_target_pairs={{0,64},{16,80},{32,96},{48,112},{64,0},{80,16},{96,32},{112,48},{1... | collective-permute-start | bytes 3145736 | tf_op jit(solution)/shard_map/ppermute | solution.py:421
  87.5 29.4 %chol_head.1 = (bf16[1024,512]{1,0:T(8,128)(2,1)}, bf16[1024,512]{1,0:T(8,128)(2,1)}, bf16[2,256,256]{2,1,0:T(8,128)(2,1)}, bf16[2,256,256]{2,1,0:T(8,128)(2,1)}, f32[512,512]{1,0:T(8,128)}) custom-call(s32[2]{0:T(128)} %pad_add_fusion.at_ref, f32[4,64,512]{2,1,0:T(8,128)} %copy-done, f32[4,64,512]{2,1,0:T(8,128)} %collective-permute-done.8.refs_1_, ...), custom_call_target="tpu_custom_call" | custom-call | flops 24999999488 | bytes 8388608 | tf_op jit(solution)/shard_map/chol_head/pallas_call | solution.py:270
  117.0 3.5 %collective-permute-start.20 = (f32[128,512]{1,0:T(8,128)S(1)}, f32[128,512]{1,0:T(8,128)S(1)}, u32[]{:S(2)}, u32[]{:S(2)}) collective-permute-start(f32[128,512]{1,0:T(8,128)S(1)} %get-tuple-element.76), channel_id=1, source_target_pairs={{0,16},{16,0},{32,48},{48,32},{64,80},{80,64},{96,112},{112,96},{1... | collective-permute-start | bytes 786440 | tf_op jit(solution)/shard_map/ppermute | solution.py:421
  120.5 1.2 collective-permute-done.20
  121.9 3.1 %collective-permute-start.21 = (f32[2,128,512]{2,1,0:T(8,128)S(1)}, f32[2,128,512]{2,1,0:T(8,128)S(1)}, u32[]{:S(2)}, u32[]{:S(2)}) collective-permute-start(f32[2,128,512]{2,1,0:T(8,128)S(1)} %pad_maximum_fusion.1.w0), channel_id=1, source_target_pairs={{0,32},{16,48},{32,0},{48,16},{64,96},{80,112},{96,64},{112,80},{1... | collective-permute-start | bytes 1572872 | tf_op jit(solution)/shard_map/ppermute | solution.py:421
  125.0 25.7 %chol_tail.1 = (bf16[512,512]{1,0:T(8,128)(2,1)}, bf16[512,512]{1,0:T(8,128)(2,1)}, bf16[2,256,256]{2,1,0:T(8,128)(2,1)}, bf16[2,256,256]{2,1,0:T(8,128)(2,1)}) custom-call(f32[512,512]{1,0:T(8,128)} %get-tuple-element.61.s_in), custom_call_target="tpu_custom_call" | custom-call | flops 24999999488 | bytes 8388608 | tf_op jit(solution)/shard_map/chol_tail/pallas_call | solution.py:270
  151.9 25.3 %finish.1 = (f32[64,1536]{1,0:T(8,128)}, f32[1536,512]{1,0:T(8,128)}) custom-call(s32[2]{0:T(128)} %pad_add_fusion.at_ref, f32[2,128,512]{2,1,0:T(8,128)} %copy-done.1, f32[2,128,512]{2,1,0:T(8,128)} %copy-done.9, f32[2,128,512]{2,1,0:T(8,128)} %copy-done.8, f32[2,128,512]{2,1,0:T(8,128)} %copy-done.7, f32[1024,1536]{1,0:T(8,128)} %all-gather.2.cloned.1.call-done.pan, ...), custom_call_target="tpu_custom_call" | custom-call | flops 15000000512 | bytes 26214400 | tf_op jit(solution)/shard_map/finish/pallas_call | solution.py:399
  (63 shorter events, 10.0 us)
Async XLA Ops:
  7.2 143.7 %all-gather.2.cloned.1.call-start = ((), (), s32[]{:S(2)}) async-start(), calls=%async_computation | async-start | bytes 6684672 | tf_op jit(solution)/shard_map/all_gather | solution.py:462
  13.9 6.3 %collective-permute-start.2 = (f32[64,512]{1,0:T(8,128)S(1)}, f32[64,512]{1,0:T(8,128)S(1)}, u32[]{:S(2)}, u32[]{:S(2)}) collective-permute-start(f32[64,512]{1,0:T(8,128)S(1)} %get-tuple-element.77), channel_id=1, source_target_pairs={{0,32},{64,96},{1,33},{65,97},{2,34},{66,98},{3,35},{67,99},{4,36}... | collective-permute-start | bytes 393224 | tf_op jit(solution)/shard_map/ppermute | solution.py:450
  14.6 5.7 %collective-permute-start.3 = (f32[64,512]{1,0:T(8,128)S(1)}, f32[64,512]{1,0:T(8,128)S(1)}, u32[]{:S(2)}, u32[]{:S(2)}) collective-permute-start(f32[64,512]{1,0:T(8,128)S(1)} %get-tuple-element.78), channel_id=1, source_target_pairs={{0,48},{64,112},{1,49},{65,113},{2,50},{66,114},{3,51},{67,115},{4... | collective-permute-start | bytes 393224 | tf_op jit(solution)/shard_map/ppermute | solution.py:450
  15.2 14.7 %collective-permute-start.1 = (f32[64,512]{1,0:T(8,128)S(1)}, f32[64,512]{1,0:T(8,128)S(1)}, u32[]{:S(2)}, u32[]{:S(2)}) collective-permute-start(f32[64,512]{1,0:T(8,128)S(1)} %get-tuple-element.78), channel_id=1, source_target_pairs={{0,16},{64,80},{1,17},{65,81},{2,18},{66,82},{3,19},{67,83},{4,20}... | collective-permute-start | bytes 393224 | tf_op jit(solution)/shard_map/ppermute | solution.py:450
  16.6 21.7 %collective-permute-start.7 = (f32[72,1536]{1,0:T(8,128)}, f32[72,1536]{1,0:T(8,128)S(1)}, u32[]{:S(2)}, u32[]{:S(2)}) collective-permute-start(f32[72,1536]{1,0:T(8,128)} %get-tuple-element.38), channel_id=1, source_target_pairs={{0,64},{16,80},{32,96},{48,112},{64,0},{80,16},{96,32},{112,48},{1... | collective-permute-start | bytes 1327112 | tf_op jit(solution)/shard_map/ppermute | solution.py:421
  30.0 5.9 %collective-permute-start.6 = (f32[64,512]{1,0:T(8,128)S(1)}, f32[64,512]{1,0:T(8,128)S(1)}, u32[]{:S(2)}, u32[]{:S(2)}) collective-permute-start(f32[64,512]{1,0:T(8,128)S(1)} %add_add_fusion), channel_id=1, source_target_pairs={{0,3},{1,2},{2,1},{3,0},{4,7},{5,6},{6,5},{7,4},{8,11},{9,10},{10,... | collective-permute-start | bytes 393224 | tf_op jit(solution)/shard_map/ppermute | solution.py:421
  32.6 5.6 %collective-permute-start.5 = (f32[64,512]{1,0:T(8,128)S(1)}, f32[64,512]{1,0:T(8,128)S(1)}, u32[]{:S(2)}, u32[]{:S(2)}) collective-permute-start(f32[64,512]{1,0:T(8,128)S(1)} %add_add_fusion), channel_id=1, source_target_pairs={{0,2},{1,3},{2,0},{3,1},{4,6},{5,7},{6,4},{7,5},{8,10},{9,11},{10,... | collective-permute-start | bytes 393224 | tf_op jit(solution)/shard_map/ppermute | solution.py:421
  33.1 5.1 %collective-permute-start.4 = (f32[64,512]{1,0:T(8,128)S(1)}, f32[64,512]{1,0:T(8,128)S(1)}, u32[]{:S(2)}, u32[]{:S(2)}) collective-permute-start(f32[64,512]{1,0:T(8,128)S(1)} %add_add_fusion), channel_id=1, source_target_pairs={{0,1},{1,0},{2,3},{3,2},{4,5},{5,4},{6,7},{7,6},{8,9},{9,8},{10,11... | collective-permute-start | bytes 393224 | tf_op jit(solution)/shard_map/ppermute | solution.py:421
  38.3 28.5 %collective-permute-start.11 = (f32[512,512]{1,0:T(8,128)S(1)}, f32[512,512]{1,0:T(8,128)}, u32[]{:S(2)}, u32[]{:S(2)}) collective-permute-start(f32[512,512]{1,0:T(8,128)S(1)} %get-tuple-element.43), channel_id=1, source_target_pairs={{0,64},{16,80},{32,96},{48,112},{64,0},{80,16},{96,32},{112,48},{1... | collective-permute-start | bytes 3145736 | tf_op jit(solution)/shard_map/ppermute | solution.py:421
  42.8 22.4 %collective-permute-start.10 = (f32[4,64,512]{2,1,0:T(8,128)S(1)}, f32[4,64,512]{2,1,0:T(8,128)}, u32[]{:S(2)}, u32[]{:S(2)}) collective-permute-start(f32[4,64,512]{2,1,0:T(8,128)S(1)} %pad_maximum_fusion.refs_0_), channel_id=1, source_target_pairs={{0,12},{1,13},{2,14},{3,15},{4,8},{5,9},{6,10},{7,11},{8,4},{9,5},... | collective-permute-start | bytes 1572872 | tf_op jit(solution)/shard_map/ppermute | solution.py:421
  44.1 21.1 %collective-permute-start.9 = (f32[4,64,512]{2,1,0:T(8,128)S(1)}, f32[4,64,512]{2,1,0:T(8,128)}, u32[]{:S(2)}, u32[]{:S(2)}) collective-permute-start(f32[4,64,512]{2,1,0:T(8,128)S(1)} %pad_maximum_fusion.refs_0_), channel_id=1, source_target_pairs={{0,8},{1,9},{2,10},{3,11},{4,12},{5,13},{6,14},{7,15},{8,0},{9,1},... | collective-permute-start | bytes 1572872 | tf_op jit(solution)/shard_map/ppermute | solution.py:421
  44.8 21.9 %collective-permute-start.8 = (f32[4,64,512]{2,1,0:T(8,128)S(1)}, f32[4,64,512]{2,1,0:T(8,128)}, u32[]{:S(2)}, u32[]{:S(2)}) collective-permute-start(f32[4,64,512]{2,1,0:T(8,128)S(1)} %pad_maximum_fusion.refs_0_), channel_id=1, source_target_pairs={{0,4},{1,5},{2,6},{3,7},{4,0},{5,1},{6,2},{7,3},{8,12},{9,13},{10,... | collective-permute-start | bytes 1572872 | tf_op jit(solution)/shard_map/ppermute | solution.py:421
  66.8 12.2 %collective-permute-start.15 = (f32[4,64,512]{2,1,0:T(8,128)S(1)}, f32[4,64,512]{2,1,0:T(8,128)S(1)}, u32[]{:S(2)}, u32[]{:S(2)}) collective-permute-start(f32[4,64,512]{2,1,0:T(8,128)S(1)} %pad_maximum_fusion.refs_0_), channel_id=1, source_target_pairs={{0,16},{16,0},{32,48},{48,32},{64,80},{80,64},{96,112},{112,96},{1... | collective-permute-start | bytes 1572872 | tf_op jit(solution)/shard_map/ppermute | solution.py:421
  70.4 10.7 %collective-permute-start.16 = (f32[4,64,512]{2,1,0:T(8,128)}, f32[4,64,512]{2,1,0:T(8,128)S(1)}, u32[]{:S(2)}, u32[]{:S(2)}) collective-permute-start(f32[4,64,512]{2,1,0:T(8,128)} %collective-permute-done.8.refs_1_), channel_id=1, source_target_pairs={{0,16},{16,0},{32,48},{48,32},{64,80},{80,64},{96,112},{112,96},{1... | collective-permute-start | bytes 1572872 | tf_op jit(solution)/shard_map/ppermute | solution.py:421
  70.5 14.0 %collective-permute-start.17 = (f32[4,64,512]{2,1,0:T(8,128)}, f32[4,64,512]{2,1,0:T(8,128)}, u32[]{:S(2)}, u32[]{:S(2)}) collective-permute-start(f32[4,64,512]{2,1,0:T(8,128)} %collective-permute-done.9.refs_2_), channel_id=1, source_target_pairs={{0,16},{16,0},{32,48},{48,32},{64,80},{80,64},{96,112},{112,96},{1... | collective-permute-start | bytes 1572872 | tf_op jit(solution)/shard_map/ppermute | solution.py:421
  70.9 16.6 %collective-permute-start.18 = (f32[4,64,512]{2,1,0:T(8,128)}, f32[4,64,512]{2,1,0:T(8,128)}, u32[]{:S(2)}, u32[]{:S(2)}) collective-permute-start(f32[4,64,512]{2,1,0:T(8,128)} %collective-permute-done.10.refs_3_), channel_id=1, source_target_pairs={{0,16},{16,0},{32,48},{48,32},{64,80},{80,64},{96,112},{112,96},{1... | collective-permute-start | bytes 1572872 | tf_op jit(solution)/shard_map/ppermute | solution.py:421
  72.1 44.8 %collective-permute-start.14 = (f32[64,512]{1,0:T(8,128)S(1)}, f32[64,512]{1,0:T(8,128)S(1)}, u32[]{:S(2)}, u32[]{:S(2)}) collective-permute-start(f32[64,512]{1,0:T(8,128)S(1)} %get-tuple-element.72), channel_id=1, source_target_pairs={{0,0},{2,16},{4,32},{6,48},{8,64},{10,80},{12,96},{14,112},{17,2},... | collective-permute-start | bytes 393224 | tf_op jit(solution)/shard_map/ppermute | solution.py:468
  78.9 37.9 %collective-permute-start.13 = (f32[64,512]{1,0:T(8,128)S(1)}, f32[64,512]{1,0:T(8,128)S(1)}, u32[]{:S(2)}, u32[]{:S(2)}) collective-permute-start(f32[64,512]{1,0:T(8,128)S(1)} %get-tuple-element.73), channel_id=1, source_target_pairs={{17,1},{19,17},{21,33},{23,49},{25,65},{27,81},{29,97},{31,113},{1... | collective-permute-start | bytes 393224 | tf_op jit(solution)/shard_map/ppermute | solution.py:468
  81.2 35.7 %collective-permute-start.12 = (f32[64,512]{1,0:T(8,128)S(1)}, f32[64,512]{1,0:T(8,128)S(1)}, u32[]{:S(2)}, u32[]{:S(2)}) collective-permute-start(f32[64,512]{1,0:T(8,128)S(1)} %get-tuple-element.74), channel_id=1, source_target_pairs={{1,0},{3,16},{5,32},{7,48},{9,64},{11,80},{13,96},{15,112},{16,1},... | collective-permute-start | bytes 393224 | tf_op jit(solution)/shard_map/ppermute | solution.py:468
  84.5 32.4 %collective-permute-start.19 = (f32[512,512]{1,0:T(8,128)S(1)}, f32[512,512]{1,0:T(8,128)S(1)}, u32[]{:S(2)}, u32[]{:S(2)}) collective-permute-start(f32[512,512]{1,0:T(8,128)S(1)} %get-tuple-element.50), channel_id=1, source_target_pairs={{0,64},{16,80},{32,96},{48,112},{64,0},{80,16},{96,32},{112,48},{1... | collective-permute-start | bytes 3145736 | tf_op jit(solution)/shard_map/ppermute | solution.py:421
  117.0 4.7 %collective-permute-start.20 = (f32[128,512]{1,0:T(8,128)S(1)}, f32[128,512]{1,0:T(8,128)S(1)}, u32[]{:S(2)}, u32[]{:S(2)}) collective-permute-start(f32[128,512]{1,0:T(8,128)S(1)} %get-tuple-element.76), channel_id=1, source_target_pairs={{0,16},{16,0},{32,48},{48,32},{64,80},{80,64},{96,112},{112,96},{1... | collective-permute-start | bytes 786440 | tf_op jit(solution)/shard_map/ppermute | solution.py:421
  121.7 29.1 %collective-permute-start.23 = (f32[2,128,512]{2,1,0:T(8,128)S(1)}, f32[2,128,512]{2,1,0:T(8,128)S(1)}, u32[]{:S(2)}, u32[]{:S(2)}) collective-permute-start(f32[2,128,512]{2,1,0:T(8,128)S(1)} %pad_maximum_fusion.1.w0), channel_id=1, source_target_pairs={{0,96},{16,112},{32,64},{48,80},{64,32},{80,48},{96,0},{112,16},{1... | collective-permute-start | bytes 1572872 | tf_op jit(solution)/shard_map/ppermute | solution.py:421
  121.8 29.0 %collective-permute-start.22 = (f32[2,128,512]{2,1,0:T(8,128)S(1)}, f32[2,128,512]{2,1,0:T(8,128)S(1)}, u32[]{:S(2)}, u32[]{:S(2)}) collective-permute-start(f32[2,128,512]{2,1,0:T(8,128)S(1)} %pad_maximum_fusion.1.w0), channel_id=1, source_target_pairs={{0,64},{16,80},{32,96},{48,112},{64,0},{80,16},{96,32},{112,48},{1... | collective-permute-start | bytes 1572872 | tf_op jit(solution)/shard_map/ppermute | solution.py:421
  121.9 28.9 %collective-permute-start.21 = (f32[2,128,512]{2,1,0:T(8,128)S(1)}, f32[2,128,512]{2,1,0:T(8,128)S(1)}, u32[]{:S(2)}, u32[]{:S(2)}) collective-permute-start(f32[2,128,512]{2,1,0:T(8,128)S(1)} %pad_maximum_fusion.1.w0), channel_id=1, source_target_pairs={{0,32},{16,48},{32,0},{48,16},{64,96},{80,112},{96,64},{112,80},{1... | collective-permute-start | bytes 1572872 | tf_op jit(solution)/shard_map/ppermute | solution.py:421
  (11 other events, 137.2 us)
Sparse Core Ops, SparseCore 0:
  66.9 71.9 all-gather.1

commit v3 on v2

--- a/solution.py
+++ b/solution.py
@@ -18,6 +18,7 @@
 NB = PB // B
 Q = 256
 HF = 512
+EA = 576
 MB = 1 << 20
 
 NATURAL = (((1,), (0,)), ((), ()))
@@ -123,61 +124,65 @@
 
 
 def chain(w_ref):
-    def rows(r):
-        x = jnp.broadcast_to(w_ref[r:r + 1, :], (8, 2 * B))
-        return x[:, :B], x[:, B:]
-
-    for q in range(4):
-        done = []
-        for t in range(4):
-            m = 4 * q + t
-            p, a = [], []
-            for i in range(8):
-                x, y = rows(8 * m + i)
-                p.append(x)
-                a.append(y)
-
-            def apply(u):
-                b = [[lane(u[j][0], 8 * m + i) for j in range(8)] for i in range(8)]
-                for i in range(8):
-                    for j in range(8):
-                        p[i] = p[i] - b[i][j] * u[j][0]
-                        a[i] = a[i] - b[i][j] * u[j][1]
-                return b
-
-            for u in done[:-1]:
-                apply(u)
-            d = {(i, j): lane(p[i], 8 * m + j) for i in range(8) for j in range(i + 1)}
-            if done:
-                b = apply(done[-1])
-                for i in range(8):
-                    for j in range(i + 1):
-                        for k in range(8):
-                            d[i, j] = d[i, j] - b[i][k] * b[j][k]
-            u = []
-            for j in range(8):
-                r = lax.rsqrt(d[j, j])
-                low = {i: d[i, j] * r for i in range(j + 1, 8)}
+    sub = lax.broadcasted_iota(jnp.int32, (8, B), 0)
+    for m in range(B // 8):
+        here = slice(8 * m, 8 * m + 8)
+        p, a = [], []
+        for i in range(8):
+            x = jnp.broadcast_to(w_ref[8 * m + i:8 * m + i + 1, :], (8, 2 * B))
+            p.append(x[:, :B])
+            a.append(x[:, B:])
+        d = {(i, j): lane(p[i], 8 * m + j) for i in range(8) for j in range(i + 1)}
+        near = m + 1 < B // 8
+        if near:
+            at = slice(8 * m + 8, 8 * m + 16)
+            np_, na = w_ref[at, :B], w_ref[at, B:]
+            c = [lane(np_, 8 * m + j) for j in range(8)]
+        u, v, r, low = [], [], [], {}
+        for j in range(8):
+            r.append(lax.rsqrt(d[j, j]))
+            for i in range(j + 1, 8):
+                low[i, j] = d[i, j] * r[j]
+            for i in range(j + 1, 8):
+                for k in range(j + 1, i + 1):
+                    d[i, k] = d[i, k] - low[i, j] * low[k, j]
+            u.append(p[j] * r[j])
+            v.append(a[j] * r[j])
+            for i in range(j + 1, 8):
+                p[i] = p[i] - low[i, j] * u[j]
+                a[i] = a[i] - low[i, j] * v[j]
+            if near:
+                cj = c[j] * r[j]
                 for i in range(j + 1, 8):
-                    for k in range(j + 1, i + 1):
-                        d[i, k] = d[i, k] - low[i] * low[k]
-                uj, vj = p[j] * r, a[j] * r
-                u.append((uj, vj))
-                for i in range(j + 1, 8):
-                    p[i] = p[i] - low[i] * uj
-                    a[i] = a[i] - low[i] * vj
-            sub = lax.broadcasted_iota(jnp.int32, (8, B), 0)
-            cu, cv = u[0]
-            for j in range(1, 8):
-                cu = jnp.where(sub == j, u[j][0], cu)
-                cv = jnp.where(sub == j, u[j][1], cv)
-            w_ref[8 * m:8 * m + 8, :B] = cu
-            w_ref[8 * m:8 * m + 8, B:] = cv
-            done.append(u)
-        if q < 3:
-            um = w_ref[32 * q:32 * q + 32, :]
-            ut = um[:, :B].T[32 * (q + 1):, :]
-            w_ref[32 * (q + 1):, :] = w_ref[32 * (q + 1):, :] - dot3(split(ut), split(um))
+                    c[i] = c[i] - low[i, j] * cj
+                np_ = np_ - cj * u[j]
+                na = na - cj * v[j]
+        if near:
+            w_ref[at, :B] = np_
+            w_ref[at, B:] = na
+        cu, cv = u[0], v[0]
+        for j in range(1, 8):
+            cu = jnp.where(sub == j, u[j], cu)
+            cv = jnp.where(sub == j, v[j], cv)
+        w_ref[here, :B] = cu
+        w_ref[here, B:] = cv
+        if m + 2 < B // 8:
+            for n in range(m + 2, B // 8):
+                at = slice(8 * n, 8 * n + 8)
+                x, y = w_ref[at, :B], w_ref[at, B:]
+                c = [lane(x, 8 * m + j) for j in range(8)]
+                g, h = u, v
+                for j in range(8):
+                    c[j] = c[j] * r[j]
+                    for i in range(j + 1, 8):
+                        c[i] = c[i] - low[i, j] * c[j]
+                sx = [c[j] * g[j] for j in range(8)]
+                sy = [c[j] * h[j] for j in range(8)]
+                while len(sx) > 1:
+                    sx = [sx[k] + sx[k + 1] for k in range(0, len(sx), 2)]
+                    sy = [sy[k] + sy[k + 1] for k in range(0, len(sy), 2)]
+                w_ref[at, :B] = x - sx[0]
+                w_ref[at, B:] = y - sy[0]
 
 
 def factor_blocks(rows, width, s_ref, w_ref, v_ref, uh, ul, lh, ll, ih, il):
@@ -303,18 +308,19 @@
     col = at_ref[1]
     copy = pltpu.make_async_copy
     lo, hi = pl.ds(0, HF), pl.ds(HF, HF)
-    loads = [
+    factors = [
         copy(ih1, ih.at[pl.ds(0, 2)], sem.at[0]), copy(il1, il.at[pl.ds(0, 2)], sem.at[1]),
         copy(lh1, lh.at[:, lo], sem.at[2]), copy(ll1, ll.at[:, lo], sem.at[3]),
         copy(ih2, ih.at[pl.ds(2, 2)], sem.at[4]), copy(il2, il.at[pl.ds(2, 2)], sem.at[5]),
         copy(lh2, lh.at[hi, hi], sem.at[6]), copy(ll2, ll.at[hi, hi], sem.at[7]),
     ]
+    window = []
     for k in range(8):
         here = pl.ds(pl.multiple_of(jnp.bitwise_xor(row, k) * B, B), B)
-        loads.append(copy((w0, w1, w2, w3)[k // 2].at[k % 2], a_ref.at[here], sem.at[8 + k]))
+        window.append(copy((w0, w1, w2, w3)[k // 2].at[k % 2], a_ref.at[here], sem.at[8 + k]))
     late = [
-        copy(child_a, c_ref.at[pl.ds(0, CR // 2)], sem.at[16]),
-        copy(child_b, c_ref.at[pl.ds(CR // 2, CR // 2)], sem.at[17]),
+        copy(child_a, c_ref.at[pl.ds(0, EA)], sem.at[16]),
+        copy(child_b, c_ref.at[pl.ds(EA, CR - EA)], sem.at[17]),
         copy(got.at[pl.ds(PC, 8)], g_ref, sem.at[18]),
     ]
 
@@ -330,7 +336,7 @@
     def out_copy(n):
         return copy(out_ref.at[n], out_out.at[pl.ds(n * 512, 512)], out_sem.at[3 + n])
 
-    for d in loads:
+    for d in factors[:2] + window + factors[2:]:
         d.start()
     panel_copy(0).start()
     for d in late:
@@ -339,18 +345,18 @@
         if n:
             panel_copy(n).start()
         trail_copy(n).start()
-    for d in loads:
-        d.wait()
-
-    def solve(src, yh, yl):
+
+    def solve(src, yh, yl, needs=((),) * 4):
         for k in range(PB // Q):
+            for d in needs[k]:
+                d.wait()
             here = slice(k * Q, (k + 1) * Q)
             v = src[here, :]
             if k:
                 v = v - dot3((lh[here, :k * Q], ll[here, :k * Q]), (yh[:k * Q, :], yl[:k * Q, :]))
             yh[here, :], yl[here, :] = split(dot3((ih[k], il[k]), split(v)))
 
-    solve(a_ref, wh, wl)
+    solve(a_ref, wh, wl, (factors[:2] + window, factors[2:4], factors[4:6], factors[6:]))
     for d in late:
         d.wait()
     ch[...], cl[...] = split(c_ref[...])
@@ -449,25 +455,22 @@
     for k, part in ((1, hi), (2, lo), (3, hi)):
         half = half + lax.ppermute(part, "row", [(0, k), (4, 4 + k)])
     x4 = jnp.stack([half] + [flip(half, "col", b, 16) for b in (1, 2, 3)])
-    x4, got, count, child_a = lax.optimization_barrier((x4, got, count, child_trail[1, :CR // 2]))
+    x4, got, count, child_a = lax.optimization_barrier((x4, got, count, child_trail[1, :EA]))
     child_a = flip(child_a, "row", 4, 8)
     mine = [x4] + [flip(x4, "col", b, 16) for b in (4, 8, 12)]
-    other = [flip(x4, "row", 1, 8)]
     panel_t = own + got[:PC]
-    trail = trail_own(count, child_map, front_trail, child_trail)
-    *mine, panel_t, trail, child_a, child_b = lax.optimization_barrier(
-        (*mine, panel_t, trail, child_a, child_trail[1, CR // 2:])
-    )
-    other += [flip(piece, "row", 1, 8) for piece in mine[1:]]
-    panel_full = lax.all_gather(panel_t, "col", axis=0, tiled=True)
-    child_b = flip(child_b, "row", 4, 8)
-
     odd = jnp.bitwise_and(col, 1)
     panes = [panel_t[:, 512 * w:512 * (w + 1)] for w in range(3)]
-    steps = [
-        lax.ppermute(jnp.where(odd == 0, panes[k], panes[(k + 2) % 3]), ("row", "col"), window_pairs(k))
-        for k in range(3)
-    ]
+    picks = [jnp.where(odd == 0, panes[k], panes[(k + 2) % 3]) for k in range(3)]
+    trail = trail_own(count, child_map, front_trail, child_trail)
+    *mine, panel_t, trail, child_a, child_b, p0, p1, p2 = lax.optimization_barrier(
+        (*mine, panel_t, trail, child_a, child_trail[1, EA:], *picks)
+    )
+    panel_full = lax.all_gather(panel_t, "col", axis=0, tiled=True)
+    other = [flip(piece, "row", 1, 8) for piece in mine]
+    steps = [lax.ppermute(p, ("row", "col"), window_pairs(k)) for k, p in enumerate((p0, p1, p2))]
+    child_b = flip(child_b, "row", 4, 8)
+
     *head, nxt = chol_head(at, mine + other)
     *steps, nxt, child_b = lax.optimization_barrier((*steps, nxt, child_b))
     at_w = (col + 2) % 3

time: 185 us -> 176 us (0.951)
  the two profiles are of different devices: /device:TPU:9 before, /device:TPU:36 now
where the time goes in v3:
time: 176 us
  Pallas kernels  74.6 us (42%)
  starting transfers between devices  42.2 us (24%)
  waiting for transfers between devices  39.1 us (22%)
  between operations  14.4 us (8%)
  local copies, waits for them, and re-layouts  3.44 us (2%)
  other arithmetic  1.91 us (1%)
    pallas_call x2, Pallas kernels, chol_call(): pl.pallas_call(kernel, name=name, out_shape=(part, part, inv, inv) + extr...  38.1 us
    ppermute x17, waiting for transfers between devices, flip(): return lax.ppermute(x, axis, [(i, i ^ bit) for i in range(size)])  29.8 us
    ppermute x17, starting transfers between devices, flip(): return lax.ppermute(x, axis, [(i, i ^ bit) for i in range(size)])  29 us
    pallas_call x1, Pallas kernels, finish(): pl.pallas_call(finish_kernel, name='finish', out_shape=(jax.ShapeDtypeStr...  24.8 us
    ppermute x3, starting transfers between devices, on_device(): lax.ppermute(p, ('row', 'col'), window_pairs(k))  9.92 us
    ppermute x3, waiting for transfers between devices, on_device(): half = half + lax.ppermute(part, 'row', [(0, k), (4, 4 + k)])  9.3 us
    pallas_call x1, Pallas kernels, trail_own(): pl.pallas_call(trail_kernel, name='trail_own', grid=(FR // 512,), out_sha...  7.36 us
    pallas_call x1, Pallas kernels, panel_parts(): pl.pallas_call(panel_kernel, name='panel_parts', out_shape=(jax.ShapeDtyp...  4.37 us
  transfers between devices with their start and end apart: 25, of which 9 were waited for; matrix products, arithmetic and copies ran while one was open for 2% of the time, Pallas kernels for 26%

profile of v3, /device:TPU:36, one launch (start us, length us, event | category | flops | bytes accessed | tf_op | source)
XLA Modules:
  0.0 175.7 jit_solution(10571378134072967044)
XLA Ops:
  7.9 4.4 %panel_parts.1 = (f32[64,1536]{1,0:T(8,128)}, f32[72,1536]{1,0:T(8,128)}, f32[64,1024]{1,0:T(8,128)}) custom-call(s32[2]{0:T(128)} %pad_add_fusion.at_ref, s32[1,2]{1,0:T(1,128)} %bitcast.24, s32[2,1024]{1,0:T(2,128)} %map_ref.3, f32[64,1536]{1,0:T(8,128)} %bitcast.19, f32[2,64,1024]{2,1,0:T(8,128)} %bitcast.17), custom_call_target="tpu_custom_call" | custom-call | tf_op jit(solution)/shard_map/panel_parts/pallas_call | solution.py:80
  13.9 1.3 collective-permute-start.2
  16.6 3.1 %collective-permute-start.7 = (f32[72,1536]{1,0:T(8,128)}, f32[72,1536]{1,0:T(8,128)S(1)}, u32[]{:S(2)}, u32[]{:S(2)}) collective-permute-start(f32[72,1536]{1,0:T(8,128)} %get-tuple-element.41), channel_id=1, source_target_pairs={{0,64},{16,80},{32,96},{48,112},{64,0},{80,16},{96,32},{112,48},{1... | collective-permute-start | bytes 1327112 | tf_op jit(solution)/shard_map/ppermute | solution.py:427
  19.7 9.3 %collective-permute-done.2 = f32[64,512]{1,0:T(8,128)S(1)} collective-permute-done((f32[64,512]{1,0:T(8,128)S(1)}, f32[64,512]{1,0:T(8,128)S(1)}, u32[]{:S(2)}, u32[]{:S(2)}) %collective-permute-start.2) | collective-permute-done | bytes 131104 | tf_op jit(solution)/shard_map/ppermute | solution.py:456
  29.6 2.7 %collective-permute-start.5 = (f32[64,512]{1,0:T(8,128)S(1)}, f32[64,512]{1,0:T(8,128)S(1)}, u32[]{:S(2)}, u32[]{:S(2)}) collective-permute-start(f32[64,512]{1,0:T(8,128)S(1)} %add_add_fusion), channel_id=1, source_target_pairs={{0,2},{1,3},{2,0},{3,1},{4,6},{5,7},{6,4},{7,5},{8,10},{9,11},{10,... | collective-permute-start | bytes 393224 | tf_op jit(solution)/shard_map/ppermute | solution.py:427
  33.2 1.4 slice_bitcast_fusion
  34.5 3.3 %collective-permute-done.6 = f32[64,512]{1,0:T(8,128)S(1)} collective-permute-done((f32[64,512]{1,0:T(8,128)S(1)}, f32[64,512]{1,0:T(8,128)S(1)}, u32[]{:S(2)}, u32[]{:S(2)}) %collective-permute-start.6) | collective-permute-done | bytes 131104 | tf_op jit(solution)/shard_map/ppermute | solution.py:427
  37.8 2.3 %collective-permute-done.4 = f32[64,512]{1,0:T(8,128)S(1)} collective-permute-done((f32[64,512]{1,0:T(8,128)S(1)}, f32[64,512]{1,0:T(8,128)S(1)}, u32[]{:S(2)}, u32[]{:S(2)}) %collective-permute-start.4) | collective-permute-done | bytes 131104 | tf_op jit(solution)/shard_map/ppermute | solution.py:427
  40.2 3.5 %collective-permute-start.11 = (f32[576,512]{1,0:T(8,128)S(1)}, f32[576,512]{1,0:T(8,128)}, u32[]{:S(2)}, u32[]{:S(2)}) collective-permute-start(f32[576,512]{1,0:T(8,128)S(1)} %slice_bitcast_fusion), channel_id=1, source_target_pairs={{0,64},{16,80},{32,96},{48,112},{64,0},{80,16},{96,32},{112,48},{1... | collective-permute-start | bytes 3538952 | tf_op jit(solution)/shard_map/ppermute | solution.py:427
  44.9 3.1 %collective-permute-start.10 = (f32[4,64,512]{2,1,0:T(8,128)S(1)}, f32[4,64,512]{2,1,0:T(8,128)}, u32[]{:S(2)}, u32[]{:S(2)}) collective-permute-start(f32[4,64,512]{2,1,0:T(8,128)S(1)} %pad_maximum_fusion.refs_0_), channel_id=1, source_target_pairs={{0,12},{1,13},{2,14},{3,15},{4,8},{5,9},{6,10},{7,11},{8,4},{9,5},... | collective-permute-start | bytes 1572872 | tf_op jit(solution)/shard_map/ppermute | solution.py:427
  49.1 7.4 %trail_own.1.trail = f32[1536,512]{1,0:T(8,128)} custom-call(s32[1,2]{1,0:T(1,128)} %bitcast.25, s32[2,1024]{1,0:T(2,128)} %map_ref.3, f32[1536,512]{1,0:T(8,128)} %front_ref.1, f32[2,1024,512]{2,1,0:T(8,128)} %child_ref.1), custom_call_target="tpu_custom_call" | custom-call | tf_op jit(solution)/shard_map/trail_own/pallas_call | solution.py:105
  56.6 14.7 %collective-permute-done.10.refs_3_ = f32[4,64,512]{2,1,0:T(8,128)} collective-permute-done((f32[4,64,512]{2,1,0:T(8,128)S(1)}, f32[4,64,512]{2,1,0:T(8,128)}, u32[]{:S(2)}, u32[]{:S(2)}) %collective-permute-start.10) | collective-permute-done | bytes 524320 | tf_op jit(solution)/shard_map/ppermute | solution.py:427
  73.1 1.7 collective-permute-start.12
  74.8 6.3 %collective-permute-start.13 = (f32[64,512]{1,0:T(8,128)S(1)}, f32[64,512]{1,0:T(8,128)S(1)}, u32[]{:S(2)}, u32[]{:S(2)}) collective-permute-start(f32[64,512]{1,0:T(8,128)S(1)} %get-tuple-element.48), channel_id=1, source_target_pairs={{17,1},{19,17},{21,33},{23,49},{25,65},{27,81},{29,97},{31,113},{1... | collective-permute-start | bytes 393224 | tf_op jit(solution)/shard_map/ppermute | solution.py:471
  81.2 1.9 %collective-permute-start.14 = (f32[64,512]{1,0:T(8,128)S(1)}, f32[64,512]{1,0:T(8,128)S(1)}, u32[]{:S(2)}, u32[]{:S(2)}) collective-permute-start(f32[64,512]{1,0:T(8,128)S(1)} %get-tuple-element.49), channel_id=1, source_target_pairs={{0,0},{2,16},{4,32},{6,48},{8,64},{10,80},{12,96},{14,112},{17,2},... | collective-permute-start | bytes 393224 | tf_op jit(solution)/shard_map/ppermute | solution.py:471
  83.2 20.9 %chol_head.1 = (bf16[1024,512]{1,0:T(8,128)(2,1)}, bf16[1024,512]{1,0:T(8,128)(2,1)}, bf16[2,256,256]{2,1,0:T(8,128)(2,1)}, bf16[2,256,256]{2,1,0:T(8,128)(2,1)}, f32[512,512]{1,0:T(8,128)}) custom-call(s32[2]{0:T(128)} %pad_add_fusion.at_ref, f32[4,64,512]{2,1,0:T(8,128)} %copy-done.1, f32[4,64,512]{2,1,0:T(8,128)} %collective-permute-done.8.refs_1_, ...), custom_call_target="tpu_custom_call" | custom-call | flops 24999999488 | bytes 8388608 | tf_op jit(solution)/shard_map/chol_head/pallas_call | solution.py:275
  104.2 1.6 collective-permute-done.19.child_b
  105.8 2.1 %collective-permute-start.20 = (f32[128,512]{1,0:T(8,128)S(1)}, f32[128,512]{1,0:T(8,128)S(1)}, u32[]{:S(2)}, u32[]{:S(2)}) collective-permute-start(f32[128,512]{1,0:T(8,128)S(1)} %get-tuple-element.80), channel_id=1, source_target_pairs={{0,16},{16,0},{32,48},{48,32},{64,80},{80,64},{96,112},{112,96},{1... | collective-permute-start | bytes 786440 | tf_op jit(solution)/shard_map/ppermute | solution.py:427
  109.1 8.7 %collective-permute-start.23 = (f32[2,128,512]{2,1,0:T(8,128)S(1)}, f32[2,128,512]{2,1,0:T(8,128)S(1)}, u32[]{:S(2)}, u32[]{:S(2)}) collective-permute-start(f32[2,128,512]{2,1,0:T(8,128)S(1)} %pad_maximum_fusion.1.w0), channel_id=1, source_target_pairs={{0,96},{16,112},{32,64},{48,80},{64,32},{80,48},{96,0},{112,16},{1... | collective-permute-start | bytes 1572872 | tf_op jit(solution)/shard_map/ppermute | solution.py:427
  117.9 2.0 %collective-permute-start.21 = (f32[2,128,512]{2,1,0:T(8,128)S(1)}, f32[2,128,512]{2,1,0:T(8,128)S(1)}, u32[]{:S(2)}, u32[]{:S(2)}) collective-permute-start(f32[2,128,512]{2,1,0:T(8,128)S(1)} %pad_maximum_fusion.1.w0), channel_id=1, source_target_pairs={{0,32},{16,48},{32,0},{48,16},{64,96},{80,112},{96,64},{112,80},{1... | collective-permute-start | bytes 1572872 | tf_op jit(solution)/shard_map/ppermute | solution.py:427
  120.0 17.1 %chol_tail.1 = (bf16[512,512]{1,0:T(8,128)(2,1)}, bf16[512,512]{1,0:T(8,128)(2,1)}, bf16[2,256,256]{2,1,0:T(8,128)(2,1)}, bf16[2,256,256]{2,1,0:T(8,128)(2,1)}) custom-call(f32[512,512]{1,0:T(8,128)} %get-tuple-element.67.s_in), custom_call_target="tpu_custom_call" | custom-call | flops 24999999488 | bytes 8388608 | tf_op jit(solution)/shard_map/chol_tail/pallas_call | solution.py:275
  137.1 4.2 %collective-permute-done.23.w3 = f32[2,128,512]{2,1,0:T(8,128)S(1)} collective-permute-done((f32[2,128,512]{2,1,0:T(8,128)S(1)}, f32[2,128,512]{2,1,0:T(8,128)S(1)}, u32[]{:S(2)}, u32[]{:S(2)}) %collective-permute-start.23) | collective-permute-done | bytes 524320 | tf_op jit(solution)/shard_map/ppermute | solution.py:427
  141.3 1.9 %collective-permute-done.21.w1 = f32[2,128,512]{2,1,0:T(8,128)S(1)} collective-permute-done((f32[2,128,512]{2,1,0:T(8,128)S(1)}, f32[2,128,512]{2,1,0:T(8,128)S(1)}, u32[]{:S(2)}, u32[]{:S(2)}) %collective-permute-start.21) | collective-permute-done | bytes 524320 | tf_op jit(solution)/shard_map/ppermute | solution.py:427
  144.0 24.8 %finish.1 = (f32[64,1536]{1,0:T(8,128)}, f32[1536,512]{1,0:T(8,128)}) custom-call(s32[2]{0:T(128)} %pad_add_fusion.at_ref, f32[2,128,512]{2,1,0:T(8,128)} %copy-done.2, f32[2,128,512]{2,1,0:T(8,128)} %copy-done.10, f32[2,128,512]{2,1,0:T(8,128)} %copy-done.9, f32[2,128,512]{2,1,0:T(8,128)} %copy-done.8, f32[1024,1536]{1,0:T(8,128)} %all-gather.2.cloned.1.call-done.pan, ...), custom_call_target="tpu_custom_call" | custom-call | flops 15000000512 | bytes 26214400 | tf_op jit(solution)/shard_map/finish/pallas_call | solution.py:405
  (66 shorter events, 11.9 us)
Async XLA Ops:
  7.2 136.0 %all-gather.2.cloned.1.call-start = ((), (), s32[]{:S(2)}) async-start(), calls=%async_computation | async-start | bytes 6684672 | tf_op jit(solution)/shard_map/all_gather | solution.py:469
  13.9 15.0 %collective-permute-start.2 = (f32[64,512]{1,0:T(8,128)S(1)}, f32[64,512]{1,0:T(8,128)S(1)}, u32[]{:S(2)}, u32[]{:S(2)}) collective-permute-start(f32[64,512]{1,0:T(8,128)S(1)} %get-tuple-element.81), channel_id=1, source_target_pairs={{0,32},{64,96},{1,33},{65,97},{2,34},{66,98},{3,35},{67,99},{4,36}... | collective-permute-start | bytes 393224 | tf_op jit(solution)/shard_map/ppermute | solution.py:456
  15.2 13.7 %collective-permute-start.3 = (f32[64,512]{1,0:T(8,128)S(1)}, f32[64,512]{1,0:T(8,128)S(1)}, u32[]{:S(2)}, u32[]{:S(2)}) collective-permute-start(f32[64,512]{1,0:T(8,128)S(1)} %get-tuple-element.82), channel_id=1, source_target_pairs={{0,48},{64,112},{1,49},{65,113},{2,50},{66,114},{3,51},{67,115},{4... | collective-permute-start | bytes 393224 | tf_op jit(solution)/shard_map/ppermute | solution.py:456
  15.9 13.0 %collective-permute-start.1 = (f32[64,512]{1,0:T(8,128)S(1)}, f32[64,512]{1,0:T(8,128)S(1)}, u32[]{:S(2)}, u32[]{:S(2)}) collective-permute-start(f32[64,512]{1,0:T(8,128)S(1)} %get-tuple-element.82), channel_id=1, source_target_pairs={{0,16},{64,80},{1,17},{65,81},{2,18},{66,82},{3,19},{67,83},{4,20}... | collective-permute-start | bytes 393224 | tf_op jit(solution)/shard_map/ppermute | solution.py:456
  16.6 23.6 %collective-permute-start.7 = (f32[72,1536]{1,0:T(8,128)}, f32[72,1536]{1,0:T(8,128)S(1)}, u32[]{:S(2)}, u32[]{:S(2)}) collective-permute-start(f32[72,1536]{1,0:T(8,128)} %get-tuple-element.41), channel_id=1, source_target_pairs={{0,64},{16,80},{32,96},{48,112},{64,0},{80,16},{96,32},{112,48},{1... | collective-permute-start | bytes 1327112 | tf_op jit(solution)/shard_map/ppermute | solution.py:427
  29.0 8.8 %collective-permute-start.6 = (f32[64,512]{1,0:T(8,128)S(1)}, f32[64,512]{1,0:T(8,128)S(1)}, u32[]{:S(2)}, u32[]{:S(2)}) collective-permute-start(f32[64,512]{1,0:T(8,128)S(1)} %add_add_fusion), channel_id=1, source_target_pairs={{0,3},{1,2},{2,1},{3,0},{4,7},{5,6},{6,5},{7,4},{8,11},{9,10},{10,... | collective-permute-start | bytes 393224 | tf_op jit(solution)/shard_map/ppermute | solution.py:427
  29.6 8.2 %collective-permute-start.5 = (f32[64,512]{1,0:T(8,128)S(1)}, f32[64,512]{1,0:T(8,128)S(1)}, u32[]{:S(2)}, u32[]{:S(2)}) collective-permute-start(f32[64,512]{1,0:T(8,128)S(1)} %add_add_fusion), channel_id=1, source_target_pairs={{0,2},{1,3},{2,0},{3,1},{4,6},{5,7},{6,4},{7,5},{8,10},{9,11},{10,... | collective-permute-start | bytes 393224 | tf_op jit(solution)/shard_map/ppermute | solution.py:427
  32.3 7.8 %collective-permute-start.4 = (f32[64,512]{1,0:T(8,128)S(1)}, f32[64,512]{1,0:T(8,128)S(1)}, u32[]{:S(2)}, u32[]{:S(2)}) collective-permute-start(f32[64,512]{1,0:T(8,128)S(1)} %add_add_fusion), channel_id=1, source_target_pairs={{0,1},{1,0},{2,3},{3,2},{4,5},{5,4},{6,7},{7,6},{8,9},{9,8},{10,11... | collective-permute-start | bytes 393224 | tf_op jit(solution)/shard_map/ppermute | solution.py:427
  40.2 31.8 %collective-permute-start.11 = (f32[576,512]{1,0:T(8,128)S(1)}, f32[576,512]{1,0:T(8,128)}, u32[]{:S(2)}, u32[]{:S(2)}) collective-permute-start(f32[576,512]{1,0:T(8,128)S(1)} %slice_bitcast_fusion), channel_id=1, source_target_pairs={{0,64},{16,80},{32,96},{48,112},{64,0},{80,16},{96,32},{112,48},{1... | collective-permute-start | bytes 3538952 | tf_op jit(solution)/shard_map/ppermute | solution.py:427
  44.9 26.3 %collective-permute-start.10 = (f32[4,64,512]{2,1,0:T(8,128)S(1)}, f32[4,64,512]{2,1,0:T(8,128)}, u32[]{:S(2)}, u32[]{:S(2)}) collective-permute-start(f32[4,64,512]{2,1,0:T(8,128)S(1)} %pad_maximum_fusion.refs_0_), channel_id=1, source_target_pairs={{0,12},{1,13},{2,14},{3,15},{4,8},{5,9},{6,10},{7,11},{8,4},{9,5},... | collective-permute-start | bytes 1572872 | tf_op jit(solution)/shard_map/ppermute | solution.py:427
  48.0 23.3 %collective-permute-start.9 = (f32[4,64,512]{2,1,0:T(8,128)S(1)}, f32[4,64,512]{2,1,0:T(8,128)}, u32[]{:S(2)}, u32[]{:S(2)}) collective-permute-start(f32[4,64,512]{2,1,0:T(8,128)S(1)} %pad_maximum_fusion.refs_0_), channel_id=1, source_target_pairs={{0,8},{1,9},{2,10},{3,11},{4,12},{5,13},{6,14},{7,15},{8,0},{9,1},... | collective-permute-start | bytes 1572872 | tf_op jit(solution)/shard_map/ppermute | solution.py:427
  48.6 23.3 %collective-permute-start.8 = (f32[4,64,512]{2,1,0:T(8,128)S(1)}, f32[4,64,512]{2,1,0:T(8,128)}, u32[]{:S(2)}, u32[]{:S(2)}) collective-permute-start(f32[4,64,512]{2,1,0:T(8,128)S(1)} %pad_maximum_fusion.refs_0_), channel_id=1, source_target_pairs={{0,4},{1,5},{2,6},{3,7},{4,0},{5,1},{6,2},{7,3},{8,12},{9,13},{10,... | collective-permute-start | bytes 1572872 | tf_op jit(solution)/shard_map/ppermute | solution.py:427
  72.0 2.8 %collective-permute-start.15 = (f32[4,64,512]{2,1,0:T(8,128)S(1)}, f32[4,64,512]{2,1,0:T(8,128)S(1)}, u32[]{:S(2)}, u32[]{:S(2)}) collective-permute-start(f32[4,64,512]{2,1,0:T(8,128)S(1)} %pad_maximum_fusion.refs_0_), channel_id=1, source_target_pairs={{0,16},{16,0},{32,48},{48,32},{64,80},{80,64},{96,112},{112,96},{1... | collective-permute-start | bytes 1572872 | tf_op jit(solution)/shard_map/ppermute | solution.py:427
  72.1 9.0 %collective-permute-start.16 = (f32[4,64,512]{2,1,0:T(8,128)}, f32[4,64,512]{2,1,0:T(8,128)S(1)}, u32[]{:S(2)}, u32[]{:S(2)}) collective-permute-start(f32[4,64,512]{2,1,0:T(8,128)} %collective-permute-done.8.refs_1_), channel_id=1, source_target_pairs={{0,16},{16,0},{32,48},{48,32},{64,80},{80,64},{96,112},{112,96},{1... | collective-permute-start | bytes 1572872 | tf_op jit(solution)/shard_map/ppermute | solution.py:427
  72.6 10.5 %collective-permute-start.17 = (f32[4,64,512]{2,1,0:T(8,128)}, f32[4,64,512]{2,1,0:T(8,128)}, u32[]{:S(2)}, u32[]{:S(2)}) collective-permute-start(f32[4,64,512]{2,1,0:T(8,128)} %collective-permute-done.9.refs_2_), channel_id=1, source_target_pairs={{0,16},{16,0},{32,48},{48,32},{64,80},{80,64},{96,112},{112,96},{1... | collective-permute-start | bytes 1572872 | tf_op jit(solution)/shard_map/ppermute | solution.py:427
  72.7 10.5 %collective-permute-start.18 = (f32[4,64,512]{2,1,0:T(8,128)}, f32[4,64,512]{2,1,0:T(8,128)}, u32[]{:S(2)}, u32[]{:S(2)}) collective-permute-start(f32[4,64,512]{2,1,0:T(8,128)} %collective-permute-done.10.refs_3_), channel_id=1, source_target_pairs={{0,16},{16,0},{32,48},{48,32},{64,80},{80,64},{96,112},{112,96},{1... | collective-permute-start | bytes 1572872 | tf_op jit(solution)/shard_map/ppermute | solution.py:427
  73.1 31.1 %collective-permute-start.12 = (f32[64,512]{1,0:T(8,128)S(1)}, f32[64,512]{1,0:T(8,128)S(1)}, u32[]{:S(2)}, u32[]{:S(2)}) collective-permute-start(f32[64,512]{1,0:T(8,128)S(1)} %get-tuple-element.47), channel_id=1, source_target_pairs={{1,0},{3,16},{5,32},{7,48},{9,64},{11,80},{13,96},{15,112},{16,1},... | collective-permute-start | bytes 393224 | tf_op jit(solution)/shard_map/ppermute | solution.py:471
  74.8 29.4 %collective-permute-start.13 = (f32[64,512]{1,0:T(8,128)S(1)}, f32[64,512]{1,0:T(8,128)S(1)}, u32[]{:S(2)}, u32[]{:S(2)}) collective-permute-start(f32[64,512]{1,0:T(8,128)S(1)} %get-tuple-element.48), channel_id=1, source_target_pairs={{17,1},{19,17},{21,33},{23,49},{25,65},{27,81},{29,97},{31,113},{1... | collective-permute-start | bytes 393224 | tf_op jit(solution)/shard_map/ppermute | solution.py:471
  81.2 23.0 %collective-permute-start.14 = (f32[64,512]{1,0:T(8,128)S(1)}, f32[64,512]{1,0:T(8,128)S(1)}, u32[]{:S(2)}, u32[]{:S(2)}) collective-permute-start(f32[64,512]{1,0:T(8,128)S(1)} %get-tuple-element.49), channel_id=1, source_target_pairs={{0,0},{2,16},{4,32},{6,48},{8,64},{10,80},{12,96},{14,112},{17,2},... | collective-permute-start | bytes 393224 | tf_op jit(solution)/shard_map/ppermute | solution.py:471
  83.1 22.6 %collective-permute-start.19 = (f32[448,512]{1,0:T(8,128)S(1)}, f32[448,512]{1,0:T(8,128)S(1)}, u32[]{:S(2)}, u32[]{:S(2)}) collective-permute-start(f32[448,512]{1,0:T(8,128)S(1)} %slice_bitcast_fusion.1), channel_id=1, source_target_pairs={{0,64},{16,80},{32,96},{48,112},{64,0},{80,16},{96,32},{112,48},{1... | collective-permute-start | bytes 2752520 | tf_op jit(solution)/shard_map/ppermute | solution.py:427
  105.8 3.2 %collective-permute-start.20 = (f32[128,512]{1,0:T(8,128)S(1)}, f32[128,512]{1,0:T(8,128)S(1)}, u32[]{:S(2)}, u32[]{:S(2)}) collective-permute-start(f32[128,512]{1,0:T(8,128)S(1)} %get-tuple-element.80), channel_id=1, source_target_pairs={{0,16},{16,0},{32,48},{48,32},{64,80},{80,64},{96,112},{112,96},{1... | collective-permute-start | bytes 786440 | tf_op jit(solution)/shard_map/ppermute | solution.py:427
  109.1 32.1 %collective-permute-start.23 = (f32[2,128,512]{2,1,0:T(8,128)S(1)}, f32[2,128,512]{2,1,0:T(8,128)S(1)}, u32[]{:S(2)}, u32[]{:S(2)}) collective-permute-start(f32[2,128,512]{2,1,0:T(8,128)S(1)} %pad_maximum_fusion.1.w0), channel_id=1, source_target_pairs={{0,96},{16,112},{32,64},{48,80},{64,32},{80,48},{96,0},{112,16},{1... | collective-permute-start | bytes 1572872 | tf_op jit(solution)/shard_map/ppermute | solution.py:427
  117.8 23.5 %collective-permute-start.22 = (f32[2,128,512]{2,1,0:T(8,128)S(1)}, f32[2,128,512]{2,1,0:T(8,128)S(1)}, u32[]{:S(2)}, u32[]{:S(2)}) collective-permute-start(f32[2,128,512]{2,1,0:T(8,128)S(1)} %pad_maximum_fusion.1.w0), channel_id=1, source_target_pairs={{0,64},{16,80},{32,96},{48,112},{64,0},{80,16},{96,32},{112,48},{1... | collective-permute-start | bytes 1572872 | tf_op jit(solution)/shard_map/ppermute | solution.py:427
  117.9 25.2 %collective-permute-start.21 = (f32[2,128,512]{2,1,0:T(8,128)S(1)}, f32[2,128,512]{2,1,0:T(8,128)S(1)}, u32[]{:S(2)}, u32[]{:S(2)}) collective-permute-start(f32[2,128,512]{2,1,0:T(8,128)S(1)} %pad_maximum_fusion.1.w0), channel_id=1, source_target_pairs={{0,32},{16,48},{32,0},{48,16},{64,96},{80,112},{96,64},{112,80},{1... | collective-permute-start | bytes 1572872 | tf_op jit(solution)/shard_map/ppermute | solution.py:427
  (12 other events, 150.2 us)
Sparse Core Ops, SparseCore 0:
  72.1 68.6 all-gather.1

commit v4 on v3

--- a/solution.py
+++ b/solution.py
@@ -18,7 +18,7 @@
 NB = PB // B
 Q = 256
 HF = 512
-EA = 576
+EA = 544
 MB = 1 << 20
 
 NATURAL = (((1,), (0,)), ((), ()))
@@ -117,6 +117,35 @@
         scratch_shapes=[pltpu.VMEM((CR, TC), bf16)] * 2,
         compiler_params=pltpu.CompilerParams(vmem_limit_bytes=58 * MB),
     )(count, child_map, front, child)
+
+
+def trail_got_kernel(got_ref, trail_ref, a_ref, b_ref, out_ref, ch, cl):
+    @pl.when(pl.program_id(0) == 0)
+    def _():
+        ch[:EA, :], cl[:EA, :] = split(a_ref[...])
+        ch[EA:, :], cl[EA:, :] = split(b_ref[...])
+
+    target = got_ref[0:1, :CR].astype(jnp.int32)
+    g = one_hot(pl.program_id(0) * 512, 512, target)
+    out_ref[...] = trail_ref[...] + (dot1(g, ch[...]) + dot1(g, cl[...]))
+
+
+def trail_got(got, trail, child_a, child_b):
+    return pl.pallas_call(
+        trail_got_kernel,
+        name="trail_got",
+        grid=(FR // 512,),
+        out_shape=jax.ShapeDtypeStruct((FR, TC), f32),
+        in_specs=[
+            pl.BlockSpec((8, FR), lambda s: (PC // 8, 0)),
+            pl.BlockSpec((512, TC), lambda s: (s, 0)),
+            pl.BlockSpec((EA, TC), lambda s: (0, 0)),
+            pl.BlockSpec((CR - EA, TC), lambda s: (0, 0)),
+        ],
+        out_specs=pl.BlockSpec((512, TC), lambda s: (s, 0)),
+        scratch_shapes=[pltpu.VMEM((CR, TC), bf16)] * 2,
+        compiler_params=pltpu.CompilerParams(vmem_limit_bytes=58 * MB),
+    )(got, trail, child_a, child_b)
 
 
 def lane(x, at):
@@ -299,10 +328,10 @@
     return chol_call(chol_tail_kernel, "chol_tail", HF, (), [nxt])
 
 
-def finish_kernel(at_ref, w0, w1, w2, w3, pan, got, trail, child_a, child_b,
+def finish_kernel(at_ref, w0, w1, w2, w3, pan, trail,
                   lh1, ll1, ih1, il1, lh2, ll2, ih2, il2,
                   fac_out, out_out,
-                  a_ref, p_ref, t_ref, c_ref, g_ref, lh, ll, ih, il, xh, xl, wh, wl, ch, cl,
+                  a_ref, p_ref, t_ref, lh, ll, ih, il, xh, xl, wh, wl,
                   fac_ref, out_ref, sem, pan_sem, trail_sem, out_sem):
     row = at_ref[0]
     col = at_ref[1]
@@ -318,12 +347,6 @@
     for k in range(8):
         here = pl.ds(pl.multiple_of(jnp.bitwise_xor(row, k) * B, B), B)
         window.append(copy((w0, w1, w2, w3)[k // 2].at[k % 2], a_ref.at[here], sem.at[8 + k]))
-    late = [
-        copy(child_a, c_ref.at[pl.ds(0, EA)], sem.at[16]),
-        copy(child_b, c_ref.at[pl.ds(EA, CR - EA)], sem.at[17]),
-        copy(got.at[pl.ds(PC, 8)], g_ref, sem.at[18]),
-    ]
-
     def panel_copy(n):
         return copy(pan.at[:, pl.ds(n * 512, 512)], p_ref.at[n], pan_sem.at[n])
 
@@ -339,8 +362,6 @@
     for d in factors[:2] + window + factors[2:]:
         d.start()
     panel_copy(0).start()
-    for d in late:
-        d.start()
     for n in range(3):
         if n:
             panel_copy(n).start()
@@ -357,10 +378,6 @@
             yh[here, :], yl[here, :] = split(dot3((ih[k], il[k]), split(v)))
 
     solve(a_ref, wh, wl, (factors[:2] + window, factors[2:4], factors[4:6], factors[6:]))
-    for d in late:
-        d.wait()
-    ch[...], cl[...] = split(c_ref[...])
-    target = g_ref[0:1, :CR].astype(jnp.int32)
     mine = pl.ds(pl.multiple_of(col * PC, PC), PC)
 
     def block(n, _):
@@ -384,11 +401,9 @@
 
         fac_ref[n] = xh[mine, :].astype(f32) + xl[mine, :].astype(f32)
         fac_copy(n).start()
-        g = one_hot(n * 512, 512, target)
-        moved = dot1(g, ch[...]) + dot1(g, cl[...])
         prod = dot3((xh[...], xl[...]), (wh[...], wl[...]), LHS_T)
         trail_copy(n).wait()
-        out_ref[n] = t_ref[n] + (moved - prod)
+        out_ref[n] = t_ref[n] - prod
         out_copy(n).start()
         return 0
 
@@ -398,7 +413,7 @@
         out_copy(n).wait()
 
 
-def finish(at, window, panel, got, trail, child, head, tail):
+def finish(at, window, panel, trail, head, tail):
     hbm = pl.BlockSpec(memory_space=pl.ANY)
     dma = pltpu.SemaphoreType.DMA
     vm = pltpu.VMEM
@@ -406,21 +421,19 @@
         finish_kernel,
         name="finish",
         out_shape=(jax.ShapeDtypeStruct((PC, FR), f32), jax.ShapeDtypeStruct((FR, TC), f32)),
-        in_specs=[pl.BlockSpec(memory_space=pltpu.SMEM)] + [hbm] * 17,
+        in_specs=[pl.BlockSpec(memory_space=pltpu.SMEM)] + [hbm] * 14,
         out_specs=(hbm, hbm),
         scratch_shapes=[
-            vm((PB, TC), f32), vm((3, PB, 512), f32), vm((3, 512, TC), f32), vm((CR, TC), f32),
-            vm((8, FR), f32),
+            vm((PB, TC), f32), vm((3, PB, 512), f32), vm((3, 512, TC), f32),
             vm((PB, PB), bf16), vm((PB, PB), bf16),
             vm((PB // Q, Q, Q), bf16), vm((PB // Q, Q, Q), bf16),
             vm((PB, 512), bf16), vm((PB, 512), bf16), vm((PB, TC), bf16), vm((PB, TC), bf16),
-            vm((CR, TC), bf16), vm((CR, TC), bf16),
             vm((3, PC, 512), f32), vm((3, 512, TC), f32),
-            dma((19,)), dma((3,)), dma((3,)), dma((6,)),
+            dma((16,)), dma((3,)), dma((3,)), dma((6,)),
         ],
         compiler_params=pltpu.CompilerParams(vmem_limit_bytes=58 * MB),
         cost_estimate=pl.CostEstimate(flops=15_000_000_000, transcendentals=0, bytes_accessed=25 * MB),
-    )(at, *window, panel, got, trail, *child, *head, *tail)
+    )(at, *window, panel, trail, *head, *tail)
 
 
 def flip(x, axis, bit, size):
@@ -481,7 +494,8 @@
     window = [pair] + [flip(pair, "row", b, 8) for b in (2, 4, 6)]
     tail = chol_tail(nxt)
 
-    factor_t, schur = finish(at, window, panel_full, got, trail, [child_a, child_b], head, tail)
+    trail = trail_got(got, trail, child_a, child_b)
+    factor_t, schur = finish(at, window, panel_full, trail, head, tail)
     return factor_t.T, schur
 
 

time: 176 us -> 175 us (level)
  the two profiles are of different devices: /device:TPU:36 before, /device:TPU:21 now
where the time goes in v4:
time: 175 us
  Pallas kernels  79.8 us (46%)
  starting transfers between devices  50.9 us (29%)
  waiting for transfers between devices  22.3 us (13%)
  between operations  14.4 us (8%)
  local copies, waits for them, and re-layouts  4.78 us (3%)
  other arithmetic  2.68 us (2%)
    pallas_call x2, Pallas kernels, chol_call(): pl.pallas_call(kernel, name=name, out_shape=(part, part, inv, inv) + extr...  38.1 us
    ppermute x17, starting transfers between devices, flip(): return lax.ppermute(x, axis, [(i, i ^ bit) for i in range(size)])  25 us
    pallas_call x1, Pallas kernels, finish(): pl.pallas_call(finish_kernel, name='finish', out_shape=(jax.ShapeDtypeStr...  22.7 us
    ppermute x3, starting transfers between devices, on_device(): lax.ppermute(p, ('row', 'col'), window_pairs(k))  22.6 us
    ppermute x17, waiting for transfers between devices, flip(): return lax.ppermute(x, axis, [(i, i ^ bit) for i in range(size)])  15.1 us
    pallas_call x1, Pallas kernels, trail_own(): pl.pallas_call(trail_kernel, name='trail_own', grid=(FR // 512,), out_sha...  7.34 us
    pallas_call x1, Pallas kernels, trail_got(): pl.pallas_call(trail_got_kernel, name='trail_got', grid=(FR // 512,), out...  7.25 us
    ppermute x3, waiting for transfers between devices, on_device(): half = half + lax.ppermute(part, 'row', [(0, k), (4, 4 + k)])  7.15 us
  transfers between devices with their start and end apart: 25, of which 6 were waited for; matrix products, arithmetic and copies ran while one was open for 3% of the time, Pallas kernels for 30%

profile of v4, /device:TPU:21, one launch (start us, length us, event | category | flops | bytes accessed | tf_op | source)
XLA Modules:
  0.0 174.8 jit_solution(16257391725639027444)
XLA Ops:
  7.8 4.4 %panel_parts.1 = (f32[64,1536]{1,0:T(8,128)}, f32[72,1536]{1,0:T(8,128)}, f32[64,1024]{1,0:T(8,128)}) custom-call(s32[2]{0:T(128)} %pad_add_fusion.at_ref, s32[1,2]{1,0:T(1,128)} %bitcast.24, s32[2,1024]{1,0:T(2,128)} %map_ref.3, f32[64,1536]{1,0:T(8,128)} %bitcast.19, f32[2,64,1024]{2,1,0:T(8,128)} %bitcast.17), custom_call_target="tpu_custom_call" | custom-call | tf_op jit(solution)/shard_map/panel_parts/pallas_call | solution.py:80
  12.8 1.0 add.28
  13.9 1.3 collective-permute-start.1
  16.5 3.7 %collective-permute-start.7 = (f32[72,1536]{1,0:T(8,128)}, f32[72,1536]{1,0:T(8,128)S(1)}, u32[]{:S(2)}, u32[]{:S(2)}) collective-permute-start(f32[72,1536]{1,0:T(8,128)} %get-tuple-element.41), channel_id=1, source_target_pairs={{0,64},{16,80},{32,96},{48,112},{64,0},{80,16},{96,32},{112,48},{1... | collective-permute-start | bytes 1327112 | tf_op jit(solution)/shard_map/ppermute | solution.py:440
  20.2 7.1 %collective-permute-done.1 = f32[64,512]{1,0:T(8,128)S(1)} collective-permute-done((f32[64,512]{1,0:T(8,128)S(1)}, f32[64,512]{1,0:T(8,128)S(1)}, u32[]{:S(2)}, u32[]{:S(2)}) %collective-permute-start.1) | collective-permute-done | bytes 131104 | tf_op jit(solution)/shard_map/ppermute | solution.py:469
  28.9 1.2 collective-permute-start.6
  30.1 1.3 slice_bitcast_fusion
  31.4 2.3 %collective-permute-done.5 = f32[64,512]{1,0:T(8,128)S(1)} collective-permute-done((f32[64,512]{1,0:T(8,128)S(1)}, f32[64,512]{1,0:T(8,128)S(1)}, u32[]{:S(2)}, u32[]{:S(2)}) %collective-permute-start.5) | collective-permute-done | bytes 131104 | tf_op jit(solution)/shard_map/ppermute | solution.py:440
  35.0 3.8 %collective-permute-start.11 = (f32[544,512]{1,0:T(8,128)S(1)}, f32[544,512]{1,0:T(8,128)S(1)}, u32[]{:S(2)}, u32[]{:S(2)}) collective-permute-start(f32[544,512]{1,0:T(8,128)S(1)} %slice_bitcast_fusion), channel_id=1, source_target_pairs={{0,64},{16,80},{32,96},{48,112},{64,0},{80,16},{96,32},{112,48},{1... | collective-permute-start | bytes 3342344 | tf_op jit(solution)/shard_map/ppermute | solution.py:440
  38.8 2.3 %slice_bitcast_fusion.1 = f32[480,512]{1,0:T(8,128)} fusion(f32[2,1024,512]{2,1,0:T(8,128)} %child_ref.1), kind=kLoop, calls=%fused_computation.1 | loop fusion | bytes 1966080 | tf_op jit(solution)/shard_map/squeeze | solution.py:480
  42.1 1.8 %collective-permute-start.9 = (f32[4,64,512]{2,1,0:T(8,128)}, f32[4,64,512]{2,1,0:T(8,128)}, u32[]{:S(2)}, u32[]{:S(2)}) collective-permute-start(f32[4,64,512]{2,1,0:T(8,128)} %pad_maximum_fusion.refs_0_), channel_id=1, source_target_pairs={{0,8},{1,9},{2,10},{3,11},{4,12},{5,13},{6,14},{7,15},{8,0},{9,1},... | collective-permute-start | bytes 1572872 | tf_op jit(solution)/shard_map/ppermute | solution.py:440
  43.9 7.3 %trail_own.1.trail_ref = f32[1536,512]{1,0:T(8,128)} custom-call(s32[1,2]{1,0:T(1,128)} %bitcast.25, s32[2,1024]{1,0:T(2,128)} %map_ref.3, f32[1536,512]{1,0:T(8,128)} %front_ref.1, f32[2,1024,512]{2,1,0:T(8,128)} %child_ref.1), custom_call_target="tpu_custom_call" | custom-call | tf_op jit(solution)/shard_map/trail_own/pallas_call | solution.py:105
  51.4 9.9 %collective-permute-done.9.refs_2_ = f32[4,64,512]{2,1,0:T(8,128)} collective-permute-done((f32[4,64,512]{2,1,0:T(8,128)}, f32[4,64,512]{2,1,0:T(8,128)}, u32[]{:S(2)}, u32[]{:S(2)}) %collective-permute-start.9) | collective-permute-done | bytes 524320 | tf_op jit(solution)/shard_map/ppermute | solution.py:440
  61.3 7.2 %collective-permute-start.15 = (f32[4,64,512]{2,1,0:T(8,128)}, f32[4,64,512]{2,1,0:T(8,128)S(1)}, u32[]{:S(2)}, u32[]{:S(2)}) collective-permute-start(f32[4,64,512]{2,1,0:T(8,128)} %pad_maximum_fusion.refs_0_), channel_id=1, source_target_pairs={{0,16},{16,0},{32,48},{48,32},{64,80},{80,64},{96,112},{112,96},{1... | collective-permute-start | bytes 1572872 | tf_op jit(solution)/shard_map/ppermute | solution.py:440
  69.3 1.0 collective-permute-done.15.refs_4_
  70.3 5.4 %collective-permute-start.12 = (f32[64,512]{1,0:T(8,128)S(1)}, f32[64,512]{1,0:T(8,128)S(1)}, u32[]{:S(2)}, u32[]{:S(2)}) collective-permute-start(f32[64,512]{1,0:T(8,128)S(1)} %get-tuple-element.47), channel_id=1, source_target_pairs={{1,0},{3,16},{5,32},{7,48},{9,64},{11,80},{13,96},{15,112},{16,1},... | collective-permute-start | bytes 393224 | tf_op jit(solution)/shard_map/ppermute | solution.py:484
  75.7 5.4 %collective-permute-start.13 = (f32[64,512]{1,0:T(8,128)S(1)}, f32[64,512]{1,0:T(8,128)S(1)}, u32[]{:S(2)}, u32[]{:S(2)}) collective-permute-start(f32[64,512]{1,0:T(8,128)S(1)} %get-tuple-element.48), channel_id=1, source_target_pairs={{17,1},{19,17},{21,33},{23,49},{25,65},{27,81},{29,97},{31,113},{1... | collective-permute-start | bytes 393224 | tf_op jit(solution)/shard_map/ppermute | solution.py:484
  81.2 11.7 %collective-permute-start.14 = (f32[64,512]{1,0:T(8,128)S(1)}, f32[64,512]{1,0:T(8,128)S(1)}, u32[]{:S(2)}, u32[]{:S(2)}) collective-permute-start(f32[64,512]{1,0:T(8,128)S(1)} %get-tuple-element.49), channel_id=1, source_target_pairs={{0,0},{2,16},{4,32},{6,48},{8,64},{10,80},{12,96},{14,112},{17,2},... | collective-permute-start | bytes 393224 | tf_op jit(solution)/shard_map/ppermute | solution.py:484
  92.9 20.9 %chol_head.1 = (bf16[1024,512]{1,0:T(8,128)(2,1)}, bf16[1024,512]{1,0:T(8,128)(2,1)}, bf16[2,256,256]{2,1,0:T(8,128)(2,1)}, bf16[2,256,256]{2,1,0:T(8,128)(2,1)}, f32[512,512]{1,0:T(8,128)}) custom-call(s32[2]{0:T(128)} %pad_add_fusion.at_ref, f32[4,64,512]{2,1,0:T(8,128)} %pad_maximum_fusion.refs_0_, f32[4,64,512]{2,1,0:T(8,128)} %collective-permute-done.8.refs_1_, ...), custom_call_target="tpu_custom_call" | custom-call | flops 24999999488 | bytes 8388608 | tf_op jit(solution)/shard_map/chol_head/pallas_call | solution.py:304
  114.1 1.5 collective-permute-done.20
  115.9 3.8 %collective-permute-start.23 = (f32[2,128,512]{2,1,0:T(8,128)S(1)}, f32[2,128,512]{2,1,0:T(8,128)S(1)}, u32[]{:S(2)}, u32[]{:S(2)}) collective-permute-start(f32[2,128,512]{2,1,0:T(8,128)S(1)} %pad_maximum_fusion.1.w0), channel_id=1, source_target_pairs={{0,96},{16,112},{32,64},{48,80},{64,32},{80,48},{96,0},{112,16},{1... | collective-permute-start | bytes 1572872 | tf_op jit(solution)/shard_map/ppermute | solution.py:440
  119.6 17.1 %chol_tail.1 = (bf16[512,512]{1,0:T(8,128)(2,1)}, bf16[512,512]{1,0:T(8,128)(2,1)}, bf16[2,256,256]{2,1,0:T(8,128)(2,1)}, bf16[2,256,256]{2,1,0:T(8,128)(2,1)}) custom-call(f32[512,512]{1,0:T(8,128)} %get-tuple-element.67.s_in), custom_call_target="tpu_custom_call" | custom-call | flops 24999999488 | bytes 8388608 | tf_op jit(solution)/shard_map/chol_tail/pallas_call | solution.py:304
  136.8 7.2 %trail_got.1.trail = f32[1536,512]{1,0:T(8,128)} custom-call(f32[72,1536]{1,0:T(8,128)} %copy-done.1, f32[1536,512]{1,0:T(8,128)} %trail_own.1.trail_ref, f32[544,512]{1,0:T(8,128)} %copy-done.2, f32[480,512]{1,0:T(8,128)} %copy-done.3), custom_call_target="tpu_custom_call" | custom-call | tf_op jit(solution)/shard_map/trail_got/pallas_call | solution.py:134
  145.2 22.7 %finish.1 = (f32[64,1536]{1,0:T(8,128)}, f32[1536,512]{1,0:T(8,128)}) custom-call(s32[2]{0:T(128)} %pad_add_fusion.at_ref, f32[2,128,512]{2,1,0:T(8,128)} %copy-done.4, f32[2,128,512]{2,1,0:T(8,128)} %copy-done.9, f32[2,128,512]{2,1,0:T(8,128)} %copy-done.10, f32[2,128,512]{2,1,0:T(8,128)} %copy-done.11, f32[1024,1536]{1,0:T(8,128)} %all-gather.2.cloned.1.call-done.pan, ...), custom_call_target="tpu_custom_call" | custom-call | flops 15000000512 | bytes 26214400 | tf_op jit(solution)/shard_map/finish/pallas_call | solution.py:420
  (69 shorter events, 8.8 us)
Async XLA Ops:
  7.2 136.9 %all-gather.2.cloned.1.call-start = ((), (), s32[]{:S(2)}) async-start(), calls=%async_computation | async-start | bytes 6684672 | tf_op jit(solution)/shard_map/all_gather | solution.py:482
  13.9 13.5 %collective-permute-start.1 = (f32[64,512]{1,0:T(8,128)S(1)}, f32[64,512]{1,0:T(8,128)S(1)}, u32[]{:S(2)}, u32[]{:S(2)}) collective-permute-start(f32[64,512]{1,0:T(8,128)S(1)} %get-tuple-element.82), channel_id=1, source_target_pairs={{0,16},{64,80},{1,17},{65,81},{2,18},{66,82},{3,19},{67,83},{4,20}... | collective-permute-start | bytes 393224 | tf_op jit(solution)/shard_map/ppermute | solution.py:469
  15.2 12.2 %collective-permute-start.3 = (f32[64,512]{1,0:T(8,128)S(1)}, f32[64,512]{1,0:T(8,128)S(1)}, u32[]{:S(2)}, u32[]{:S(2)}) collective-permute-start(f32[64,512]{1,0:T(8,128)S(1)} %get-tuple-element.82), channel_id=1, source_target_pairs={{0,48},{64,112},{1,49},{65,113},{2,50},{66,114},{3,51},{67,115},{4... | collective-permute-start | bytes 393224 | tf_op jit(solution)/shard_map/ppermute | solution.py:469
  15.8 11.5 %collective-permute-start.2 = (f32[64,512]{1,0:T(8,128)S(1)}, f32[64,512]{1,0:T(8,128)S(1)}, u32[]{:S(2)}, u32[]{:S(2)}) collective-permute-start(f32[64,512]{1,0:T(8,128)S(1)} %get-tuple-element.81), channel_id=1, source_target_pairs={{0,32},{64,96},{1,33},{65,97},{2,34},{66,98},{3,35},{67,99},{4,36}... | collective-permute-start | bytes 393224 | tf_op jit(solution)/shard_map/ppermute | solution.py:469
  16.5 18.5 %collective-permute-start.7 = (f32[72,1536]{1,0:T(8,128)}, f32[72,1536]{1,0:T(8,128)S(1)}, u32[]{:S(2)}, u32[]{:S(2)}) collective-permute-start(f32[72,1536]{1,0:T(8,128)} %get-tuple-element.41), channel_id=1, source_target_pairs={{0,64},{16,80},{32,96},{48,112},{64,0},{80,16},{96,32},{112,48},{1... | collective-permute-start | bytes 1327112 | tf_op jit(solution)/shard_map/ppermute | solution.py:440
  27.4 4.1 %collective-permute-start.4 = (f32[64,512]{1,0:T(8,128)S(1)}, f32[64,512]{1,0:T(8,128)S(1)}, u32[]{:S(2)}, u32[]{:S(2)}) collective-permute-start(f32[64,512]{1,0:T(8,128)S(1)} %add_add_fusion), channel_id=1, source_target_pairs={{0,1},{1,0},{2,3},{3,2},{4,5},{5,4},{6,7},{7,6},{8,9},{9,8},{10,11... | collective-permute-start | bytes 393224 | tf_op jit(solution)/shard_map/ppermute | solution.py:440
  28.4 5.4 %collective-permute-start.5 = (f32[64,512]{1,0:T(8,128)S(1)}, f32[64,512]{1,0:T(8,128)S(1)}, u32[]{:S(2)}, u32[]{:S(2)}) collective-permute-start(f32[64,512]{1,0:T(8,128)S(1)} %add_add_fusion), channel_id=1, source_target_pairs={{0,2},{1,3},{2,0},{3,1},{4,6},{5,7},{6,4},{7,5},{8,10},{9,11},{10,... | collective-permute-start | bytes 393224 | tf_op jit(solution)/shard_map/ppermute | solution.py:440
  28.9 5.2 %collective-permute-start.6 = (f32[64,512]{1,0:T(8,128)S(1)}, f32[64,512]{1,0:T(8,128)S(1)}, u32[]{:S(2)}, u32[]{:S(2)}) collective-permute-start(f32[64,512]{1,0:T(8,128)S(1)} %add_add_fusion), channel_id=1, source_target_pairs={{0,3},{1,2},{2,1},{3,0},{4,7},{5,6},{6,5},{7,4},{8,11},{9,10},{10,... | collective-permute-start | bytes 393224 | tf_op jit(solution)/shard_map/ppermute | solution.py:440
  35.0 26.3 %collective-permute-start.11 = (f32[544,512]{1,0:T(8,128)S(1)}, f32[544,512]{1,0:T(8,128)S(1)}, u32[]{:S(2)}, u32[]{:S(2)}) collective-permute-start(f32[544,512]{1,0:T(8,128)S(1)} %slice_bitcast_fusion), channel_id=1, source_target_pairs={{0,64},{16,80},{32,96},{48,112},{64,0},{80,16},{96,32},{112,48},{1... | collective-permute-start | bytes 3342344 | tf_op jit(solution)/shard_map/ppermute | solution.py:440
  41.1 10.2 %collective-permute-start.10 = (f32[4,64,512]{2,1,0:T(8,128)}, f32[4,64,512]{2,1,0:T(8,128)}, u32[]{:S(2)}, u32[]{:S(2)}) collective-permute-start(f32[4,64,512]{2,1,0:T(8,128)} %pad_maximum_fusion.refs_0_), channel_id=1, source_target_pairs={{0,12},{1,13},{2,14},{3,15},{4,8},{5,9},{6,10},{7,11},{8,4},{9,5},... | collective-permute-start | bytes 1572872 | tf_op jit(solution)/shard_map/ppermute | solution.py:440
  41.3 10.1 %collective-permute-start.8 = (f32[4,64,512]{2,1,0:T(8,128)}, f32[4,64,512]{2,1,0:T(8,128)}, u32[]{:S(2)}, u32[]{:S(2)}) collective-permute-start(f32[4,64,512]{2,1,0:T(8,128)} %pad_maximum_fusion.refs_0_), channel_id=1, source_target_pairs={{0,4},{1,5},{2,6},{3,7},{4,0},{5,1},{6,2},{7,3},{8,12},{9,13},{10,... | collective-permute-start | bytes 1572872 | tf_op jit(solution)/shard_map/ppermute | solution.py:440
  42.1 19.1 %collective-permute-start.9 = (f32[4,64,512]{2,1,0:T(8,128)}, f32[4,64,512]{2,1,0:T(8,128)}, u32[]{:S(2)}, u32[]{:S(2)}) collective-permute-start(f32[4,64,512]{2,1,0:T(8,128)} %pad_maximum_fusion.refs_0_), channel_id=1, source_target_pairs={{0,8},{1,9},{2,10},{3,11},{4,12},{5,13},{6,14},{7,15},{8,0},{9,1},... | collective-permute-start | bytes 1572872 | tf_op jit(solution)/shard_map/ppermute | solution.py:440
  61.3 9.0 %collective-permute-start.15 = (f32[4,64,512]{2,1,0:T(8,128)}, f32[4,64,512]{2,1,0:T(8,128)S(1)}, u32[]{:S(2)}, u32[]{:S(2)}) collective-permute-start(f32[4,64,512]{2,1,0:T(8,128)} %pad_maximum_fusion.refs_0_), channel_id=1, source_target_pairs={{0,16},{16,0},{32,48},{48,32},{64,80},{80,64},{96,112},{112,96},{1... | collective-permute-start | bytes 1572872 | tf_op jit(solution)/shard_map/ppermute | solution.py:440
  68.5 7.2 %collective-permute-start.16 = (f32[4,64,512]{2,1,0:T(8,128)}, f32[4,64,512]{2,1,0:T(8,128)S(1)}, u32[]{:S(2)}, u32[]{:S(2)}) collective-permute-start(f32[4,64,512]{2,1,0:T(8,128)} %collective-permute-done.8.refs_1_), channel_id=1, source_target_pairs={{0,16},{16,0},{32,48},{48,32},{64,80},{80,64},{96,112},{112,96},{1... | collective-permute-start | bytes 1572872 | tf_op jit(solution)/shard_map/ppermute | solution.py:440
  68.6 12.6 %collective-permute-start.17 = (f32[4,64,512]{2,1,0:T(8,128)}, f32[4,64,512]{2,1,0:T(8,128)S(1)}, u32[]{:S(2)}, u32[]{:S(2)}) collective-permute-start(f32[4,64,512]{2,1,0:T(8,128)} %collective-permute-done.9.refs_2_), channel_id=1, source_target_pairs={{0,16},{16,0},{32,48},{48,32},{64,80},{80,64},{96,112},{112,96},{1... | collective-permute-start | bytes 1572872 | tf_op jit(solution)/shard_map/ppermute | solution.py:440
  69.0 23.9 %collective-permute-start.18 = (f32[4,64,512]{2,1,0:T(8,128)}, f32[4,64,512]{2,1,0:T(8,128)}, u32[]{:S(2)}, u32[]{:S(2)}) collective-permute-start(f32[4,64,512]{2,1,0:T(8,128)} %collective-permute-done.10.refs_3_), channel_id=1, source_target_pairs={{0,16},{16,0},{32,48},{48,32},{64,80},{80,64},{96,112},{112,96},{1... | collective-permute-start | bytes 1572872 | tf_op jit(solution)/shard_map/ppermute | solution.py:440
  69.1 44.8 %collective-permute-start.19 = (f32[480,512]{1,0:T(8,128)}, f32[480,512]{1,0:T(8,128)S(1)}, u32[]{:S(2)}, u32[]{:S(2)}) collective-permute-start(f32[480,512]{1,0:T(8,128)} %slice_bitcast_fusion.1), channel_id=1, source_target_pairs={{0,64},{16,80},{32,96},{48,112},{64,0},{80,16},{96,32},{112,48},{1... | collective-permute-start | bytes 2949128 | tf_op jit(solution)/shard_map/ppermute | solution.py:440
  70.3 43.6 %collective-permute-start.12 = (f32[64,512]{1,0:T(8,128)S(1)}, f32[64,512]{1,0:T(8,128)S(1)}, u32[]{:S(2)}, u32[]{:S(2)}) collective-permute-start(f32[64,512]{1,0:T(8,128)S(1)} %get-tuple-element.47), channel_id=1, source_target_pairs={{1,0},{3,16},{5,32},{7,48},{9,64},{11,80},{13,96},{15,112},{16,1},... | collective-permute-start | bytes 393224 | tf_op jit(solution)/shard_map/ppermute | solution.py:484
  75.7 38.1 %collective-permute-start.13 = (f32[64,512]{1,0:T(8,128)S(1)}, f32[64,512]{1,0:T(8,128)S(1)}, u32[]{:S(2)}, u32[]{:S(2)}) collective-permute-start(f32[64,512]{1,0:T(8,128)S(1)} %get-tuple-element.48), channel_id=1, source_target_pairs={{17,1},{19,17},{21,33},{23,49},{25,65},{27,81},{29,97},{31,113},{1... | collective-permute-start | bytes 393224 | tf_op jit(solution)/shard_map/ppermute | solution.py:484
  81.2 32.7 %collective-permute-start.14 = (f32[64,512]{1,0:T(8,128)S(1)}, f32[64,512]{1,0:T(8,128)S(1)}, u32[]{:S(2)}, u32[]{:S(2)}) collective-permute-start(f32[64,512]{1,0:T(8,128)S(1)} %get-tuple-element.49), channel_id=1, source_target_pairs={{0,0},{2,16},{4,32},{6,48},{8,64},{10,80},{12,96},{14,112},{17,2},... | collective-permute-start | bytes 393224 | tf_op jit(solution)/shard_map/ppermute | solution.py:484
  114.0 1.6 collective-permute-start.20
  115.7 28.3 %collective-permute-start.21 = (f32[2,128,512]{2,1,0:T(8,128)S(1)}, f32[2,128,512]{2,1,0:T(8,128)S(1)}, u32[]{:S(2)}, u32[]{:S(2)}) collective-permute-start(f32[2,128,512]{2,1,0:T(8,128)S(1)} %pad_maximum_fusion.1.w0), channel_id=1, source_target_pairs={{0,32},{16,48},{32,0},{48,16},{64,96},{80,112},{96,64},{112,80},{1... | collective-permute-start | bytes 1572872 | tf_op jit(solution)/shard_map/ppermute | solution.py:440
  115.8 28.3 %collective-permute-start.22 = (f32[2,128,512]{2,1,0:T(8,128)S(1)}, f32[2,128,512]{2,1,0:T(8,128)S(1)}, u32[]{:S(2)}, u32[]{:S(2)}) collective-permute-start(f32[2,128,512]{2,1,0:T(8,128)S(1)} %pad_maximum_fusion.1.w0), channel_id=1, source_target_pairs={{0,64},{16,80},{32,96},{48,112},{64,0},{80,16},{96,32},{112,48},{1... | collective-permute-start | bytes 1572872 | tf_op jit(solution)/shard_map/ppermute | solution.py:440
  115.9 28.2 %collective-permute-start.23 = (f32[2,128,512]{2,1,0:T(8,128)S(1)}, f32[2,128,512]{2,1,0:T(8,128)S(1)}, u32[]{:S(2)}, u32[]{:S(2)}) collective-permute-start(f32[2,128,512]{2,1,0:T(8,128)S(1)} %pad_maximum_fusion.1.w0), channel_id=1, source_target_pairs={{0,96},{16,112},{32,64},{48,80},{64,32},{80,48},{96,0},{112,16},{1... | collective-permute-start | bytes 1572872 | tf_op jit(solution)/shard_map/ppermute | solution.py:440
  (13 other events, 188.1 us)
Sparse Core Ops, SparseCore 0:
  61.4 78.9 all-gather.1

commit v5 on v4

--- a/solution.py
+++ b/solution.py
@@ -126,7 +126,7 @@
         ch[EA:, :], cl[EA:, :] = split(b_ref[...])
 
     target = got_ref[0:1, :CR].astype(jnp.int32)
-    g = one_hot(pl.program_id(0) * 512, 512, target)
+    g = one_hot(pl.program_id(0) * 256, 256, target)
     out_ref[...] = trail_ref[...] + (dot1(g, ch[...]) + dot1(g, cl[...]))
 
 
@@ -134,15 +134,15 @@
     return pl.pallas_call(
         trail_got_kernel,
         name="trail_got",
-        grid=(FR // 512,),
+        grid=(FR // 256,),
         out_shape=jax.ShapeDtypeStruct((FR, TC), f32),
         in_specs=[
             pl.BlockSpec((8, FR), lambda s: (PC // 8, 0)),
-            pl.BlockSpec((512, TC), lambda s: (s, 0)),
+            pl.BlockSpec((256, TC), lambda s: (s, 0)),
             pl.BlockSpec((EA, TC), lambda s: (0, 0)),
             pl.BlockSpec((CR - EA, TC), lambda s: (0, 0)),
         ],
-        out_specs=pl.BlockSpec((512, TC), lambda s: (s, 0)),
+        out_specs=pl.BlockSpec((256, TC), lambda s: (s, 0)),
         scratch_shapes=[pltpu.VMEM((CR, TC), bf16)] * 2,
         compiler_params=pltpu.CompilerParams(vmem_limit_bytes=58 * MB),
     )(got, trail, child_a, child_b)

time: 175 us -> 176 us (level)
  transfers between devices with their start and end apart: 25 -> 25, of which waited for: 6 -> 6; matrix products, arithmetic and copies ran while one was open for 3% -> 3% of each run, Pallas kernels for 30% -> 31%
where the time goes in v5:
time: 176 us
  Pallas kernels  80.7 us (46%)
  starting transfers between devices  50.9 us (29%)
  waiting for transfers between devices  22.3 us (13%)
  between operations  14.4 us (8%)
  local copies, waits for them, and re-layouts  4.78 us (3%)
  other arithmetic  2.68 us (2%)
    pallas_call x2, Pallas kernels, chol_call(): pl.pallas_call(kernel, name=name, out_shape=(part, part, inv, inv) + extr...  38.1 us
    ppermute x17, starting transfers between devices, flip(): return lax.ppermute(x, axis, [(i, i ^ bit) for i in range(size)])  25 us
    pallas_call x1, Pallas kernels, finish(): pl.pallas_call(finish_kernel, name='finish', out_shape=(jax.ShapeDtypeStr...  22.7 us
    ppermute x3, starting transfers between devices, on_device(): lax.ppermute(p, ('row', 'col'), window_pairs(k))  22.6 us
    ppermute x17, waiting for transfers between devices, flip(): return lax.ppermute(x, axis, [(i, i ^ bit) for i in range(size)])  15.1 us
    pallas_call x1, Pallas kernels, trail_got(): pl.pallas_call(trail_got_kernel, name='trail_got', grid=(FR // 256,), out...  8.24 us
    pallas_call x1, Pallas kernels, trail_own(): pl.pallas_call(trail_kernel, name='trail_own', grid=(FR // 512,), out_sha...  7.34 us
    ppermute x3, waiting for transfers between devices, on_device(): half = half + lax.ppermute(part, 'row', [(0, k), (4, 4 + k)])  7.15 us
  transfers between devices with their start and end apart: 25, of which 6 were waited for; matrix products, arithmetic and copies ran while one was open for 3% of the time, Pallas kernels for 31%

profile of v5, /device:TPU:21, one launch (start us, length us, event | category | flops | bytes accessed | tf_op | source)
XLA Modules:
  0.0 175.8 jit_solution(8385424685322318386)
XLA Ops:
  7.8 4.4 %panel_parts.1 = (f32[64,1536]{1,0:T(8,128)}, f32[72,1536]{1,0:T(8,128)}, f32[64,1024]{1,0:T(8,128)}) custom-call(s32[2]{0:T(128)} %pad_add_fusion.at_ref, s32[1,2]{1,0:T(1,128)} %bitcast.24, s32[2,1024]{1,0:T(2,128)} %map_ref.3, f32[64,1536]{1,0:T(8,128)} %bitcast.19, f32[2,64,1024]{2,1,0:T(8,128)} %bitcast.17), custom_call_target="tpu_custom_call" | custom-call | tf_op jit(solution)/shard_map/panel_parts/pallas_call | solution.py:80
  12.8 1.0 add.28
  13.9 1.3 collective-permute-start.1
  16.5 3.7 %collective-permute-start.7 = (f32[72,1536]{1,0:T(8,128)}, f32[72,1536]{1,0:T(8,128)S(1)}, u32[]{:S(2)}, u32[]{:S(2)}) collective-permute-start(f32[72,1536]{1,0:T(8,128)} %get-tuple-element.41), channel_id=1, source_target_pairs={{0,64},{16,80},{32,96},{48,112},{64,0},{80,16},{96,32},{112,48},{1... | collective-permute-start | bytes 1327112 | tf_op jit(solution)/shard_map/ppermute | solution.py:440
  20.2 7.1 %collective-permute-done.1 = f32[64,512]{1,0:T(8,128)S(1)} collective-permute-done((f32[64,512]{1,0:T(8,128)S(1)}, f32[64,512]{1,0:T(8,128)S(1)}, u32[]{:S(2)}, u32[]{:S(2)}) %collective-permute-start.1) | collective-permute-done | bytes 131104 | tf_op jit(solution)/shard_map/ppermute | solution.py:469
  28.9 1.2 collective-permute-start.6
  30.1 1.3 slice_bitcast_fusion
  31.4 2.3 %collective-permute-done.5 = f32[64,512]{1,0:T(8,128)S(1)} collective-permute-done((f32[64,512]{1,0:T(8,128)S(1)}, f32[64,512]{1,0:T(8,128)S(1)}, u32[]{:S(2)}, u32[]{:S(2)}) %collective-permute-start.5) | collective-permute-done | bytes 131104 | tf_op jit(solution)/shard_map/ppermute | solution.py:440
  35.0 3.8 %collective-permute-start.11 = (f32[544,512]{1,0:T(8,128)S(1)}, f32[544,512]{1,0:T(8,128)S(1)}, u32[]{:S(2)}, u32[]{:S(2)}) collective-permute-start(f32[544,512]{1,0:T(8,128)S(1)} %slice_bitcast_fusion), channel_id=1, source_target_pairs={{0,64},{16,80},{32,96},{48,112},{64,0},{80,16},{96,32},{112,48},{1... | collective-permute-start | bytes 3342344 | tf_op jit(solution)/shard_map/ppermute | solution.py:440
  38.8 2.3 %slice_bitcast_fusion.1 = f32[480,512]{1,0:T(8,128)} fusion(f32[2,1024,512]{2,1,0:T(8,128)} %child_ref.1), kind=kLoop, calls=%fused_computation.1 | loop fusion | bytes 1966080 | tf_op jit(solution)/shard_map/squeeze | solution.py:480
  42.1 1.8 %collective-permute-start.9 = (f32[4,64,512]{2,1,0:T(8,128)}, f32[4,64,512]{2,1,0:T(8,128)}, u32[]{:S(2)}, u32[]{:S(2)}) collective-permute-start(f32[4,64,512]{2,1,0:T(8,128)} %pad_maximum_fusion.refs_0_), channel_id=1, source_target_pairs={{0,8},{1,9},{2,10},{3,11},{4,12},{5,13},{6,14},{7,15},{8,0},{9,1},... | collective-permute-start | bytes 1572872 | tf_op jit(solution)/shard_map/ppermute | solution.py:440
  43.9 7.3 %trail_own.1.trail_ref = f32[1536,512]{1,0:T(8,128)} custom-call(s32[1,2]{1,0:T(1,128)} %bitcast.25, s32[2,1024]{1,0:T(2,128)} %map_ref.3, f32[1536,512]{1,0:T(8,128)} %front_ref.1, f32[2,1024,512]{2,1,0:T(8,128)} %child_ref.1), custom_call_target="tpu_custom_call" | custom-call | tf_op jit(solution)/shard_map/trail_own/pallas_call | solution.py:105
  51.4 9.9 %collective-permute-done.9.refs_2_ = f32[4,64,512]{2,1,0:T(8,128)} collective-permute-done((f32[4,64,512]{2,1,0:T(8,128)}, f32[4,64,512]{2,1,0:T(8,128)}, u32[]{:S(2)}, u32[]{:S(2)}) %collective-permute-start.9) | collective-permute-done | bytes 524320 | tf_op jit(solution)/shard_map/ppermute | solution.py:440
  61.3 7.2 %collective-permute-start.15 = (f32[4,64,512]{2,1,0:T(8,128)}, f32[4,64,512]{2,1,0:T(8,128)S(1)}, u32[]{:S(2)}, u32[]{:S(2)}) collective-permute-start(f32[4,64,512]{2,1,0:T(8,128)} %pad_maximum_fusion.refs_0_), channel_id=1, source_target_pairs={{0,16},{16,0},{32,48},{48,32},{64,80},{80,64},{96,112},{112,96},{1... | collective-permute-start | bytes 1572872 | tf_op jit(solution)/shard_map/ppermute | solution.py:440
  69.3 1.0 collective-permute-done.15.refs_4_
  70.3 5.4 %collective-permute-start.12 = (f32[64,512]{1,0:T(8,128)S(1)}, f32[64,512]{1,0:T(8,128)S(1)}, u32[]{:S(2)}, u32[]{:S(2)}) collective-permute-start(f32[64,512]{1,0:T(8,128)S(1)} %get-tuple-element.47), channel_id=1, source_target_pairs={{1,0},{3,16},{5,32},{7,48},{9,64},{11,80},{13,96},{15,112},{16,1},... | collective-permute-start | bytes 393224 | tf_op jit(solution)/shard_map/ppermute | solution.py:484
  75.7 5.4 %collective-permute-start.13 = (f32[64,512]{1,0:T(8,128)S(1)}, f32[64,512]{1,0:T(8,128)S(1)}, u32[]{:S(2)}, u32[]{:S(2)}) collective-permute-start(f32[64,512]{1,0:T(8,128)S(1)} %get-tuple-element.48), channel_id=1, source_target_pairs={{17,1},{19,17},{21,33},{23,49},{25,65},{27,81},{29,97},{31,113},{1... | collective-permute-start | bytes 393224 | tf_op jit(solution)/shard_map/ppermute | solution.py:484
  81.2 11.7 %collective-permute-start.14 = (f32[64,512]{1,0:T(8,128)S(1)}, f32[64,512]{1,0:T(8,128)S(1)}, u32[]{:S(2)}, u32[]{:S(2)}) collective-permute-start(f32[64,512]{1,0:T(8,128)S(1)} %get-tuple-element.49), channel_id=1, source_target_pairs={{0,0},{2,16},{4,32},{6,48},{8,64},{10,80},{12,96},{14,112},{17,2},... | collective-permute-start | bytes 393224 | tf_op jit(solution)/shard_map/ppermute | solution.py:484
  92.9 20.9 %chol_head.1 = (bf16[1024,512]{1,0:T(8,128)(2,1)}, bf16[1024,512]{1,0:T(8,128)(2,1)}, bf16[2,256,256]{2,1,0:T(8,128)(2,1)}, bf16[2,256,256]{2,1,0:T(8,128)(2,1)}, f32[512,512]{1,0:T(8,128)}) custom-call(s32[2]{0:T(128)} %pad_add_fusion.at_ref, f32[4,64,512]{2,1,0:T(8,128)} %pad_maximum_fusion.refs_0_, f32[4,64,512]{2,1,0:T(8,128)} %collective-permute-done.8.refs_1_, ...), custom_call_target="tpu_custom_call" | custom-call | flops 24999999488 | bytes 8388608 | tf_op jit(solution)/shard_map/chol_head/pallas_call | solution.py:304
  114.1 1.5 collective-permute-done.20
  115.9 3.8 %collective-permute-start.23 = (f32[2,128,512]{2,1,0:T(8,128)S(1)}, f32[2,128,512]{2,1,0:T(8,128)S(1)}, u32[]{:S(2)}, u32[]{:S(2)}) collective-permute-start(f32[2,128,512]{2,1,0:T(8,128)S(1)} %pad_maximum_fusion.1.w0), channel_id=1, source_target_pairs={{0,96},{16,112},{32,64},{48,80},{64,32},{80,48},{96,0},{112,16},{1... | collective-permute-start | bytes 1572872 | tf_op jit(solution)/shard_map/ppermute | solution.py:440
  119.6 17.1 %chol_tail.1 = (bf16[512,512]{1,0:T(8,128)(2,1)}, bf16[512,512]{1,0:T(8,128)(2,1)}, bf16[2,256,256]{2,1,0:T(8,128)(2,1)}, bf16[2,256,256]{2,1,0:T(8,128)(2,1)}) custom-call(f32[512,512]{1,0:T(8,128)} %get-tuple-element.67.s_in), custom_call_target="tpu_custom_call" | custom-call | flops 24999999488 | bytes 8388608 | tf_op jit(solution)/shard_map/chol_tail/pallas_call | solution.py:304
  136.8 8.2 %trail_got.1.trail = f32[1536,512]{1,0:T(8,128)} custom-call(f32[72,1536]{1,0:T(8,128)} %copy-done.1, f32[1536,512]{1,0:T(8,128)} %trail_own.1.trail_ref, f32[544,512]{1,0:T(8,128)} %copy-done.2, f32[480,512]{1,0:T(8,128)} %copy-done.3), custom_call_target="tpu_custom_call" | custom-call | tf_op jit(solution)/shard_map/trail_got/pallas_call | solution.py:134
  146.2 22.7 %finish.1 = (f32[64,1536]{1,0:T(8,128)}, f32[1536,512]{1,0:T(8,128)}) custom-call(s32[2]{0:T(128)} %pad_add_fusion.at_ref, f32[2,128,512]{2,1,0:T(8,128)} %copy-done.4, f32[2,128,512]{2,1,0:T(8,128)} %copy-done.9, f32[2,128,512]{2,1,0:T(8,128)} %copy-done.10, f32[2,128,512]{2,1,0:T(8,128)} %copy-done.11, f32[1024,1536]{1,0:T(8,128)} %all-gather.2.cloned.1.call-done.pan, ...), custom_call_target="tpu_custom_call" | custom-call | flops 15000000512 | bytes 26214400 | tf_op jit(solution)/shard_map/finish/pallas_call | solution.py:420
  (69 shorter events, 8.8 us)
Async XLA Ops:
  7.2 137.9 %all-gather.2.cloned.1.call-start = ((), (), s32[]{:S(2)}) async-start(), calls=%async_computation | async-start | bytes 6684672 | tf_op jit(solution)/shard_map/all_gather | solution.py:482
  13.9 13.5 %collective-permute-start.1 = (f32[64,512]{1,0:T(8,128)S(1)}, f32[64,512]{1,0:T(8,128)S(1)}, u32[]{:S(2)}, u32[]{:S(2)}) collective-permute-start(f32[64,512]{1,0:T(8,128)S(1)} %get-tuple-element.82), channel_id=1, source_target_pairs={{0,16},{64,80},{1,17},{65,81},{2,18},{66,82},{3,19},{67,83},{4,20}... | collective-permute-start | bytes 393224 | tf_op jit(solution)/shard_map/ppermute | solution.py:469
  15.2 12.2 %collective-permute-start.3 = (f32[64,512]{1,0:T(8,128)S(1)}, f32[64,512]{1,0:T(8,128)S(1)}, u32[]{:S(2)}, u32[]{:S(2)}) collective-permute-start(f32[64,512]{1,0:T(8,128)S(1)} %get-tuple-element.82), channel_id=1, source_target_pairs={{0,48},{64,112},{1,49},{65,113},{2,50},{66,114},{3,51},{67,115},{4... | collective-permute-start | bytes 393224 | tf_op jit(solution)/shard_map/ppermute | solution.py:469
  15.8 11.5 %collective-permute-start.2 = (f32[64,512]{1,0:T(8,128)S(1)}, f32[64,512]{1,0:T(8,128)S(1)}, u32[]{:S(2)}, u32[]{:S(2)}) collective-permute-start(f32[64,512]{1,0:T(8,128)S(1)} %get-tuple-element.81), channel_id=1, source_target_pairs={{0,32},{64,96},{1,33},{65,97},{2,34},{66,98},{3,35},{67,99},{4,36}... | collective-permute-start | bytes 393224 | tf_op jit(solution)/shard_map/ppermute | solution.py:469
  16.5 18.5 %collective-permute-start.7 = (f32[72,1536]{1,0:T(8,128)}, f32[72,1536]{1,0:T(8,128)S(1)}, u32[]{:S(2)}, u32[]{:S(2)}) collective-permute-start(f32[72,1536]{1,0:T(8,128)} %get-tuple-element.41), channel_id=1, source_target_pairs={{0,64},{16,80},{32,96},{48,112},{64,0},{80,16},{96,32},{112,48},{1... | collective-permute-start | bytes 1327112 | tf_op jit(solution)/shard_map/ppermute | solution.py:440
  27.4 4.1 %collective-permute-start.4 = (f32[64,512]{1,0:T(8,128)S(1)}, f32[64,512]{1,0:T(8,128)S(1)}, u32[]{:S(2)}, u32[]{:S(2)}) collective-permute-start(f32[64,512]{1,0:T(8,128)S(1)} %add_add_fusion), channel_id=1, source_target_pairs={{0,1},{1,0},{2,3},{3,2},{4,5},{5,4},{6,7},{7,6},{8,9},{9,8},{10,11... | collective-permute-start | bytes 393224 | tf_op jit(solution)/shard_map/ppermute | solution.py:440
  28.4 5.4 %collective-permute-start.5 = (f32[64,512]{1,0:T(8,128)S(1)}, f32[64,512]{1,0:T(8,128)S(1)}, u32[]{:S(2)}, u32[]{:S(2)}) collective-permute-start(f32[64,512]{1,0:T(8,128)S(1)} %add_add_fusion), channel_id=1, source_target_pairs={{0,2},{1,3},{2,0},{3,1},{4,6},{5,7},{6,4},{7,5},{8,10},{9,11},{10,... | collective-permute-start | bytes 393224 | tf_op jit(solution)/shard_map/ppermute | solution.py:440
  28.9 5.2 %collective-permute-start.6 = (f32[64,512]{1,0:T(8,128)S(1)}, f32[64,512]{1,0:T(8,128)S(1)}, u32[]{:S(2)}, u32[]{:S(2)}) collective-permute-start(f32[64,512]{1,0:T(8,128)S(1)} %add_add_fusion), channel_id=1, source_target_pairs={{0,3},{1,2},{2,1},{3,0},{4,7},{5,6},{6,5},{7,4},{8,11},{9,10},{10,... | collective-permute-start | bytes 393224 | tf_op jit(solution)/shard_map/ppermute | solution.py:440
  35.0 26.3 %collective-permute-start.11 = (f32[544,512]{1,0:T(8,128)S(1)}, f32[544,512]{1,0:T(8,128)S(1)}, u32[]{:S(2)}, u32[]{:S(2)}) collective-permute-start(f32[544,512]{1,0:T(8,128)S(1)} %slice_bitcast_fusion), channel_id=1, source_target_pairs={{0,64},{16,80},{32,96},{48,112},{64,0},{80,16},{96,32},{112,48},{1... | collective-permute-start | bytes 3342344 | tf_op jit(solution)/shard_map/ppermute | solution.py:440
  41.1 10.2 %collective-permute-start.10 = (f32[4,64,512]{2,1,0:T(8,128)}, f32[4,64,512]{2,1,0:T(8,128)}, u32[]{:S(2)}, u32[]{:S(2)}) collective-permute-start(f32[4,64,512]{2,1,0:T(8,128)} %pad_maximum_fusion.refs_0_), channel_id=1, source_target_pairs={{0,12},{1,13},{2,14},{3,15},{4,8},{5,9},{6,10},{7,11},{8,4},{9,5},... | collective-permute-start | bytes 1572872 | tf_op jit(solution)/shard_map/ppermute | solution.py:440
  41.3 10.1 %collective-permute-start.8 = (f32[4,64,512]{2,1,0:T(8,128)}, f32[4,64,512]{2,1,0:T(8,128)}, u32[]{:S(2)}, u32[]{:S(2)}) collective-permute-start(f32[4,64,512]{2,1,0:T(8,128)} %pad_maximum_fusion.refs_0_), channel_id=1, source_target_pairs={{0,4},{1,5},{2,6},{3,7},{4,0},{5,1},{6,2},{7,3},{8,12},{9,13},{10,... | collective-permute-start | bytes 1572872 | tf_op jit(solution)/shard_map/ppermute | solution.py:440
  42.1 19.1 %collective-permute-start.9 = (f32[4,64,512]{2,1,0:T(8,128)}, f32[4,64,512]{2,1,0:T(8,128)}, u32[]{:S(2)}, u32[]{:S(2)}) collective-permute-start(f32[4,64,512]{2,1,0:T(8,128)} %pad_maximum_fusion.refs_0_), channel_id=1, source_target_pairs={{0,8},{1,9},{2,10},{3,11},{4,12},{5,13},{6,14},{7,15},{8,0},{9,1},... | collective-permute-start | bytes 1572872 | tf_op jit(solution)/shard_map/ppermute | solution.py:440
  61.3 9.0 %collective-permute-start.15 = (f32[4,64,512]{2,1,0:T(8,128)}, f32[4,64,512]{2,1,0:T(8,128)S(1)}, u32[]{:S(2)}, u32[]{:S(2)}) collective-permute-start(f32[4,64,512]{2,1,0:T(8,128)} %pad_maximum_fusion.refs_0_), channel_id=1, source_target_pairs={{0,16},{16,0},{32,48},{48,32},{64,80},{80,64},{96,112},{112,96},{1... | collective-permute-start | bytes 1572872 | tf_op jit(solution)/shard_map/ppermute | solution.py:440
  68.5 7.2 %collective-permute-start.16 = (f32[4,64,512]{2,1,0:T(8,128)}, f32[4,64,512]{2,1,0:T(8,128)S(1)}, u32[]{:S(2)}, u32[]{:S(2)}) collective-permute-start(f32[4,64,512]{2,1,0:T(8,128)} %collective-permute-done.8.refs_1_), channel_id=1, source_target_pairs={{0,16},{16,0},{32,48},{48,32},{64,80},{80,64},{96,112},{112,96},{1... | collective-permute-start | bytes 1572872 | tf_op jit(solution)/shard_map/ppermute | solution.py:440
  68.6 12.6 %collective-permute-start.17 = (f32[4,64,512]{2,1,0:T(8,128)}, f32[4,64,512]{2,1,0:T(8,128)S(1)}, u32[]{:S(2)}, u32[]{:S(2)}) collective-permute-start(f32[4,64,512]{2,1,0:T(8,128)} %collective-permute-done.9.refs_2_), channel_id=1, source_target_pairs={{0,16},{16,0},{32,48},{48,32},{64,80},{80,64},{96,112},{112,96},{1... | collective-permute-start | bytes 1572872 | tf_op jit(solution)/shard_map/ppermute | solution.py:440
  69.0 23.9 %collective-permute-start.18 = (f32[4,64,512]{2,1,0:T(8,128)}, f32[4,64,512]{2,1,0:T(8,128)}, u32[]{:S(2)}, u32[]{:S(2)}) collective-permute-start(f32[4,64,512]{2,1,0:T(8,128)} %collective-permute-done.10.refs_3_), channel_id=1, source_target_pairs={{0,16},{16,0},{32,48},{48,32},{64,80},{80,64},{96,112},{112,96},{1... | collective-permute-start | bytes 1572872 | tf_op jit(solution)/shard_map/ppermute | solution.py:440
  69.1 44.8 %collective-permute-start.19 = (f32[480,512]{1,0:T(8,128)}, f32[480,512]{1,0:T(8,128)S(1)}, u32[]{:S(2)}, u32[]{:S(2)}) collective-permute-start(f32[480,512]{1,0:T(8,128)} %slice_bitcast_fusion.1), channel_id=1, source_target_pairs={{0,64},{16,80},{32,96},{48,112},{64,0},{80,16},{96,32},{112,48},{1... | collective-permute-start | bytes 2949128 | tf_op jit(solution)/shard_map/ppermute | solution.py:440
  70.3 43.6 %collective-permute-start.12 = (f32[64,512]{1,0:T(8,128)S(1)}, f32[64,512]{1,0:T(8,128)S(1)}, u32[]{:S(2)}, u32[]{:S(2)}) collective-permute-start(f32[64,512]{1,0:T(8,128)S(1)} %get-tuple-element.47), channel_id=1, source_target_pairs={{1,0},{3,16},{5,32},{7,48},{9,64},{11,80},{13,96},{15,112},{16,1},... | collective-permute-start | bytes 393224 | tf_op jit(solution)/shard_map/ppermute | solution.py:484
  75.7 38.1 %collective-permute-start.13 = (f32[64,512]{1,0:T(8,128)S(1)}, f32[64,512]{1,0:T(8,128)S(1)}, u32[]{:S(2)}, u32[]{:S(2)}) collective-permute-start(f32[64,512]{1,0:T(8,128)S(1)} %get-tuple-element.48), channel_id=1, source_target_pairs={{17,1},{19,17},{21,33},{23,49},{25,65},{27,81},{29,97},{31,113},{1... | collective-permute-start | bytes 393224 | tf_op jit(solution)/shard_map/ppermute | solution.py:484
  81.2 32.7 %collective-permute-start.14 = (f32[64,512]{1,0:T(8,128)S(1)}, f32[64,512]{1,0:T(8,128)S(1)}, u32[]{:S(2)}, u32[]{:S(2)}) collective-permute-start(f32[64,512]{1,0:T(8,128)S(1)} %get-tuple-element.49), channel_id=1, source_target_pairs={{0,0},{2,16},{4,32},{6,48},{8,64},{10,80},{12,96},{14,112},{17,2},... | collective-permute-start | bytes 393224 | tf_op jit(solution)/shard_map/ppermute | solution.py:484
  114.0 1.6 collective-permute-start.20
  115.7 29.3 %collective-permute-start.21 = (f32[2,128,512]{2,1,0:T(8,128)S(1)}, f32[2,128,512]{2,1,0:T(8,128)S(1)}, u32[]{:S(2)}, u32[]{:S(2)}) collective-permute-start(f32[2,128,512]{2,1,0:T(8,128)S(1)} %pad_maximum_fusion.1.w0), channel_id=1, source_target_pairs={{0,32},{16,48},{32,0},{48,16},{64,96},{80,112},{96,64},{112,80},{1... | collective-permute-start | bytes 1572872 | tf_op jit(solution)/shard_map/ppermute | solution.py:440
  115.8 29.2 %collective-permute-start.22 = (f32[2,128,512]{2,1,0:T(8,128)S(1)}, f32[2,128,512]{2,1,0:T(8,128)S(1)}, u32[]{:S(2)}, u32[]{:S(2)}) collective-permute-start(f32[2,128,512]{2,1,0:T(8,128)S(1)} %pad_maximum_fusion.1.w0), channel_id=1, source_target_pairs={{0,64},{16,80},{32,96},{48,112},{64,0},{80,16},{96,32},{112,48},{1... | collective-permute-start | bytes 1572872 | tf_op jit(solution)/shard_map/ppermute | solution.py:440
  115.9 29.2 %collective-permute-start.23 = (f32[2,128,512]{2,1,0:T(8,128)S(1)}, f32[2,128,512]{2,1,0:T(8,128)S(1)}, u32[]{:S(2)}, u32[]{:S(2)}) collective-permute-start(f32[2,128,512]{2,1,0:T(8,128)S(1)} %pad_maximum_fusion.1.w0), channel_id=1, source_target_pairs={{0,96},{16,112},{32,64},{48,80},{64,32},{80,48},{96,0},{112,16},{1... | collective-permute-start | bytes 1572872 | tf_op jit(solution)/shard_map/ppermute | solution.py:440
  (13 other events, 188.1 us)
Sparse Core Ops, SparseCore 0:
  61.4 78.9 all-gather.1

commit v6 on v4

--- a/solution.py
+++ b/solution.py
@@ -54,14 +54,10 @@
     for slab in range(2):
         target = live_target(count_ref[0, slab], map_ref[slab:slab + 1, :])
         c = child_ref[slab]
-        hi = c.astype(bf16)
-        rest = c - hi.astype(f32)
-        mid = rest.astype(bf16)
-        low = (rest - mid.astype(f32)).astype(bf16)
-        parts = jnp.concatenate([hi, mid, low], axis=0)
+        parts = jnp.concatenate(split(c), axis=0)
         for at in range(0, FR, 512):
             moved = dot1(parts, one_hot(at, 512, target), RHS_T)
-            moved = moved[:PC] + (moved[PC:2 * PC] + moved[2 * PC:])
+            moved = moved[:PC] + moved[PC:]
             if slab == 0:
                 own_ref[:, at:at + 512] = front_ref[:, at:at + 512] + moved
             else:

time: 175 us -> 175 us (level)
  no operation moved by 1% of the time
where the time goes in v6:
time: 175 us
  Pallas kernels  79.7 us (46%)
  starting transfers between devices  50.9 us (29%)
  waiting for transfers between devices  22.3 us (13%)
  between operations  14.4 us (8%)
  local copies, waits for them, and re-layouts  4.78 us (3%)
  other arithmetic  2.68 us (2%)
    pallas_call x2, Pallas kernels, chol_call(): pl.pallas_call(kernel, name=name, out_shape=(part, part, inv, inv) + extr...  38.1 us
    ppermute x17, starting transfers between devices, flip(): return lax.ppermute(x, axis, [(i, i ^ bit) for i in range(size)])  25 us
    pallas_call x1, Pallas kernels, finish(): pl.pallas_call(finish_kernel, name='finish', out_shape=(jax.ShapeDtypeStr...  22.7 us
    ppermute x3, starting transfers between devices, on_device(): lax.ppermute(p, ('row', 'col'), window_pairs(k))  22.6 us
    ppermute x17, waiting for transfers between devices, flip(): return lax.ppermute(x, axis, [(i, i ^ bit) for i in range(size)])  15.1 us
    pallas_call x1, Pallas kernels, trail_own(): pl.pallas_call(trail_kernel, name='trail_own', grid=(FR // 512,), out_sha...  7.35 us
    pallas_call x1, Pallas kernels, trail_got(): pl.pallas_call(trail_got_kernel, name='trail_got', grid=(FR // 512,), out...  7.24 us
    ppermute x3, waiting for transfers between devices, on_device(): half = half + lax.ppermute(part, 'row', [(0, k), (4, 4 + k)])  7.13 us
  transfers between devices with their start and end apart: 25, of which 6 were waited for; matrix products, arithmetic and copies ran while one was open for 3% of the time, Pallas kernels for 30%

profile of v6, /device:TPU:21, one launch (start us, length us, event | category | flops | bytes accessed | tf_op | source)
XLA Modules:
  0.0 174.8 jit_solution(13884407613946716553)
XLA Ops:
  7.8 4.4 %panel_parts.1 = (f32[64,1536]{1,0:T(8,128)}, f32[72,1536]{1,0:T(8,128)}, f32[64,1024]{1,0:T(8,128)}) custom-call(s32[2]{0:T(128)} %pad_add_fusion.at_ref, s32[1,2]{1,0:T(1,128)} %bitcast.24, s32[2,1024]{1,0:T(2,128)} %map_ref.3, f32[64,1536]{1,0:T(8,128)} %bitcast.19, f32[2,64,1024]{2,1,0:T(8,128)} %bitcast.17), custom_call_target="tpu_custom_call" | custom-call | tf_op jit(solution)/shard_map/panel_parts/pallas_call | solution.py:76
  13.8 1.3 collective-permute-start.1
  16.5 3.7 %collective-permute-start.7 = (f32[72,1536]{1,0:T(8,128)}, f32[72,1536]{1,0:T(8,128)S(1)}, u32[]{:S(2)}, u32[]{:S(2)}) collective-permute-start(f32[72,1536]{1,0:T(8,128)} %get-tuple-element.41), channel_id=1, source_target_pairs={{0,64},{16,80},{32,96},{48,112},{64,0},{80,16},{96,32},{112,48},{1... | collective-permute-start | bytes 1327112 | tf_op jit(solution)/shard_map/ppermute | solution.py:436
  20.2 7.1 %collective-permute-done.1 = f32[64,512]{1,0:T(8,128)S(1)} collective-permute-done((f32[64,512]{1,0:T(8,128)S(1)}, f32[64,512]{1,0:T(8,128)S(1)}, u32[]{:S(2)}, u32[]{:S(2)}) %collective-permute-start.1) | collective-permute-done | bytes 131104 | tf_op jit(solution)/shard_map/ppermute | solution.py:465
  27.4 1.0 collective-permute-start.4
  28.9 1.2 collective-permute-start.6
  30.1 1.3 slice_bitcast_fusion
  31.4 2.4 %collective-permute-done.5 = f32[64,512]{1,0:T(8,128)S(1)} collective-permute-done((f32[64,512]{1,0:T(8,128)S(1)}, f32[64,512]{1,0:T(8,128)S(1)}, u32[]{:S(2)}, u32[]{:S(2)}) %collective-permute-start.5) | collective-permute-done | bytes 131104 | tf_op jit(solution)/shard_map/ppermute | solution.py:436
  35.0 3.8 %collective-permute-start.11 = (f32[544,512]{1,0:T(8,128)S(1)}, f32[544,512]{1,0:T(8,128)S(1)}, u32[]{:S(2)}, u32[]{:S(2)}) collective-permute-start(f32[544,512]{1,0:T(8,128)S(1)} %slice_bitcast_fusion), channel_id=1, source_target_pairs={{0,64},{16,80},{32,96},{48,112},{64,0},{80,16},{96,32},{112,48},{1... | collective-permute-start | bytes 3342344 | tf_op jit(solution)/shard_map/ppermute | solution.py:436
  38.8 2.3 %slice_bitcast_fusion.1 = f32[480,512]{1,0:T(8,128)} fusion(f32[2,1024,512]{2,1,0:T(8,128)} %child_ref.1), kind=kLoop, calls=%fused_computation.1 | loop fusion | bytes 1966080 | tf_op jit(solution)/shard_map/squeeze | solution.py:476
  42.1 1.8 %collective-permute-start.9 = (f32[4,64,512]{2,1,0:T(8,128)}, f32[4,64,512]{2,1,0:T(8,128)}, u32[]{:S(2)}, u32[]{:S(2)}) collective-permute-start(f32[4,64,512]{2,1,0:T(8,128)} %pad_maximum_fusion.refs_0_), channel_id=1, source_target_pairs={{0,8},{1,9},{2,10},{3,11},{4,12},{5,13},{6,14},{7,15},{8,0},{9,1},... | collective-permute-start | bytes 1572872 | tf_op jit(solution)/shard_map/ppermute | solution.py:436
  43.9 7.4 %trail_own.1.trail_ref = f32[1536,512]{1,0:T(8,128)} custom-call(s32[1,2]{1,0:T(1,128)} %bitcast.25, s32[2,1024]{1,0:T(2,128)} %map_ref.3, f32[1536,512]{1,0:T(8,128)} %front_ref.1, f32[2,1024,512]{2,1,0:T(8,128)} %child_ref.1), custom_call_target="tpu_custom_call" | custom-call | tf_op jit(solution)/shard_map/trail_own/pallas_call | solution.py:101
  51.4 9.9 %collective-permute-done.9.refs_2_ = f32[4,64,512]{2,1,0:T(8,128)} collective-permute-done((f32[4,64,512]{2,1,0:T(8,128)}, f32[4,64,512]{2,1,0:T(8,128)}, u32[]{:S(2)}, u32[]{:S(2)}) %collective-permute-start.9) | collective-permute-done | bytes 524320 | tf_op jit(solution)/shard_map/ppermute | solution.py:436
  61.3 7.2 %collective-permute-start.15 = (f32[4,64,512]{2,1,0:T(8,128)}, f32[4,64,512]{2,1,0:T(8,128)S(1)}, u32[]{:S(2)}, u32[]{:S(2)}) collective-permute-start(f32[4,64,512]{2,1,0:T(8,128)} %pad_maximum_fusion.refs_0_), channel_id=1, source_target_pairs={{0,16},{16,0},{32,48},{48,32},{64,80},{80,64},{96,112},{112,96},{1... | collective-permute-start | bytes 1572872 | tf_op jit(solution)/shard_map/ppermute | solution.py:436
  69.3 1.0 collective-permute-done.15.refs_4_
  70.3 5.4 %collective-permute-start.12 = (f32[64,512]{1,0:T(8,128)S(1)}, f32[64,512]{1,0:T(8,128)S(1)}, u32[]{:S(2)}, u32[]{:S(2)}) collective-permute-start(f32[64,512]{1,0:T(8,128)S(1)} %get-tuple-element.47), channel_id=1, source_target_pairs={{1,0},{3,16},{5,32},{7,48},{9,64},{11,80},{13,96},{15,112},{16,1},... | collective-permute-start | bytes 393224 | tf_op jit(solution)/shard_map/ppermute | solution.py:480
  75.7 5.4 %collective-permute-start.13 = (f32[64,512]{1,0:T(8,128)S(1)}, f32[64,512]{1,0:T(8,128)S(1)}, u32[]{:S(2)}, u32[]{:S(2)}) collective-permute-start(f32[64,512]{1,0:T(8,128)S(1)} %get-tuple-element.48), channel_id=1, source_target_pairs={{17,1},{19,17},{21,33},{23,49},{25,65},{27,81},{29,97},{31,113},{1... | collective-permute-start | bytes 393224 | tf_op jit(solution)/shard_map/ppermute | solution.py:480
  81.2 11.7 %collective-permute-start.14 = (f32[64,512]{1,0:T(8,128)S(1)}, f32[64,512]{1,0:T(8,128)S(1)}, u32[]{:S(2)}, u32[]{:S(2)}) collective-permute-start(f32[64,512]{1,0:T(8,128)S(1)} %get-tuple-element.49), channel_id=1, source_target_pairs={{0,0},{2,16},{4,32},{6,48},{8,64},{10,80},{12,96},{14,112},{17,2},... | collective-permute-start | bytes 393224 | tf_op jit(solution)/shard_map/ppermute | solution.py:480
  92.9 20.9 %chol_head.1 = (bf16[1024,512]{1,0:T(8,128)(2,1)}, bf16[1024,512]{1,0:T(8,128)(2,1)}, bf16[2,256,256]{2,1,0:T(8,128)(2,1)}, bf16[2,256,256]{2,1,0:T(8,128)(2,1)}, f32[512,512]{1,0:T(8,128)}) custom-call(s32[2]{0:T(128)} %pad_add_fusion.at_ref, f32[4,64,512]{2,1,0:T(8,128)} %pad_maximum_fusion.refs_0_, f32[4,64,512]{2,1,0:T(8,128)} %collective-permute-done.8.refs_1_, ...), custom_call_target="tpu_custom_call" | custom-call | flops 24999999488 | bytes 8388608 | tf_op jit(solution)/shard_map/chol_head/pallas_call | solution.py:300
  114.1 1.5 collective-permute-done.20
  115.9 3.8 %collective-permute-start.23 = (f32[2,128,512]{2,1,0:T(8,128)S(1)}, f32[2,128,512]{2,1,0:T(8,128)S(1)}, u32[]{:S(2)}, u32[]{:S(2)}) collective-permute-start(f32[2,128,512]{2,1,0:T(8,128)S(1)} %pad_maximum_fusion.1.w0), channel_id=1, source_target_pairs={{0,96},{16,112},{32,64},{48,80},{64,32},{80,48},{96,0},{112,16},{1... | collective-permute-start | bytes 1572872 | tf_op jit(solution)/shard_map/ppermute | solution.py:436
  119.6 17.1 %chol_tail.1 = (bf16[512,512]{1,0:T(8,128)(2,1)}, bf16[512,512]{1,0:T(8,128)(2,1)}, bf16[2,256,256]{2,1,0:T(8,128)(2,1)}, bf16[2,256,256]{2,1,0:T(8,128)(2,1)}) custom-call(f32[512,512]{1,0:T(8,128)} %get-tuple-element.67.s_in), custom_call_target="tpu_custom_call" | custom-call | flops 24999999488 | bytes 8388608 | tf_op jit(solution)/shard_map/chol_tail/pallas_call | solution.py:300
  136.8 7.2 %trail_got.1.trail = f32[1536,512]{1,0:T(8,128)} custom-call(f32[72,1536]{1,0:T(8,128)} %copy-done.1, f32[1536,512]{1,0:T(8,128)} %trail_own.1.trail_ref, f32[544,512]{1,0:T(8,128)} %copy-done.2, f32[480,512]{1,0:T(8,128)} %copy-done.3), custom_call_target="tpu_custom_call" | custom-call | tf_op jit(solution)/shard_map/trail_got/pallas_call | solution.py:130
  145.2 22.7 %finish.1 = (f32[64,1536]{1,0:T(8,128)}, f32[1536,512]{1,0:T(8,128)}) custom-call(s32[2]{0:T(128)} %pad_add_fusion.at_ref, f32[2,128,512]{2,1,0:T(8,128)} %copy-done.4, f32[2,128,512]{2,1,0:T(8,128)} %copy-done.9, f32[2,128,512]{2,1,0:T(8,128)} %copy-done.10, f32[2,128,512]{2,1,0:T(8,128)} %copy-done.11, f32[1024,1536]{1,0:T(8,128)} %all-gather.2.cloned.1.call-done.pan, ...), custom_call_target="tpu_custom_call" | custom-call | flops 15000000512 | bytes 26214400 | tf_op jit(solution)/shard_map/finish/pallas_call | solution.py:416
  (69 shorter events, 8.8 us)
Async XLA Ops:
  7.2 136.9 %all-gather.2.cloned.1.call-start = ((), (), s32[]{:S(2)}) async-start(), calls=%async_computation | async-start | bytes 6684672 | tf_op jit(solution)/shard_map/all_gather | solution.py:478
  13.8 13.5 %collective-permute-start.1 = (f32[64,512]{1,0:T(8,128)S(1)}, f32[64,512]{1,0:T(8,128)S(1)}, u32[]{:S(2)}, u32[]{:S(2)}) collective-permute-start(f32[64,512]{1,0:T(8,128)S(1)} %get-tuple-element.82), channel_id=1, source_target_pairs={{0,16},{64,80},{1,17},{65,81},{2,18},{66,82},{3,19},{67,83},{4,20}... | collective-permute-start | bytes 393224 | tf_op jit(solution)/shard_map/ppermute | solution.py:465
  15.1 12.2 %collective-permute-start.3 = (f32[64,512]{1,0:T(8,128)S(1)}, f32[64,512]{1,0:T(8,128)S(1)}, u32[]{:S(2)}, u32[]{:S(2)}) collective-permute-start(f32[64,512]{1,0:T(8,128)S(1)} %get-tuple-element.82), channel_id=1, source_target_pairs={{0,48},{64,112},{1,49},{65,113},{2,50},{66,114},{3,51},{67,115},{4... | collective-permute-start | bytes 393224 | tf_op jit(solution)/shard_map/ppermute | solution.py:465
  15.8 11.5 %collective-permute-start.2 = (f32[64,512]{1,0:T(8,128)S(1)}, f32[64,512]{1,0:T(8,128)S(1)}, u32[]{:S(2)}, u32[]{:S(2)}) collective-permute-start(f32[64,512]{1,0:T(8,128)S(1)} %get-tuple-element.81), channel_id=1, source_target_pairs={{0,32},{64,96},{1,33},{65,97},{2,34},{66,98},{3,35},{67,99},{4,36}... | collective-permute-start | bytes 393224 | tf_op jit(solution)/shard_map/ppermute | solution.py:465
  16.5 18.5 %collective-permute-start.7 = (f32[72,1536]{1,0:T(8,128)}, f32[72,1536]{1,0:T(8,128)S(1)}, u32[]{:S(2)}, u32[]{:S(2)}) collective-permute-start(f32[72,1536]{1,0:T(8,128)} %get-tuple-element.41), channel_id=1, source_target_pairs={{0,64},{16,80},{32,96},{48,112},{64,0},{80,16},{96,32},{112,48},{1... | collective-permute-start | bytes 1327112 | tf_op jit(solution)/shard_map/ppermute | solution.py:436
  27.4 4.1 %collective-permute-start.4 = (f32[64,512]{1,0:T(8,128)S(1)}, f32[64,512]{1,0:T(8,128)S(1)}, u32[]{:S(2)}, u32[]{:S(2)}) collective-permute-start(f32[64,512]{1,0:T(8,128)S(1)} %add_add_fusion), channel_id=1, source_target_pairs={{0,1},{1,0},{2,3},{3,2},{4,5},{5,4},{6,7},{7,6},{8,9},{9,8},{10,11... | collective-permute-start | bytes 393224 | tf_op jit(solution)/shard_map/ppermute | solution.py:436
  28.4 5.4 %collective-permute-start.5 = (f32[64,512]{1,0:T(8,128)S(1)}, f32[64,512]{1,0:T(8,128)S(1)}, u32[]{:S(2)}, u32[]{:S(2)}) collective-permute-start(f32[64,512]{1,0:T(8,128)S(1)} %add_add_fusion), channel_id=1, source_target_pairs={{0,2},{1,3},{2,0},{3,1},{4,6},{5,7},{6,4},{7,5},{8,10},{9,11},{10,... | collective-permute-start | bytes 393224 | tf_op jit(solution)/shard_map/ppermute | solution.py:436
  28.9 5.2 %collective-permute-start.6 = (f32[64,512]{1,0:T(8,128)S(1)}, f32[64,512]{1,0:T(8,128)S(1)}, u32[]{:S(2)}, u32[]{:S(2)}) collective-permute-start(f32[64,512]{1,0:T(8,128)S(1)} %add_add_fusion), channel_id=1, source_target_pairs={{0,3},{1,2},{2,1},{3,0},{4,7},{5,6},{6,5},{7,4},{8,11},{9,10},{10,... | collective-permute-start | bytes 393224 | tf_op jit(solution)/shard_map/ppermute | solution.py:436
  35.0 26.3 %collective-permute-start.11 = (f32[544,512]{1,0:T(8,128)S(1)}, f32[544,512]{1,0:T(8,128)S(1)}, u32[]{:S(2)}, u32[]{:S(2)}) collective-permute-start(f32[544,512]{1,0:T(8,128)S(1)} %slice_bitcast_fusion), channel_id=1, source_target_pairs={{0,64},{16,80},{32,96},{48,112},{64,0},{80,16},{96,32},{112,48},{1... | collective-permute-start | bytes 3342344 | tf_op jit(solution)/shard_map/ppermute | solution.py:436
  41.1 10.3 %collective-permute-start.10 = (f32[4,64,512]{2,1,0:T(8,128)}, f32[4,64,512]{2,1,0:T(8,128)}, u32[]{:S(2)}, u32[]{:S(2)}) collective-permute-start(f32[4,64,512]{2,1,0:T(8,128)} %pad_maximum_fusion.refs_0_), channel_id=1, source_target_pairs={{0,12},{1,13},{2,14},{3,15},{4,8},{5,9},{6,10},{7,11},{8,4},{9,5},... | collective-permute-start | bytes 1572872 | tf_op jit(solution)/shard_map/ppermute | solution.py:436
  41.3 10.1 %collective-permute-start.8 = (f32[4,64,512]{2,1,0:T(8,128)}, f32[4,64,512]{2,1,0:T(8,128)}, u32[]{:S(2)}, u32[]{:S(2)}) collective-permute-start(f32[4,64,512]{2,1,0:T(8,128)} %pad_maximum_fusion.refs_0_), channel_id=1, source_target_pairs={{0,4},{1,5},{2,6},{3,7},{4,0},{5,1},{6,2},{7,3},{8,12},{9,13},{10,... | collective-permute-start | bytes 1572872 | tf_op jit(solution)/shard_map/ppermute | solution.py:436
  42.1 19.1 %collective-permute-start.9 = (f32[4,64,512]{2,1,0:T(8,128)}, f32[4,64,512]{2,1,0:T(8,128)}, u32[]{:S(2)}, u32[]{:S(2)}) collective-permute-start(f32[4,64,512]{2,1,0:T(8,128)} %pad_maximum_fusion.refs_0_), channel_id=1, source_target_pairs={{0,8},{1,9},{2,10},{3,11},{4,12},{5,13},{6,14},{7,15},{8,0},{9,1},... | collective-permute-start | bytes 1572872 | tf_op jit(solution)/shard_map/ppermute | solution.py:436
  61.3 9.0 %collective-permute-start.15 = (f32[4,64,512]{2,1,0:T(8,128)}, f32[4,64,512]{2,1,0:T(8,128)S(1)}, u32[]{:S(2)}, u32[]{:S(2)}) collective-permute-start(f32[4,64,512]{2,1,0:T(8,128)} %pad_maximum_fusion.refs_0_), channel_id=1, source_target_pairs={{0,16},{16,0},{32,48},{48,32},{64,80},{80,64},{96,112},{112,96},{1... | collective-permute-start | bytes 1572872 | tf_op jit(solution)/shard_map/ppermute | solution.py:436
  68.5 7.2 %collective-permute-start.16 = (f32[4,64,512]{2,1,0:T(8,128)}, f32[4,64,512]{2,1,0:T(8,128)S(1)}, u32[]{:S(2)}, u32[]{:S(2)}) collective-permute-start(f32[4,64,512]{2,1,0:T(8,128)} %collective-permute-done.8.refs_1_), channel_id=1, source_target_pairs={{0,16},{16,0},{32,48},{48,32},{64,80},{80,64},{96,112},{112,96},{1... | collective-permute-start | bytes 1572872 | tf_op jit(solution)/shard_map/ppermute | solution.py:436
  68.6 12.5 %collective-permute-start.17 = (f32[4,64,512]{2,1,0:T(8,128)}, f32[4,64,512]{2,1,0:T(8,128)S(1)}, u32[]{:S(2)}, u32[]{:S(2)}) collective-permute-start(f32[4,64,512]{2,1,0:T(8,128)} %collective-permute-done.9.refs_2_), channel_id=1, source_target_pairs={{0,16},{16,0},{32,48},{48,32},{64,80},{80,64},{96,112},{112,96},{1... | collective-permute-start | bytes 1572872 | tf_op jit(solution)/shard_map/ppermute | solution.py:436
  69.0 23.9 %collective-permute-start.18 = (f32[4,64,512]{2,1,0:T(8,128)}, f32[4,64,512]{2,1,0:T(8,128)}, u32[]{:S(2)}, u32[]{:S(2)}) collective-permute-start(f32[4,64,512]{2,1,0:T(8,128)} %collective-permute-done.10.refs_3_), channel_id=1, source_target_pairs={{0,16},{16,0},{32,48},{48,32},{64,80},{80,64},{96,112},{112,96},{1... | collective-permute-start | bytes 1572872 | tf_op jit(solution)/shard_map/ppermute | solution.py:436
  69.1 44.8 %collective-permute-start.19 = (f32[480,512]{1,0:T(8,128)}, f32[480,512]{1,0:T(8,128)S(1)}, u32[]{:S(2)}, u32[]{:S(2)}) collective-permute-start(f32[480,512]{1,0:T(8,128)} %slice_bitcast_fusion.1), channel_id=1, source_target_pairs={{0,64},{16,80},{32,96},{48,112},{64,0},{80,16},{96,32},{112,48},{1... | collective-permute-start | bytes 2949128 | tf_op jit(solution)/shard_map/ppermute | solution.py:436
  70.3 43.6 %collective-permute-start.12 = (f32[64,512]{1,0:T(8,128)S(1)}, f32[64,512]{1,0:T(8,128)S(1)}, u32[]{:S(2)}, u32[]{:S(2)}) collective-permute-start(f32[64,512]{1,0:T(8,128)S(1)} %get-tuple-element.47), channel_id=1, source_target_pairs={{1,0},{3,16},{5,32},{7,48},{9,64},{11,80},{13,96},{15,112},{16,1},... | collective-permute-start | bytes 393224 | tf_op jit(solution)/shard_map/ppermute | solution.py:480
  75.7 38.2 %collective-permute-start.13 = (f32[64,512]{1,0:T(8,128)S(1)}, f32[64,512]{1,0:T(8,128)S(1)}, u32[]{:S(2)}, u32[]{:S(2)}) collective-permute-start(f32[64,512]{1,0:T(8,128)S(1)} %get-tuple-element.48), channel_id=1, source_target_pairs={{17,1},{19,17},{21,33},{23,49},{25,65},{27,81},{29,97},{31,113},{1... | collective-permute-start | bytes 393224 | tf_op jit(solution)/shard_map/ppermute | solution.py:480
  81.2 32.7 %collective-permute-start.14 = (f32[64,512]{1,0:T(8,128)S(1)}, f32[64,512]{1,0:T(8,128)S(1)}, u32[]{:S(2)}, u32[]{:S(2)}) collective-permute-start(f32[64,512]{1,0:T(8,128)S(1)} %get-tuple-element.49), channel_id=1, source_target_pairs={{0,0},{2,16},{4,32},{6,48},{8,64},{10,80},{12,96},{14,112},{17,2},... | collective-permute-start | bytes 393224 | tf_op jit(solution)/shard_map/ppermute | solution.py:480
  114.0 1.6 collective-permute-start.20
  115.7 28.3 %collective-permute-start.21 = (f32[2,128,512]{2,1,0:T(8,128)S(1)}, f32[2,128,512]{2,1,0:T(8,128)S(1)}, u32[]{:S(2)}, u32[]{:S(2)}) collective-permute-start(f32[2,128,512]{2,1,0:T(8,128)S(1)} %pad_maximum_fusion.1.w0), channel_id=1, source_target_pairs={{0,32},{16,48},{32,0},{48,16},{64,96},{80,112},{96,64},{112,80},{1... | collective-permute-start | bytes 1572872 | tf_op jit(solution)/shard_map/ppermute | solution.py:436
  115.8 28.2 %collective-permute-start.22 = (f32[2,128,512]{2,1,0:T(8,128)S(1)}, f32[2,128,512]{2,1,0:T(8,128)S(1)}, u32[]{:S(2)}, u32[]{:S(2)}) collective-permute-start(f32[2,128,512]{2,1,0:T(8,128)S(1)} %pad_maximum_fusion.1.w0), channel_id=1, source_target_pairs={{0,64},{16,80},{32,96},{48,112},{64,0},{80,16},{96,32},{112,48},{1... | collective-permute-start | bytes 1572872 | tf_op jit(solution)/shard_map/ppermute | solution.py:436
  115.9 28.1 %collective-permute-start.23 = (f32[2,128,512]{2,1,0:T(8,128)S(1)}, f32[2,128,512]{2,1,0:T(8,128)S(1)}, u32[]{:S(2)}, u32[]{:S(2)}) collective-permute-start(f32[2,128,512]{2,1,0:T(8,128)S(1)} %pad_maximum_fusion.1.w0), channel_id=1, source_target_pairs={{0,96},{16,112},{32,64},{48,80},{64,32},{80,48},{96,0},{112,16},{1... | collective-permute-start | bytes 1572872 | tf_op jit(solution)/shard_map/ppermute | solution.py:436
  (13 other events, 188.1 us)
Sparse Core Ops, SparseCore 0:
  61.4 77.5 all-gather.1
